TPU v7x, 32 devices: a whole 2x2x4 slice. The times are simulated.
32 devices in a mesh: cell: 16 (over z, y, core), inst: 2 (over x).
Axes of the slice: x: 2, y: 2, z: 4, core: 2. Of those that a mesh axis runs over, the one named last changes fastest.
Arguments:
- initial: float32 [80, 32768], P('inst', 'cell'), may hold values from -6 to 6
- source: float32 [80, 32768], P('inst', 'cell'), may hold values from -6 to 6
- neighbors: int32 [4, 32768], P(None, 'cell'), may hold values from -256 to 256, as said below
- face_weights: float32 [4, 32768], P(None, 'cell'), may hold values from 0.25 to 1
- damping: float32 [32768], P('cell'), may hold values from 0.5 to 2
Outputs:
- solution: float32 [80, 32768], P('inst', 'cell')
Inputs may be any that keep to these rules, and one draw needn't show every extreme that they name: `neighbors`: entries 0 and 2 of a cell's offsets are at or below zero, entries 1 and 3 at or above zero; a cell plus each of its offsets is a cell of the grid; in every draw some offsets are exactly -256 and exactly 256.
All inputs are finite; a program needn't handle non-finite values.
Results may differ from a plain program's by a relative error of at most 0.0001.
Values sent between devices are 32-bit elements; how exact they have to be, the bound alone decides.
No kernel may reach another device: no remote copies, remote signals or barrier semaphores. Data moves between devices by JAX's collectives and lax.ppermute only.
A program may use at most 64 MiB of HBM per device.

v0:
```python
import jax
import jax.numpy as jnp
from jax import lax
from jax.sharding import PartitionSpec as P

NI = 16
NC = 4
COMP = 5
NEIGH = 4
SWEEPS_FINE = 2
SWEEPS_COARSE = 3
PLANE = 256


FREQ = 0.15
RELAX = 0.6


def padded_2(block, sides, width):
    for axis, dim in sides:
        count = lax.axis_size(axis)
        forward = [(i, i + 1) for i in range(count - 1)]
        backward = [(target, source) for source, target in forward]
        low = lax.ppermute(
            lax.slice_in_dim(block, block.shape[dim] - width, None, axis=dim), axis, forward
        )
        high = lax.ppermute(lax.slice_in_dim(block, 0, width, axis=dim), axis, backward)
        block = jnp.concatenate([low, block, high], axis=dim)
    return block


def spectral_matrix(points):
    steps = jnp.arange(points, dtype=jnp.float32)
    offset = steps[:, None] - steps[None, :]
    parity = 1.0 - 2.0 * jnp.mod(offset, 2.0)
    angle = jnp.where(offset == 0, 0.5, jnp.pi * offset / points)
    return jnp.where(offset == 0, 0.0, 0.5 * parity / jnp.tan(angle))


def restrict_matrix():
    coarse_t = jnp.arange(NC, dtype=jnp.float32) / NC
    fine_t = jnp.arange(NI, dtype=jnp.float32) / NI
    return (1.0 + 2.0 * jnp.cos(2.0 * jnp.pi * (coarse_t[:, None] - fine_t[None, :]))) / NI


def prolong_matrix():
    coarse_t = jnp.arange(NC, dtype=jnp.float32) / NC
    fine_t = jnp.arange(NI, dtype=jnp.float32) / NI
    return (1.0 + 2.0 * jnp.cos(2.0 * jnp.pi * (fine_t[:, None] - coarse_t[None, :]))) / NC


def expand(matrix):
    return jnp.kron(matrix, jnp.eye(COMP, dtype=jnp.float32))


def neighbour_terms(padded, flat_index, face_weights):
    cells = face_weights.shape[1]
    picked = jnp.take(padded, flat_index, axis=1).reshape(padded.shape[0], NEIGH, cells)
    return jnp.sum(face_weights[None, :, :] * picked, axis=1)


def fine_stencil(values, flat_index, face_weights):
    padded = padded_2(values, (("cell", 1),), PLANE)
    return neighbour_terms(padded, flat_index, face_weights)


def coarse_stencil(values, flat_index, face_weights):
    padded = padded_2(values, ((("cell", "inst"), 1),), PLANE)
    return neighbour_terms(padded, flat_index, face_weights)


def per_device(initial, source, neighbors, face_weights, damping):
    cells = initial.shape[1]
    own_count = initial.shape[0]
    inst_count = lax.axis_size("inst")
    inst_id = lax.axis_index("inst")
    highest = lax.Precision.HIGHEST
    fine_matrix = expand(spectral_matrix(NI))
    coarse_matrix = expand(spectral_matrix(NC))
    own_rows = lax.dynamic_slice_in_dim(fine_matrix, inst_id * own_count, own_count, 0)
    diagonal = damping + jnp.sum(face_weights, axis=0)
    position = jnp.arange(cells, dtype=jnp.int32)
    fine_index = (neighbors + position[None, :] + PLANE).reshape(-1)

    def derivative(values):
        gathered = lax.all_gather(values, "inst", axis=0, tiled=True)
        return jnp.dot(own_rows, gathered, precision=highest)

    def fine_operator(values):
        return (
            FREQ * derivative(values)
            + diagonal * values
            - fine_stencil(values, fine_index, face_weights)
        )

    solution = initial
    for sweep in range(SWEEPS_FINE):
        solution = solution + RELAX * (source - fine_operator(solution)) / diagonal
    residual = source - fine_operator(solution)
    own_columns = lax.dynamic_slice_in_dim(
        expand(restrict_matrix()), inst_id * own_count, own_count, 1
    )
    partial_terms = jnp.dot(own_columns, residual, precision=highest)
    prolong_rows = lax.dynamic_slice_in_dim(
        expand(prolong_matrix()), inst_id * own_count, own_count, 0
    )
    coarse_rhs = lax.psum_scatter(partial_terms, "inst", scatter_dimension=1, tiled=True)
    share = cells // inst_count
    share_weights = lax.dynamic_slice_in_dim(face_weights, inst_id * share, share, 1)
    share_diagonal = lax.dynamic_slice_in_dim(diagonal, inst_id * share, share, 0)
    share_offsets = lax.dynamic_slice_in_dim(neighbors, inst_id * share, share, 1)
    share_position = jnp.arange(share, dtype=jnp.int32)
    share_index = (share_offsets + share_position[None, :] + PLANE).reshape(-1)
    correction = RELAX * coarse_rhs / share_diagonal
    for sweep in range(SWEEPS_COARSE - 1):
        spectral = jnp.dot(coarse_matrix, correction, precision=highest)
        applied = (
            FREQ * spectral
            + share_diagonal * correction
            - coarse_stencil(correction, share_index, share_weights)
        )
        correction = correction + RELAX * (coarse_rhs - applied) / share_diagonal
    whole_correction = lax.all_gather(correction, "inst", axis=1, tiled=True)
    return solution + jnp.dot(prolong_rows, whole_correction, precision=highest)


def solution(mesh):
    return jax.shard_map(
        per_device,
        mesh=mesh,
        in_specs=(
            P("inst", "cell"),
            P("inst", "cell"),
            P(None, "cell"),
            P(None, "cell"),
            P("cell"),
        ),
        out_specs=P("inst", "cell"),
        check_vma=False,
    )
```

profile of v0, /device:TPU:19, one launch (start us, length us, event | category | flops | bytes accessed | tf_op | source)
XLA Modules:
  0.0 242.3 jit_solution(3188418022927423007)
XLA Ops:
  6.5 0.8 fusion.63
  7.3 3.7 %collective-permute-start = (f32[40,256]{1,0:T(8,128)S(1)}, f32[40,256]{1,0:T(8,128)S(1)}, u32[]{:S(2)}, u32[]{:S(2)}) collective-permute-start(f32[40,256]{1,0:T(8,128)S(1)} %get-tuple-element.11), channel_id=1, source_target_pairs={{0,2},{2,4},{4,6},{6,8},{8,10},{10,12},{12,14},{14,16},{16,18},{18... | collective-permute-start | bytes 122888 | tf_op jit(solution)/shard_map/ppermute | solution.py:24
  11.0 1.9 collective-permute-start.1
  13.0 0.8 add_bitcast_fusion
  13.9 0.7 add_bitcast_fusion.1
  14.7 0.1 add_multiply_fusion
  14.8 0.1 add_multiply_fusion.1
  14.9 0.1 broadcast_multiply_fusion
  15.1 8.6 %all_gather.12 = f32[80,2048]{1,0:T(8,128)S(1)} all-gather(f32[40,2048]{1,0:T(8,128)} %param.9), channel_id=1, replica_groups=mesh['cell'=16,'inst'=2] {'inst'}, dimensions={0}, use_global_device_ids=true | all-gather | bytes 983040 | tf_op jit(solution)/shard_map/all_gather | solution.py:86
  23.7 0.3 mul.297
  24.0 0.1 mul.324
  24.2 0.8 reduce_sum.54
  25.0 0.7 add.129
  25.7 1.0 pad_maximum_fusion
  26.7 0.4 copy.21
  27.1 27.7 %gather_fusion = f32[8192,40]{1,0:T(8,128)} fusion(f32[40,2560]{0,1:T(8,128)S(1)} %copy.21, s32[8192]{0:T(1024)S(1)} %fusion.27), kind=kCustom, calls=%fused_computation.clone | custom fusion | bytes 2654208 | tf_op jit(solution)/shard_map/jit(_take)/gather | solution.py:58
  54.8 6.2 %broadcast_select_fusion.2 = f32[8192,40]{1,0:T(8,128)S(1)} fusion(f32[8192,40]{1,0:T(8,128)} %gather_fusion, pred[8192]{0:T(1024)(128)(4,1)S(1)} %compare_and_fusion), kind=kLoop, calls=%fused_computation.29 | loop fusion | flops 327680 | bytes 2629632 | tf_op jit(solution)/shard_map/jit(_take)/select_n | solution.py:58
  61.1 1.6 multiply_reduce_fusion.2
  62.7 0.3 copy.22
  63.0 0.6 fusion.5
  63.6 5.4 %collective-permute-start.2 = (f32[40,256]{1,0:T(8,128)S(1)}, f32[40,256]{1,0:T(8,128)S(1)}, u32[]{:S(2)}, u32[]{:S(2)}) collective-permute-start(f32[40,256]{1,0:T(8,128)S(1)} %get-tuple-element.9), channel_id=1, source_target_pairs={{0,2},{2,4},{4,6},{6,8},{8,10},{10,12},{12,14},{14,16},{16,18},{18... | collective-permute-start | bytes 122888 | tf_op jit(solution)/shard_map/ppermute | solution.py:24
  69.0 1.9 collective-permute-start.3
  70.9 8.4 %all_gather.13 = f32[80,2048]{1,0:T(8,128)S(1)} all-gather(f32[40,2048]{1,0:T(8,128)S(1)} %fusion.5), channel_id=1, replica_groups=mesh['cell'=16,'inst'=2] {'inst'}, dimensions={0}, use_global_device_ids=true | all-gather | bytes 983040 | tf_op jit(solution)/shard_map/all_gather | solution.py:86
  79.4 0.4 copy.23
  79.8 27.7 %gather_fusion.1 = f32[8192,40]{1,0:T(8,128)} fusion(f32[40,2560]{0,1:T(8,128)S(1)} %copy.23, s32[8192]{0:T(1024)S(1)} %fusion.27), kind=kCustom, calls=%fused_computation.2.clone | custom fusion | bytes 2654208 | tf_op jit(solution)/shard_map/jit(_take)/gather | solution.py:58
  107.5 6.2 %broadcast_select_fusion.1 = f32[8192,40]{1,0:T(8,128)S(1)} fusion(f32[8192,40]{1,0:T(8,128)} %gather_fusion.1, pred[8192]{0:T(1024)(128)(4,1)S(1)} %compare_and_fusion), kind=kLoop, calls=%fused_computation.28 | loop fusion | flops 327680 | bytes 2629632 | tf_op jit(solution)/shard_map/jit(_take)/select_n | solution.py:58
  113.7 1.6 multiply_reduce_fusion.1
  115.3 0.3 copy.24
  115.6 0.5 fusion.11
  116.2 5.4 %collective-permute-start.4 = (f32[40,256]{1,0:T(8,128)S(1)}, f32[40,256]{1,0:T(8,128)S(1)}, u32[]{:S(2)}, u32[]{:S(2)}) collective-permute-start(f32[40,256]{1,0:T(8,128)S(1)} %get-tuple-element.6), channel_id=1, source_target_pairs={{0,2},{2,4},{4,6},{6,8},{8,10},{10,12},{12,14},{14,16},{16,18},{18... | collective-permute-start | bytes 122888 | tf_op jit(solution)/shard_map/ppermute | solution.py:24
  121.6 1.9 collective-permute-start.5
  123.5 8.4 %all_gather.14 = f32[80,2048]{1,0:T(8,128)S(1)} all-gather(f32[40,2048]{1,0:T(8,128)S(1)} %fusion.11), channel_id=1, replica_groups=mesh['cell'=16,'inst'=2] {'inst'}, dimensions={0}, use_global_device_ids=true | all-gather | bytes 983040 | tf_op jit(solution)/shard_map/all_gather | solution.py:86
  132.0 0.4 copy.26
  132.4 27.7 %gather_fusion.2 = f32[8192,40]{1,0:T(8,128)} fusion(f32[40,2560]{0,1:T(8,128)S(1)} %copy.26, s32[8192]{0:T(1024)S(1)} %fusion.27), kind=kCustom, calls=%fused_computation.3.clone | custom fusion | bytes 2654208 | tf_op jit(solution)/shard_map/jit(_take)/gather | solution.py:58
  160.1 6.2 %broadcast_select_fusion = f32[8192,40]{1,0:T(8,128)S(1)} fusion(f32[8192,40]{1,0:T(8,128)} %gather_fusion.2, pred[8192]{0:T(1024)(128)(4,1)S(1)} %compare_and_fusion), kind=kLoop, calls=%fused_computation.27 | loop fusion | flops 327680 | bytes 2629632 | tf_op jit(solution)/shard_map/jit(_take)/select_n | solution.py:58
  166.3 1.6 multiply_reduce_fusion
  167.9 0.3 copy.27
  168.2 0.5 fusion.14
  168.7 1.1 fusion.32
  169.9 10.7 %reduce-scatter.2.cloned.1.call-done = f32[20,1024]{1,0:T(8,128)} async-done(((f32[20,2048]{1,0:T(8,128)}), f32[20,1024]{1,0:T(8,128)}) %reduce-scatter.2.cloned.1.call-update) | async-done | bytes 81936 | tf_op jit(solution)/shard_map/reduce_scatter | solution.py:107
  180.7 0.9 multiply_divide_fusion
  181.6 4.8 %collective-permute-start.6 = (f32[20,256]{1,0:T(8,128)S(1)}, f32[20,256]{1,0:T(8,128)S(1)}, u32[]{:S(2)}, u32[]{:S(2)}) collective-permute-start(f32[20,256]{1,0:T(8,128)S(1)} %get-tuple-element.15), channel_id=1, source_target_pairs={{0,1},{1,2},{2,3},{3,4},{4,5},{5,6},{6,7},{7,8},{8,9},{9,10},{10,1... | collective-permute-start | bytes 61448 | tf_op jit(solution)/shard_map/ppermute | solution.py:24
  186.4 1.9 collective-permute-start.7
  188.3 0.1 copy.25
  188.4 0.1 mul.335
  188.5 3.9 %collective-permute-done.7 = f32[20,256]{1,0:T(8,128)S(1)} collective-permute-done((f32[20,256]{1,0:T(8,128)S(1)}, f32[20,256]{1,0:T(8,128)S(1)}, u32[]{:S(2)}, u32[]{:S(2)}) %collective-permute-start.7) | collective-permute-done | bytes 20512 | tf_op jit(solution)/shard_map/ppermute | solution.py:27
  192.4 0.3 copy.28
  192.7 10.8 %gather_fusion.3 = f32[4096,20]{1,0:T(8,128)S(1)} fusion(f32[20,1536]{0,1:T(8,128)S(1)} %copy.28, s32[4096]{0:T(1024)S(1)} %fusion.31), kind=kCustom, calls=%fused_computation.1.clone | custom fusion | bytes 671744 | tf_op jit(solution)/shard_map/jit(_take)/gather | solution.py:58
  203.5 2.1 broadcast_select_fusion.4
  205.7 0.7 multiply_reduce_fusion.4
  206.4 0.2 copy.29
  206.6 0.3 fusion.26
  206.9 2.2 collective-permute-start.8
  209.0 3.1 %collective-permute-start.9 = (f32[20,256]{1,0:T(8,128)S(1)}, f32[20,256]{1,0:T(8,128)S(1)}, u32[]{:S(2)}, u32[]{:S(2)}) collective-permute-start(f32[20,256]{1,0:T(8,128)S(1)} %get-tuple-element.14), channel_id=1, source_target_pairs={{1,0},{2,1},{3,2},{4,3},{5,4},{6,5},{7,6},{8,7},{9,8},{10,9},{11,1... | collective-permute-start | bytes 61448 | tf_op jit(solution)/shard_map/ppermute | solution.py:27
  212.2 0.1 mul.316
  212.4 2.9 %collective-permute-done.9 = f32[20,256]{1,0:T(8,128)S(1)} collective-permute-done((f32[20,256]{1,0:T(8,128)S(1)}, f32[20,256]{1,0:T(8,128)S(1)}, u32[]{:S(2)}, u32[]{:S(2)}) %collective-permute-start.9) | collective-permute-done | bytes 20512 | tf_op jit(solution)/shard_map/ppermute | solution.py:27
  215.3 0.3 copy.30
  215.6 10.8 %gather_fusion.4 = f32[4096,20]{1,0:T(8,128)S(1)} fusion(f32[20,1536]{0,1:T(8,128)S(1)} %copy.30, s32[4096]{0:T(1024)S(1)} %fusion.31), kind=kCustom, calls=%fused_computation.4.clone | custom fusion | bytes 671744 | tf_op jit(solution)/shard_map/jit(_take)/gather | solution.py:58
  226.4 2.1 broadcast_select_fusion.3
  228.5 0.7 multiply_reduce_fusion.3
  229.3 0.2 copy.31
  229.5 0.3 fusion.24
  229.7 4.4 %all_gather.15 = f32[20,2048]{1,0:T(8,128)S(1)} all-gather(f32[20,1024]{1,0:T(8,128)S(1)} %fusion.24), channel_id=1, replica_groups=mesh['cell'=16,'inst'=2] {'inst'}, dimensions={1}, use_global_device_ids=true | all-gather | bytes 245760 | tf_op jit(solution)/shard_map/all_gather | solution.py:123
  234.2 1.3 convolution_add_fusion
  (41 shorter events, 0.6 us)
Async XLA Ops:
  6.5 174.1 %reduce-scatter.2.cloned.1.call-start = ((), (), s32[]{:S(2)}) async-start(), calls=%async_computation.1 | async-start | bytes 294912 | tf_op jit(solution)/shard_map/reduce_scatter | solution.py:107
  7.3 18.3 %collective-permute-start = (f32[40,256]{1,0:T(8,128)S(1)}, f32[40,256]{1,0:T(8,128)S(1)}, u32[]{:S(2)}, u32[]{:S(2)}) collective-permute-start(f32[40,256]{1,0:T(8,128)S(1)} %get-tuple-element.11), channel_id=1, source_target_pairs={{0,2},{2,4},{4,6},{6,8},{8,10},{10,12},{12,14},{14,16},{16,18},{18... | collective-permute-start | bytes 122888 | tf_op jit(solution)/shard_map/ppermute | solution.py:24
  11.0 14.6 %collective-permute-start.1 = (f32[40,256]{1,0:T(8,128)S(1)}, f32[40,256]{1,0:T(8,128)S(1)}, u32[]{:S(2)}, u32[]{:S(2)}) collective-permute-start(f32[40,256]{1,0:T(8,128)S(1)} %get-tuple-element.12), channel_id=1, source_target_pairs={{2,0},{4,2},{6,4},{8,6},{10,8},{12,10},{14,12},{16,14},{18,16},{20... | collective-permute-start | bytes 122888 | tf_op jit(solution)/shard_map/ppermute | solution.py:27
  54.8 6.3 %copy-start.2 = (f32[4,2048]{1,0:T(4,128)S(1)}, f32[4,2048]{1,0:T(4,128)}, u32[]{:S(2)}) copy-start(f32[4,2048]{1,0:T(4,128)} %param.12) | copy-start | bytes 98308
  61.0 1.9 copy-start
  61.0 1.9 copy-start.1
  63.6 15.8 %collective-permute-start.2 = (f32[40,256]{1,0:T(8,128)S(1)}, f32[40,256]{1,0:T(8,128)S(1)}, u32[]{:S(2)}, u32[]{:S(2)}) collective-permute-start(f32[40,256]{1,0:T(8,128)S(1)} %get-tuple-element.9), channel_id=1, source_target_pairs={{0,2},{2,4},{4,6},{6,8},{8,10},{10,12},{12,14},{14,16},{16,18},{18... | collective-permute-start | bytes 122888 | tf_op jit(solution)/shard_map/ppermute | solution.py:24
  69.0 10.4 %collective-permute-start.3 = (f32[40,256]{1,0:T(8,128)S(1)}, f32[40,256]{1,0:T(8,128)S(1)}, u32[]{:S(2)}, u32[]{:S(2)}) collective-permute-start(f32[40,256]{1,0:T(8,128)S(1)} %get-tuple-element.10), channel_id=1, source_target_pairs={{2,0},{4,2},{6,4},{8,6},{10,8},{12,10},{14,12},{16,14},{18,16},{20... | collective-permute-start | bytes 122888 | tf_op jit(solution)/shard_map/ppermute | solution.py:27
  116.2 15.8 %collective-permute-start.4 = (f32[40,256]{1,0:T(8,128)S(1)}, f32[40,256]{1,0:T(8,128)S(1)}, u32[]{:S(2)}, u32[]{:S(2)}) collective-permute-start(f32[40,256]{1,0:T(8,128)S(1)} %get-tuple-element.6), channel_id=1, source_target_pairs={{0,2},{2,4},{4,6},{6,8},{8,10},{10,12},{12,14},{14,16},{16,18},{18... | collective-permute-start | bytes 122888 | tf_op jit(solution)/shard_map/ppermute | solution.py:24
  121.6 10.4 %collective-permute-start.5 = (f32[40,256]{1,0:T(8,128)S(1)}, f32[40,256]{1,0:T(8,128)S(1)}, u32[]{:S(2)}, u32[]{:S(2)}) collective-permute-start(f32[40,256]{1,0:T(8,128)S(1)} %get-tuple-element.8), channel_id=1, source_target_pairs={{2,0},{4,2},{6,4},{8,6},{10,8},{12,10},{14,12},{16,14},{18,16},{20... | collective-permute-start | bytes 122888 | tf_op jit(solution)/shard_map/ppermute | solution.py:27
  181.6 6.9 %collective-permute-start.6 = (f32[20,256]{1,0:T(8,128)S(1)}, f32[20,256]{1,0:T(8,128)S(1)}, u32[]{:S(2)}, u32[]{:S(2)}) collective-permute-start(f32[20,256]{1,0:T(8,128)S(1)} %get-tuple-element.15), channel_id=1, source_target_pairs={{0,1},{1,2},{2,3},{3,4},{4,5},{5,6},{6,7},{7,8},{8,9},{9,10},{10,1... | collective-permute-start | bytes 61448 | tf_op jit(solution)/shard_map/ppermute | solution.py:24
  186.4 6.0 %collective-permute-start.7 = (f32[20,256]{1,0:T(8,128)S(1)}, f32[20,256]{1,0:T(8,128)S(1)}, u32[]{:S(2)}, u32[]{:S(2)}) collective-permute-start(f32[20,256]{1,0:T(8,128)S(1)} %get-tuple-element.16), channel_id=1, source_target_pairs={{1,0},{2,1},{3,2},{4,3},{5,4},{6,5},{7,6},{8,7},{9,8},{10,9},{11,1... | collective-permute-start | bytes 61448 | tf_op jit(solution)/shard_map/ppermute | solution.py:27
  203.5 3.1 %copy-start.3 = (f32[20,1024]{1,0:T(8,128)S(1)}, f32[20,1024]{1,0:T(8,128)}, u32[]{:S(2)}) copy-start(f32[20,1024]{1,0:T(8,128)} %reduce-scatter.2.cloned.1.call-done) | copy-start | bytes 245764
  206.9 5.5 %collective-permute-start.8 = (f32[20,256]{1,0:T(8,128)S(1)}, f32[20,256]{1,0:T(8,128)S(1)}, u32[]{:S(2)}, u32[]{:S(2)}) collective-permute-start(f32[20,256]{1,0:T(8,128)S(1)} %get-tuple-element.13), channel_id=1, source_target_pairs={{0,1},{1,2},{2,3},{3,4},{4,5},{5,6},{6,7},{7,8},{8,9},{9,10},{10,1... | collective-permute-start | bytes 61448 | tf_op jit(solution)/shard_map/ppermute | solution.py:24
  209.0 6.2 %collective-permute-start.9 = (f32[20,256]{1,0:T(8,128)S(1)}, f32[20,256]{1,0:T(8,128)S(1)}, u32[]{:S(2)}, u32[]{:S(2)}) collective-permute-start(f32[20,256]{1,0:T(8,128)S(1)} %get-tuple-element.14), channel_id=1, source_target_pairs={{1,0},{2,1},{3,2},{4,3},{5,4},{6,5},{7,6},{8,7},{9,8},{10,9},{11,1... | collective-permute-start | bytes 61448 | tf_op jit(solution)/shard_map/ppermute | solution.py:27
Sparse Core Ops, SparseCore 0:
  169.9 10.7 reduce-scatter.1
where the time goes:
time: 244 us; the launch traced here: 242 us
  local copies, waits for them, and re-layouts  109 us (45%)
  other arithmetic  34.9 us (14%)
  starting transfers between devices  32.2 us (13%)
  blocking collectives  29.9 us (12%)
  waiting for transfers between devices  17.6 us (7%)
  between operations  13.9 us (6%)
  matrix products  4.44 us (2%)
    gather x5, local copies, waits for them, and re-layouts, neighbour_terms(): jnp.take(padded, flat_index, axis=1).reshape(padded.shape[0], NEIGH, cells)  105 us
    all_gather x3, blocking collectives, derivative(): gathered = lax.all_gather(values, 'inst', axis=0, tiled=True)  25.5 us
    select_n x5, other arithmetic, neighbour_terms(): jnp.take(padded, flat_index, axis=1).reshape(padded.shape[0], NEIGH, cells)  22.9 us
    ppermute x5, starting transfers between devices, padded_2(): lax.ppermute(lax.slice_in_dim(block, block.shape[dim] - width, None, axis...  21.4 us
    ppermute x5, starting transfers between devices, padded_2(): lax.ppermute(lax.slice_in_dim(block, 0, width, axis=dim), axis, backward)  10.8 us
    reduce_scatter x1, waiting for transfers between devices, per_device(): lax.psum_scatter(partial_terms, 'inst', scatter_dimension=1, tiled=True)  10.7 us
    ppermute x5, waiting for transfers between devices, padded_2(): lax.ppermute(lax.slice_in_dim(block, 0, width, axis=dim), axis, backward)  6.83 us
    reduce_sum x5, other arithmetic, neighbour_terms(): return jnp.sum(face_weights[None, :, :] * picked, axis=1)  6.23 us
  transfers between devices with their start and end apart: 11, of which 3 were waited for; matrix products, arithmetic and copies ran while one was open for 2% of the time, Pallas kernels for 0%

commit v1 on v0

v1 whole, which is shorter than its diff:
```python
import functools

import jax
import jax.numpy as jnp
import numpy as np
from jax import lax
from jax.experimental import pallas as pl
from jax.experimental.pallas import tpu as pltpu
from jax.sharding import PartitionSpec as P

NI = 16
NC = 4
COMP = 5
NEIGH = 4
SWEEPS_FINE = 2
SWEEPS_COARSE = 3
PLANE = 256
FREQ = 0.15
RELAX = 0.6
KEEP = 1.0 - RELAX

LANES = 128
PB = PLANE // LANES
MODES = 16
HIGH = lax.Precision.HIGHEST

FV = SWEEPS_FINE * PB
FS = (SWEEPS_FINE - 1) * PB
MV = (SWEEPS_FINE + SWEEPS_COARSE) * PB
MS = MV - PB


def up8(count):
    return -(-count // 8) * 8


def row_map(own):
    rows = [divmod(r, COMP) for r in range(own)]
    rows += [None] * (up8(own) - own)
    other = NI * COMP - own
    rows += [divmod(own + r, COMP) for r in range(other)]
    rows += [None] * (up8(other) - other)
    return rows


def constants(own):
    rows = row_map(own)
    count = len(rows)
    derive = np.zeros((count, count))
    restrict = np.zeros((MODES, count))
    prolong = np.zeros((count, MODES))
    for i, left in enumerate(rows):
        if left is None:
            continue
        n, c = left
        phase = 2.0 * np.pi * n / NI
        shape = (1.0, np.cos(phase), np.sin(phase))
        for h in range(3):
            restrict[h * COMP + c, i] = shape[h] * (1.0 if h == 0 else 2.0) / NI
            prolong[i, h * COMP + c] = shape[h]
        for j, right in enumerate(rows):
            if right is not None and right[1] == c and right[0] != n:
                gap = n - right[0]
                derive[i, j] = 0.5 * (-1.0) ** gap / np.tan(np.pi * gap / NI)
    mode_derive = np.zeros((MODES, MODES))
    for c in range(COMP):
        mode_derive[COMP + c, 2 * COMP + c] = 1.0
        mode_derive[2 * COMP + c, COMP + c] = -1.0
    return [np.asarray(m, np.float32) for m in (derive, restrict, prolong, mode_derive)]


def dot(a, b):
    return jnp.dot(a, b, precision=HIGH, preferred_element_type=jnp.float32)


def lanes(start, count=1):
    return slice(start * LANES, (start + count) * LANES)


def lane_ds(block):
    return pl.ds(pl.multiple_of(block * LANES, LANES), LANES)


def build_table(idx_ref, wt_ref, at, near, bw, bf):
    target = near + lax.broadcasted_iota(jnp.int32, near.shape, 1)
    slot = lax.broadcasted_iota(jnp.int32, near.shape, 0)
    base = (target >> 7) + jnp.where((slot & 1) == 0, PB, 0)
    idx_ref[at, 0:NEIGH, :] = target & (LANES - 1)
    for j in range(PB + 1):
        wt_ref[at, NEIGH * j : NEIGH * (j + 1), :] = jnp.where(base == j, bw, 0.0)
    wt_ref[at, NEIGH * (PB + 1) : NEIGH * (PB + 1) + 1, :] = bf


def stencil(src_ref, center, idx_ref, wt_ref, at, groups):
    sources = [
        [src_ref[8 * g : 8 * g + 8, lane_ds(center + j - PB)] for j in range(2 * PB + 1)]
        for g in groups
    ]
    sums = [None] * len(groups)
    for k in range(NEIGH):
        index = idx_ref[at, pl.ds(k, 8, stride=0), :]
        for j in range(PB + 1):
            weight = wt_ref[at, pl.ds(NEIGH * j + k, 8, stride=0), :]
            for g in range(len(groups)):
                source = sources[g][j + (PB if k % 2 else 0)]
                term = weight * jnp.take_along_axis(source, index, axis=1)
                sums[g] = term if sums[g] is None else sums[g] + term
    return sums


def coefficient(wt_ref, at):
    return wt_ref[at, pl.ds(NEIGH * (PB + 1), 8, stride=0), :]


def blocks_loop(count, body, unroll):
    def step(i, carry):
        body(i)
        return carry

    lax.fori_loop(0, count, step, 0, unroll=min(unroll, count))


def pack_kernel(own_pad, init_ref, src_ref, near_ref, face_ref, damp_ref, restrict_ref,
                a_ref, b_ref, scaled_ref, coef_ref, mode_ref):
    cells = init_ref.shape[1]
    nblk = cells // LANES
    face = face_ref[...]
    diagonal = damp_ref[...] + jnp.sum(face, axis=0, keepdims=True)
    inverse = RELAX / diagonal
    bw = inverse * face
    coef_ref[0:NEIGH, :] = bw
    coef_ref[NEIGH : NEIGH + 1, :] = FREQ * inverse
    for g in range(own_pad // 8):
        scaled_ref[8 * g : 8 * g + 8, :] = src_ref[8 * g : 8 * g + 8, :] * inverse
    restrict = restrict_ref[:, 0:own_pad]
    mode_ref[...] = dot(restrict, scaled_ref[...])
    low_modes = dot(restrict, init_ref[:, lanes(FV, nblk - 2 * FV)])
    groups = own_pad // 8
    near = near_ref[...].astype(jnp.float32)

    def pack(out, high):
        t = 0
        first = nblk - FV if high else 0
        for g in range(groups):
            for d in range(FV):
                out[t] = init_ref[8 * g : 8 * g + 8, lanes(first + d)]
                t += 1
        first = nblk - FS if high else 0
        for g in range(groups):
            for d in range(FS):
                out[t] = scaled_ref[8 * g : 8 * g + 8, lanes(first + d)]
                t += 1
        first = nblk - MV if high else FV
        for g in range(MODES // 8):
            for d in range(MV - FV):
                out[t] = low_modes[8 * g : 8 * g + 8, lanes(first + d - FV)]
                t += 1
        first = nblk - MS if high else FS
        for g in range(MODES // 8):
            for d in range(MS - FS):
                out[t] = mode_ref[8 * g : 8 * g + 8, lanes(first + d)]
                t += 1
        first = nblk - MS if high else 0
        for d in range(MS):
            out[t, 0:NEIGH, :] = coef_ref[0:NEIGH, lanes(first + d)]
            out[t, NEIGH : 2 * NEIGH, :] = near[:, lanes(first + d)]
            t += 1
        for d in range(MS):
            out[t, d : d + 1, :] = coef_ref[NEIGH : NEIGH + 1, lanes(first + d)]

    odd = lax.axis_index("cell") & 1

    @pl.when(odd == 0)
    def _():
        pack(a_ref, True)
        pack(b_ref, False)

    @pl.when(odd == 1)
    def _():
        pack(a_ref, False)
        pack(b_ref, True)


def halo_tiles(own_pad):
    groups = own_pad // 8
    return groups * (FV + FS) + (MODES // 8) * (MV - FV + MS - FS) + MS + 1


def inner_kernel(own_pad, init_ref, scaled_ref, near_ref, coef_ref, derive_ref, restrict_ref,
                 own_ref, cross_ref, v1_ref, m1_ref, m2_ref, idx_ref, wt_ref,
                 first, deriv):
    cells = init_ref.shape[1]
    nblk = cells // LANES
    rows = derive_ref.shape[0]
    own_groups = range(own_pad // 8)
    all_groups = range(rows // 8)
    for b in range(nblk):
        build_table(idx_ref, wt_ref, b, near_ref[:, lanes(b)],
                    coef_ref[0:NEIGH, lanes(b)], coef_ref[NEIGH : NEIGH + 1, lanes(b)])
    width1 = nblk - 2 * PB
    deriv[:, 0 : width1 * LANES] = dot(derive_ref[:, 0:own_pad], init_ref[:, lanes(PB, width1)])

    def sweep1(i):
        b = i + PB
        sums = stencil(init_ref, b, idx_ref, wt_ref, b, own_groups)
        bf = coefficient(wt_ref, b)
        for g in all_groups:
            part = slice(8 * g, 8 * g + 8)
            value = -bf * deriv[part, lane_ds(i)]
            if g in own_groups:
                value = value + (KEEP * init_ref[part, lane_ds(b)] + scaled_ref[part, lane_ds(b)] + sums[g])
            first[part, lane_ds(i)] = value

    blocks_loop(width1, sweep1, 2)
    width2 = nblk - 4 * PB
    deriv[:, 0 : width2 * LANES] = dot(derive_ref[...], first[:, lanes(PB, width2)])

    def sweep2(i):
        b = i + 2 * PB
        sums = stencil(first, i + PB, idx_ref, wt_ref, b, all_groups)
        bf = coefficient(wt_ref, b)
        for g in all_groups:
            part = slice(8 * g, 8 * g + 8)
            value = KEEP * first[part, lane_ds(i + PB)] - bf * deriv[part, lane_ds(i)] + sums[g]
            if g in own_groups:
                own_ref[part, lane_ds(i)] = value + scaled_ref[part, lane_ds(b)]
            else:
                cross_ref[8 * g - own_pad : 8 * g + 8 - own_pad, lane_ds(i)] = value

    blocks_loop(width2, sweep2, 2)
    v1_ref[:, lanes(0, 2 * PB)] = first[:, lanes(0, 2 * PB)]
    v1_ref[:, lanes(2 * PB, 2 * PB)] = first[:, lanes(width1 - 2 * PB, 2 * PB)]
    m1_ref[...] = dot(restrict_ref[...], first[...])
    m2_ref[...] = dot(restrict_ref[:, 0:own_pad], own_ref[...]) + dot(
        restrict_ref[:, own_pad:], cross_ref[...]
    )


def outer_kernel(own_pad, a_ref, b_ref, init_ref, scaled_ref, smode_ref, own_ref, v1_ref,
                 m1i_ref, m2i_ref, idx_in, wt_in, derive_ref, restrict_ref, prolong_ref, turn_ref,
                 edge_ref, mid_ref, send_ref,
                 v0e, se, v1e, v2e, deriv, m0x, sx, m1x, m2x, rx, c1x, c2x, dm, idx, wt):
    cells = init_ref.shape[1]
    nblk = cells // LANES
    rows = derive_ref.shape[0]
    own_groups = range(own_pad // 8)
    all_groups = range(rows // 8)
    restrict = restrict_ref[...]
    derive = derive_ref[...]
    turn = turn_ref[...]
    idx[MS : MS + nblk] = idx_in[...]
    wt[MS : MS + nblk] = wt_in[...]
    v0e[:, lanes(FV, 2 * PB)] = init_ref[:, lanes(0, 2 * PB)]
    v0e[:, lanes(FV + 2 * PB, 2 * PB)] = init_ref[:, lanes(nblk - 2 * PB, 2 * PB)]
    se[:, lanes(FS, 2 * PB)] = scaled_ref[:, lanes(0, 2 * PB)]
    se[:, lanes(FS + 2 * PB, 2 * PB)] = scaled_ref[:, lanes(nblk - 2 * PB, 2 * PB)]
    sx[:, lanes(MS, nblk)] = smode_ref[...]
    v1e[:, lanes(2 * PB, 2 * PB)] = v1_ref[:, lanes(0, 2 * PB)]
    v1e[:, lanes(4 * PB, 2 * PB)] = v1_ref[:, lanes(2 * PB, 2 * PB)]
    m1x[:, lanes(MS + PB, nblk - 2 * PB)] = m1i_ref[...]
    far2 = MS - PB
    m2x[:, lanes(far2 + 2 * PB, nblk - 4 * PB)] = m2i_ref[...]

    def unpack(tiles, right):
        t = 0
        at = FV + 4 * PB if right else 0
        for g in own_groups:
            for d in range(FV):
                v0e[8 * g : 8 * g + 8, lanes(at + d)] = tiles[t]
                t += 1
        at = FS + 4 * PB if right else 0
        for g in own_groups:
            for d in range(FS):
                se[8 * g : 8 * g + 8, lanes(at + d)] = tiles[t]
                t += 1
        at = MV + FV if right else 0
        for g in range(MODES // 8):
            for d in range(MV - FV):
                m0x[8 * g : 8 * g + 8, lanes(at + d)] = tiles[t]
                t += 1
        at = MS + nblk + FS if right else 0
        for g in range(MODES // 8):
            for d in range(MS - FS):
                sx[8 * g : 8 * g + 8, lanes(at + d)] = tiles[t]
                t += 1
        at = MS + nblk if right else 0
        for d in range(MS):
            near = tiles[t + d, NEIGH : 2 * NEIGH, :].astype(jnp.int32)
            build_table(idx, wt, at + d, near, tiles[t + d, 0:NEIGH, :],
                        tiles[t + MS, d : d + 1, :])

    odd = lax.axis_index("cell") & 1

    @pl.when(odd == 0)
    def _():
        unpack(a_ref, True)
        unpack(b_ref, False)

    @pl.when(odd == 1)
    def _():
        unpack(a_ref, False)
        unpack(b_ref, True)

    restrict_own = restrict_ref[:, 0:own_pad]
    m0x[:, lanes(MV - FV, FV)] = dot(restrict_own, v0e[:, lanes(0, FV)])
    m0x[:, lanes(MV, FV)] = dot(restrict_own, v0e[:, lanes(FV + 4 * PB, FV)])
    sx[:, lanes(MS - FS, FS)] = dot(restrict_own, se[:, lanes(0, FS)])
    sx[:, lanes(MS + nblk, FS)] = dot(restrict_own, se[:, lanes(FS + 4 * PB, FS)])

    span = 2 * PB
    for side in range(2):
        from0 = side * (FV + 2 * PB) + PB
        deriv[:, lanes(side * span, span)] = dot(
            derive_ref[:, 0:own_pad], v0e[:, lanes(from0, span)]
        )
    for side in range(2):
        from0 = side * (FV + 2 * PB) + PB
        from_s = side * (FS + 3 * PB)
        table = MS - PB + side * nblk
        to = side * 6 * PB

        def sweep1(i, from0=from0, from_s=from_s, table=table, to=to, side=side):
            sums = stencil(v0e, i + from0, idx, wt, i + table, own_groups)
            bf = coefficient(wt, i + table)
            for g in all_groups:
                part = slice(8 * g, 8 * g + 8)
                value = -bf * deriv[part, lane_ds(i + side * span)]
                if g in own_groups:
                    value = value + (
                        KEEP * v0e[part, lane_ds(i + from0)] + se[part, lane_ds(i + from_s)] + sums[g]
                    )
                v1e[part, lane_ds(i + to)] = value

        blocks_loop(span, sweep1, 2)
    m1x[:, lanes(MS - PB, span)] = dot(restrict, v1e[:, lanes(0, span)])
    m1x[:, lanes(MS - PB + nblk, span)] = dot(restrict, v1e[:, lanes(6 * PB, span)])

    def relax(src, from_, out, to, table, count, source=None):
        dm[:, 0 : count * LANES] = dot(turn, src[:, lanes(from_, count)])
        rhs_ref, rhs_at, keep = source

        def body(i):
            sums = stencil(src, i + from_, idx, wt, i + table, range(MODES // 8))
            bf = coefficient(wt, i + table)
            for g in range(MODES // 8):
                part = slice(8 * g, 8 * g + 8)
                out[part, lane_ds(i + to)] = (
                    keep * src[part, lane_ds(i + from_)]
                    + rhs_ref[part, lane_ds(i + rhs_at)]
                    - bf * dm[part, lane_ds(i)]
                    + sums[g]
                )

        blocks_loop(count, body, 4)

    far = MS - PB
    relax(m0x, PB, m1x, 0, 0, far, (sx, 0, KEEP))
    right = MS + nblk + PB
    relax(m0x, MV + PB, m1x, right, right, far, (sx, right, KEEP))

    for side in range(2):
        deriv[:, lanes(side * span, span)] = dot(derive, v1e[:, lanes(PB + side * 4 * PB, span)])
    for side in range(2):
        from1 = PB + side * 4 * PB
        from_s = FS + side * 2 * PB
        table = MS + side * (nblk - 2 * PB)

        def sweep2(i, from1=from1, from_s=from_s, table=table, side=side):
            sums = stencil(v1e, i + from1, idx, wt, i + table, all_groups)
            bf = coefficient(wt, i + table)
            for g in all_groups:
                part = slice(8 * g, 8 * g + 8)
                value = (
                    KEEP * v1e[part, lane_ds(i + from1)]
                    - bf * deriv[part, lane_ds(i + side * span)]
                    + sums[g]
                )
                if g in own_groups:
                    value = value + se[part, lane_ds(i + from_s)]
                v2e[part, lane_ds(i + side * span)] = value

        blocks_loop(span, sweep2, 2)
    for side in range(2):
        m2x[:, lanes(far2 + side * (nblk - 2 * PB), span)] = dot(restrict, v2e[:, lanes(side * span, span)])

    relax(m1x, PB, m2x, 0, PB, far2, (sx, PB, KEEP))
    relax(m1x, MS + nblk, m2x, far2 + nblk, MS + nblk, far2, (sx, MS + nblk, KEEP))

    deep = MS - 2 * PB
    relax(m2x, PB, rx, 0, 2 * PB, nblk + 2 * deep, (sx, 2 * PB, -RELAX))
    relax(rx, PB, c1x, 0, 3 * PB, nblk + 2 * PB, (rx, PB, KEEP))
    relax(c1x, PB, c2x, 0, 4 * PB, nblk, (rx, 2 * PB, KEEP))

    prolong = prolong_ref[...]
    lead = (rows - own_pad)
    for side in range(2):
        part = lanes(side * span, span)
        lifted = v2e[:, part] + dot(prolong, c2x[:, lanes(side * (nblk - 2 * PB), span)])
        edge_ref[:, part] = lifted[0:own_pad, :]
        send_ref[0:lead, part] = lifted[own_pad:, :]
    middle = lanes(2 * PB, nblk - 4 * PB)
    send_ref[lead:, :] = c2x[:, middle]
    mid_ref[...] = own_ref[...] + dot(prolong_ref[0:own_pad, :], c2x[:, middle])


def final_kernel(count, edge_ref, mid_ref, lift_ref, *refs):
    out_ref = refs[-1]
    own_pad = edge_ref.shape[0]
    nblk = out_ref.shape[1] // LANES
    span = 2 * PB
    edge = edge_ref[...]
    mid = mid_ref[...]
    for k in range(count):
        early, late = refs[2 * k], refs[2 * k + 1]
        edge = edge + late[0:own_pad, :]
        mid = mid + early[...] + dot(lift_ref[k], late[own_pad:, :])
    out_ref[:, lanes(0, span)] = edge[:, lanes(0, span)]
    out_ref[:, lanes(nblk - span, span)] = edge[:, lanes(span, span)]
    out_ref[:, lanes(span, nblk - 2 * span)] = mid


def vm(*shape):
    return pltpu.VMEM(shape, jnp.float32)


def f32(*shape):
    return jax.ShapeDtypeStruct(shape, jnp.float32)


def call(kernel, name, out_shape, scratch, cost_us, *args):
    whole = pl.BlockSpec(memory_space=pltpu.VMEM)
    single = not isinstance(out_shape, (tuple, list))
    return pl.pallas_call(
        kernel,
        name=name,
        out_shape=out_shape,
        in_specs=[whole] * len(args),
        out_specs=whole if single else [whole] * len(out_shape),
        scratch_shapes=scratch,
        compiler_params=pltpu.CompilerParams(vmem_limit_bytes=16 * 1024 * 1024),
        cost_estimate=pl.CostEstimate(
            flops=int(cost_us * 1e8), bytes_accessed=int(cost_us * 3e6), transcendentals=0
        ),
    )(*args)


def per_device(initial, source, neighbors, face_weights, damping):
    own, cells = initial.shape
    nblk = cells // LANES
    inst_count = lax.axis_size("inst")
    cell_count = lax.axis_size("cell")
    own_pad = up8(own)
    derive, restrict, prolong, turn = constants(own)
    rows = derive.shape[0]
    cross = rows - own_pad
    if own_pad != own:
        initial = jnp.pad(initial, ((0, own_pad - own), (0, 0)))
        source = jnp.pad(source, ((0, own_pad - own), (0, 0)))
    tiles = halo_tiles(own_pad)
    span = 2 * PB
    mid_blocks = nblk - 2 * span
    slots = NEIGH * (PB + 1) + 4

    pack_a, pack_b, scaled, coef, smode = call(
        functools.partial(pack_kernel, own_pad), "pack",
        [f32(tiles, 8, LANES), f32(tiles, 8, LANES), f32(own_pad, cells), f32(8, cells),
         f32(MODES, cells)],
        [], 2, initial, source, neighbors, face_weights, damping.reshape(1, cells),
        jnp.asarray(restrict),
    )
    near_pairs = [(i, i ^ 1) for i in range(cell_count) if i ^ 1 < cell_count]
    far_pairs = []
    for i in range(1, cell_count - 1, 2):
        far_pairs += [(i, i + 1), (i + 1, i)]
    halo_b = lax.ppermute(pack_b, "cell", far_pairs)
    halo_a = lax.ppermute(pack_a, "cell", near_pairs)

    own_mid, cross_mid, v1, m1, m2, idx, wt = call(
        functools.partial(inner_kernel, own_pad), "inner",
        [f32(own_pad, mid_blocks * LANES), f32(cross, mid_blocks * LANES),
         f32(rows, 4 * PB * LANES), f32(MODES, (nblk - 2 * PB) * LANES),
         f32(MODES, mid_blocks * LANES),
         jax.ShapeDtypeStruct((nblk, 8, LANES), jnp.int32), f32(nblk, slots, LANES)],
        [vm(rows, (nblk - 2 * PB) * LANES), vm(rows, (nblk - 2 * PB) * LANES)], 5,
        initial, scaled, neighbors, coef, jnp.asarray(derive), jnp.asarray(restrict),
    )

    def share(array, k):
        if cross == own_pad:
            return array
        part = lax.slice_in_dim(array, (k - 1) * own, k * own, axis=0)
        return jnp.pad(part, ((0, own_pad - own), (0, 0)))

    def shift(k):
        return [(i, (i + k) % inst_count) for i in range(inst_count)]

    early = [lax.ppermute(share(cross_mid, k), "inst", shift(k)) for k in range(1, inst_count)]

    ext = nblk + 2 * MS
    edge, mid, send = call(
        functools.partial(outer_kernel, own_pad), "outer",
        [f32(own_pad, 2 * span * LANES), f32(own_pad, mid_blocks * LANES),
         f32(cross + MODES, 2 * span * LANES)],
        [vm(own_pad, 2 * (FV + 2 * PB) * LANES), vm(own_pad, 2 * (FS + 2 * PB) * LANES),
         vm(rows, 8 * PB * LANES), vm(rows, 2 * span * LANES), vm(rows, 2 * span * LANES),
         vm(MODES, 2 * MV * LANES), vm(MODES, ext * LANES), vm(MODES, ext * LANES),
         vm(MODES, (ext - 2 * PB) * LANES), vm(MODES, (ext - 4 * PB) * LANES),
         vm(MODES, (nblk + 2 * PB) * LANES), vm(MODES, cells), vm(MODES, ext * LANES),
         pltpu.VMEM((ext, 8, LANES), jnp.int32), vm(ext, slots, LANES)],
        8, halo_a, halo_b, initial, scaled, smode, own_mid, v1, m1, m2, idx, wt,
        jnp.asarray(derive), jnp.asarray(restrict), jnp.asarray(prolong), jnp.asarray(turn),
    )

    def share_late(k):
        if cross == own_pad:
            return send
        return jnp.concatenate([share(send[:cross], k), send[cross:]], axis=0)

    late = [lax.ppermute(share_late(k), "inst", shift(k)) for k in range(1, inst_count)]
    other = prolong[own_pad:]
    lift = np.zeros((inst_count - 1, own_pad, MODES), np.float32)
    for k in range(1, inst_count):
        lift[k - 1, :own] = other[(k - 1) * own : k * own]
    received = [r for pair in zip(early, late) for r in pair]
    out = call(
        functools.partial(final_kernel, inst_count - 1), "final", f32(own_pad, cells), [], 1,
        edge, mid, jnp.asarray(lift), *received,
    )
    return out[:own] if own_pad != own else out


def solution(mesh):
    return jax.shard_map(
        per_device,
        mesh=mesh,
        in_specs=(
            P("inst", "cell"),
            P("inst", "cell"),
            P(None, "cell"),
            P(None, "cell"),
            P("cell"),
        ),
        out_specs=P("inst", "cell"),
        check_vma=False,
    )
```

time: 244 us -> 37.7 us (0.15)
  local copies, waits for them, and re-layouts: 109 us -> 4.87 us
  other arithmetic: 34.9 us -> 0 us
  blocking collectives: 29.9 us -> 0 us
  starting transfers between devices: 32.2 us -> 5.21 us
  Pallas kernels: 0 us -> 15.9 us
  between operations: 13.9 us -> 0.06 us
  waiting for transfers between devices: 17.6 us -> 11.2 us
  matrix products: 4.44 us -> 0 us
    gather x5 -> x0, local copies, waits for them, and re-layouts: 105 us -> none  [neighbour_terms(): jnp.take(padded, flat_index, axis=1).reshape(padded.shape[0], NEIGH, cells)]
    all_gather x4 -> x0, blocking collectives: 29.9 us -> none  [the longest x3 25.5 us: derivative(): gathered = lax.all_gather(values, 'inst', axis=0, tiled=True)]
    ppermute x10 -> x4, starting transfers between devices: 32.2 us -> 5.21 us  [the longest x1 3.03 us: per_device(): halo_b = lax.ppermute(pack_b, 'cell', far_pairs)]
    select_n x7 -> x0, other arithmetic: 23.1 us -> none  [the longest x5 22.9 us: neighbour_terms(): jnp.take(padded, flat_index, axis=1).reshape(padded.shape[0], NEIGH, cells)]
    pallas_call x0 -> x4, Pallas kernels: none -> 15.9 us  [call(): pl.pallas_call(kernel, name=name, out_shape=out_shape, in_specs=[whole] *...]
    reduce_scatter x1 -> x0, waiting for transfers between devices: 10.7 us -> none  [per_device(): lax.psum_scatter(partial_terms, 'inst', scatter_dimension=1, tiled=True)]
    reduce_sum x6 -> x0, other arithmetic: 7.01 us -> none  [the longest x5 6.23 us: neighbour_terms(): return jnp.sum(face_weights[None, :, :] * picked, axis=1)]
    unnamed x9 -> x22, local copies, waits for them, and re-layouts: 0.03 us -> 4.87 us
  transfers between devices with their start and end apart: 11 -> 4, of which waited for: 3 -> 2; matrix products, arithmetic and copies ran while one was open for 2% -> 0% of each run, Pallas kernels for 0% -> 11%
where the time goes in v1:
time: 37.7 us; the launch traced here: 37.2 us
  Pallas kernels  15.9 us (42%)
  waiting for transfers between devices  11.2 us (30%)
  starting transfers between devices  5.21 us (14%)
  local copies, waits for them, and re-layouts  4.87 us (13%)
    pallas_call x4, Pallas kernels, call(): pl.pallas_call(kernel, name=name, out_shape=out_shape, in_specs=[whole] *...  15.9 us
    ppermute x1, waiting for transfers between devices, per_device(): lax.ppermute(share(cross_mid, k), 'inst', shift(k))  8.12 us
    unnamed x22, local copies, waits for them, and re-layouts  4.87 us
    ppermute x1, waiting for transfers between devices, per_device(): halo_b = lax.ppermute(pack_b, 'cell', far_pairs)  3.11 us
    ppermute x1, starting transfers between devices, per_device(): halo_b = lax.ppermute(pack_b, 'cell', far_pairs)  3.03 us
    ppermute x1, starting transfers between devices, per_device(): lax.ppermute(share(cross_mid, k), 'inst', shift(k))  1.21 us
  transfers between devices with their start and end apart: 4, of which 2 were waited for; matrix products, arithmetic and copies ran while one was open for 0% of the time, Pallas kernels for 11%

profile of v1, /device:TPU:19, one launch (start us, length us, event | category | flops | bytes accessed | tf_op | source)
XLA Modules:
  0.0 37.2 jit_solution(11300548844870107108)
XLA Ops:
  0.0 0.0 copy-start.9
  0.0 0.7 %copy-done.9 = f32[16,80]{1,0:T(8,128)S(1)} copy-done((f32[16,80]{1,0:T(8,128)S(1)}, f32[16,80]{1,0:T(8,128)}, u32[]{:S(2)}) %copy-start.9) | copy-done | bytes 5144
  0.7 0.0 copy-start.1
  0.7 1.0 %copy-done.1 = f32[40,2048]{1,0:T(8,128)S(1)} copy-done((f32[40,2048]{1,0:T(8,128)S(1)}, f32[40,2048]{1,0:T(8,128)}, u32[]{:S(2)}) %copy-start.1) | copy-done | bytes 327704
  1.7 0.0 copy-start.2
  1.7 1.0 %copy-done.2 = f32[40,2048]{1,0:T(8,128)S(1)} copy-done((f32[40,2048]{1,0:T(8,128)S(1)}, f32[40,2048]{1,0:T(8,128)}, u32[]{:S(2)}) %copy-start.2) | copy-done | bytes 327704
  2.6 0.0 copy-start.3
  2.6 0.8 %copy-done.3 = f32[4,2048]{1,0:T(4,128)S(1)} copy-done((f32[4,2048]{1,0:T(4,128)S(1)}, f32[4,2048]{1,0:T(4,128)}, u32[]{:S(2)}) %copy-start.3) | copy-done | bytes 32792
  3.4 0.0 copy-start.4
  3.4 0.8 %copy-done.4 = s32[4,2048]{1,0:T(4,128)S(1)} copy-done((s32[4,2048]{1,0:T(4,128)S(1)}, s32[4,2048]{1,0:T(4,128)}, u32[]{:S(2)}) %copy-start.4) | copy-done | bytes 32792
  4.2 0.0 copy-start.6
  4.2 0.7 %copy-done.6 = f32[2048]{0:T(1024)S(1)} copy-done((f32[2048]{0:T(1024)S(1)}, f32[2048]{0:T(1024)}, u32[]{:S(2)}) %copy-start.6) | copy-done | bytes 8216
  4.9 0.0 copy-start.5
  4.9 0.0 copy-start.7
  4.9 0.5 %pack.1 = (f32[63,8,128]{2,1,0:T(8,128)S(1)}, f32[63,8,128]{2,1,0:T(8,128)S(1)}, f32[40,2048]{1,0:T(8,128)S(1)}, f32[8,2048]{1,0:T(8,128)S(1)}, f32[16,2048]{1,0:T(8,128)S(1)}) custom-call(f32[40,2048]{1,0:T(8,128)S(1)} %copy-done.2, f32[40,2048]{1,0:T(8,128)S(1)} %copy-done.1, s32[4,2048]{1,0:T(4,128)S(1)} %copy-done.4, f32[4,2048]{1,0:T(4,128)S(1)} %copy-done.3, ...), custom_call_target="tpu_custom_call" | custom-call | flops 200000000 | bytes 6000000 | tf_op jit(solution)/shard_map/pack/pallas_call | solution.py:433
  5.3 0.7 %collective-permute-start = (f32[63,8,128]{2,1,0:T(8,128)S(1)}, f32[63,8,128]{2,1,0:T(8,128)S(1)}, u32[]{:S(2)}, u32[]{:S(2)}) collective-permute-start(f32[63,8,128]{2,1,0:T(8,128)S(1)} %get-tuple-element.20), channel_id=1, source_target_pairs={{0,2},{2,0},{4,6},{6,4},{8,10},{10,8},{12,14},{14,12},{16,18},{18,... | collective-permute-start | bytes 774152 | tf_op jit(solution)/shard_map/ppermute | solution.py:476
  6.0 3.0 %collective-permute-start.1 = (f32[63,8,128]{2,1,0:T(8,128)S(1)}, f32[63,8,128]{2,1,0:T(8,128)S(1)}, u32[]{:S(2)}, u32[]{:S(2)}) collective-permute-start(f32[63,8,128]{2,1,0:T(8,128)S(1)} %get-tuple-element.21), channel_id=1, source_target_pairs={{2,4},{4,2},{6,8},{8,6},{10,12},{12,10},{14,16},{16,14},{18,20},{2... | collective-permute-start | bytes 774152 | tf_op jit(solution)/shard_map/ppermute | solution.py:475
  9.0 0.0 copy-done.5
  9.0 0.0 copy-done.7
  9.0 0.0 copy-start.8
  9.0 4.2 %inner.1 = (f32[40,1024]{1,0:T(8,128)S(1)}, f32[40,1024]{1,0:T(8,128)S(1)}, f32[80,1024]{1,0:T(8,128)S(1)}, f32[16,1536]{1,0:T(8,128)S(1)}, f32[16,1024]{1,0:T(8...) custom-call(f32[40,2048]{1,0:T(8,128)S(1)} %copy-done.2, f32[40,2048]{1,0:T(8,128)S(1)} %get-tuple-element.22.scaled_ref, ...), custom_call_target="tpu_custom_call" | custom-call | flops 500000000 | bytes 15000000 | tf_op jit(solution)/shard_map/inner/pallas_call | solution.py:433
  13.3 0.0 copy-start.10
  13.3 0.0 collective-permute-done.a_ref
  13.3 3.1 %collective-permute-done.1.b_ref = f32[63,8,128]{2,1,0:T(8,128)S(1)} collective-permute-done((f32[63,8,128]{2,1,0:T(8,128)S(1)}, f32[63,8,128]{2,1,0:T(8,128)S(1)}, u32[]{:S(2)}, u32[]{:S(2)}) %collective-permute-start.1) | collective-permute-done | bytes 258080 | tf_op jit(solution)/shard_map/ppermute | solution.py:475
  16.4 0.0 copy-done.8
  16.4 0.0 copy-done.10
  16.4 0.0 copy-start
  16.4 10.2 %outer.1 = (f32[40,1024]{1,0:T(8,128)S(1)}, f32[40,1024]{1,0:T(8,128)S(1)}, f32[56,1024]{1,0:T(8,128)S(1)}) custom-call(f32[63,8,128]{2,1,0:T(8,128)S(1)} %collective-permute-done.a_ref, f32[63,8,128]{2,1,0:T(8,128)S(1)} %collective-permute-done.1.b_ref, f32[40,2048]{1,0:T(8,128)S(1)} %copy-done.2, f32[40,2048]{1,0:T(8,128)S(1)} %get-tuple-element.22.scaled_ref, ...), custom_call_target="tpu_custom_call" | custom-call | flops 800000000 | bytes 24000000 | tf_op jit(solution)/shard_map/outer/pallas_call | solution.py:433
  26.6 0.3 collective-permute-start.3
  26.9 1.2 %collective-permute-start.2 = (f32[40,1024]{1,0:T(8,128)S(1)}, f32[40,1024]{1,0:T(8,128)S(1)}, u32[]{:S(2)}, u32[]{:S(2)}) collective-permute-start(f32[40,1024]{1,0:T(8,128)S(1)} %get-tuple-element.33), channel_id=1, source_target_pairs={{0,1},{1,0},{2,3},{3,2},{4,5},{5,4},{6,7},{7,6},{8,9},{9,8},{10,11... | collective-permute-start | bytes 491528 | tf_op jit(solution)/shard_map/ppermute | solution.py:497
  28.1 8.1 %collective-permute-done.2.refs_0_ = f32[40,1024]{1,0:T(8,128)S(1)} collective-permute-done((f32[40,1024]{1,0:T(8,128)S(1)}, f32[40,1024]{1,0:T(8,128)S(1)}, u32[]{:S(2)}, u32[]{:S(2)}) %collective-permute-start.2) | collective-permute-done | bytes 163872 | tf_op jit(solution)/shard_map/ppermute | solution.py:497
  36.2 0.0 collective-permute-done.3.refs_1_
  36.3 0.0 copy-done
  36.3 1.0 %final.1 = f32[40,2048]{1,0:T(8,128)} custom-call(f32[40,1024]{1,0:T(8,128)S(1)} %get-tuple-element.31.edge_ref, f32[40,1024]{1,0:T(8,128)S(1)} %get-tuple-element.32.mid_ref, f32[1,40,16]{2,1,0:T(8,128)S(1)} %copy-done, f32[40,1024]{1,0:T(8,128)S(1)} %collective-permute-done.2.refs_0_, f32[56,1024]{1,0:T(8,128)S(1)} %collective-permute-done.3.refs_1_), custom_call_target="tpu_custom_call" | custom-call | flops 100000000 | bytes 3000000 | tf_op jit(solution)/shard_map/final/pallas_call | solution.py:433
Async XLA Ops:
  0.0 0.7 %copy-start.9 = (f32[16,80]{1,0:T(8,128)S(1)}, f32[16,80]{1,0:T(8,128)}, u32[]{:S(2)}) copy-start(f32[16,80]{1,0:T(8,128)} %constant.10.clone.restrict_ref) | copy-start | bytes 15364
  0.7 1.0 %copy-start.1 = (f32[40,2048]{1,0:T(8,128)S(1)}, f32[40,2048]{1,0:T(8,128)}, u32[]{:S(2)}) copy-start(f32[40,2048]{1,0:T(8,128)} %src_ref.1) | copy-start | bytes 983044
  1.7 1.0 %copy-start.2 = (f32[40,2048]{1,0:T(8,128)S(1)}, f32[40,2048]{1,0:T(8,128)}, u32[]{:S(2)}) copy-start(f32[40,2048]{1,0:T(8,128)} %init_ref.5) | copy-start | bytes 983044
  2.6 0.8 %copy-start.3 = (f32[4,2048]{1,0:T(4,128)S(1)}, f32[4,2048]{1,0:T(4,128)}, u32[]{:S(2)}) copy-start(f32[4,2048]{1,0:T(4,128)} %face_ref.1) | copy-start | bytes 98308
  3.4 0.8 %copy-start.4 = (s32[4,2048]{1,0:T(4,128)S(1)}, s32[4,2048]{1,0:T(4,128)}, u32[]{:S(2)}) copy-start(s32[4,2048]{1,0:T(4,128)} %near_ref.3) | copy-start | bytes 98308
  4.2 0.7 %copy-start.6 = (f32[2048]{0:T(1024)S(1)}, f32[2048]{0:T(1024)}, u32[]{:S(2)}) copy-start(f32[2048]{0:T(1024)} %param.14) | copy-start | bytes 24580
  4.9 4.2 %copy-start.5 = (s32[4,2048]{1,0:T(4,128)S(1)}, s32[4,2048]{1,0:T(4,128)}, u32[]{:S(2)}) copy-start(s32[4,2048]{1,0:T(4,128)} %near_ref.3) | copy-start | bytes 98308
  4.9 4.2 %copy-start.7 = (f32[80,80]{1,0:T(8,128)S(1)}, f32[80,80]{1,0:T(8,128)}, u32[]{:S(2)}) copy-start(f32[80,80]{1,0:T(8,128)} %constant.11.clone.derive_ref) | copy-start | bytes 76804
  5.3 7.9 %collective-permute-start = (f32[63,8,128]{2,1,0:T(8,128)S(1)}, f32[63,8,128]{2,1,0:T(8,128)S(1)}, u32[]{:S(2)}, u32[]{:S(2)}) collective-permute-start(f32[63,8,128]{2,1,0:T(8,128)S(1)} %get-tuple-element.20), channel_id=1, source_target_pairs={{0,2},{2,0},{4,6},{6,4},{8,10},{10,8},{12,14},{14,12},{16,18},{18,... | collective-permute-start | bytes 774152 | tf_op jit(solution)/shard_map/ppermute | solution.py:476
  6.0 10.4 %collective-permute-start.1 = (f32[63,8,128]{2,1,0:T(8,128)S(1)}, f32[63,8,128]{2,1,0:T(8,128)S(1)}, u32[]{:S(2)}, u32[]{:S(2)}) collective-permute-start(f32[63,8,128]{2,1,0:T(8,128)S(1)} %get-tuple-element.21), channel_id=1, source_target_pairs={{2,4},{4,2},{6,8},{8,6},{10,12},{12,10},{14,16},{16,14},{18,20},{2... | collective-permute-start | bytes 774152 | tf_op jit(solution)/shard_map/ppermute | solution.py:475
  9.0 7.3 %copy-start.8 = (f32[80,16]{1,0:T(8,128)S(1)}, f32[80,16]{1,0:T(8,128)}, u32[]{:S(2)}) copy-start(f32[80,16]{1,0:T(8,128)} %constant.12.clone.prolong_ref) | copy-start | bytes 15364
  13.3 3.1 %copy-start.10 = (f32[16,16]{1,0:T(8,128)S(1)}, f32[16,16]{1,0:T(8,128)}, u32[]{:S(2)}) copy-start(f32[16,16]{1,0:T(8,128)} %constant.13.clone.turn_ref) | copy-start | bytes 3076
  16.4 19.9 %copy-start = (f32[1,40,16]{2,1,0:T(8,128)S(1)}, f32[1,40,16]{2,1,0:T(8,128)}, u32[]{:S(2)}) copy-start(f32[1,40,16]{2,1,0:T(8,128)} %constant.14.clone.lift_ref) | copy-start | bytes 7684
  26.6 9.7 %collective-permute-start.3 = (f32[56,1024]{1,0:T(8,128)S(1)}, f32[56,1024]{1,0:T(8,128)S(1)}, u32[]{:S(2)}, u32[]{:S(2)}) collective-permute-start(f32[56,1024]{1,0:T(8,128)S(1)} %get-tuple-element.34), channel_id=1, source_target_pairs={{0,1},{1,0},{2,3},{3,2},{4,5},{5,4},{6,7},{7,6},{8,9},{9,8},{10,11... | collective-permute-start | bytes 688136 | tf_op jit(solution)/shard_map/ppermute | solution.py:519
  26.9 9.3 %collective-permute-start.2 = (f32[40,1024]{1,0:T(8,128)S(1)}, f32[40,1024]{1,0:T(8,128)S(1)}, u32[]{:S(2)}, u32[]{:S(2)}) collective-permute-start(f32[40,1024]{1,0:T(8,128)S(1)} %get-tuple-element.33), channel_id=1, source_target_pairs={{0,1},{1,0},{2,3},{3,2},{4,5},{5,4},{6,7},{7,6},{8,9},{9,8},{10,11... | collective-permute-start | bytes 491528 | tf_op jit(solution)/shard_map/ppermute | solution.py:497

commit v2 on v1

v2 whole, which is shorter than its diff:
```python
import functools

import jax
import jax.numpy as jnp
import numpy as np
from jax import lax
from jax.experimental import pallas as pl
from jax.experimental.pallas import tpu as pltpu
from jax.sharding import PartitionSpec as P


NI = 16
COMP = 5
NEIGH = 4
SWEEPS_FINE = 2
SWEEPS_COARSE = 3
PLANE = 256
FREQ = 0.15
RELAX = 0.6
KEEP = 1.0 - RELAX

LANES = 128
PB = PLANE // LANES
MODES = 16

FV = SWEEPS_FINE * PB
FS = (SWEEPS_FINE - 1) * PB
MV = (SWEEPS_FINE + SWEEPS_COARSE) * PB
MS = MV - PB


def up8(count):
    return -(-count // 8) * 8


def row_map(own):
    rows = [divmod(r, COMP) for r in range(own)]
    rows += [None] * (up8(own) - own)
    other = NI * COMP - own
    rows += [divmod(own + r, COMP) for r in range(other)]
    rows += [None] * (up8(other) - other)
    return rows


def mode_row(h, c):
    if h:
        return 8 * (h - 1) + 3 + c
    return c if c < 3 else 5 + c


def split_matrix(matrix):
    high = matrix.astype(jnp.bfloat16)
    low = (matrix - high.astype(np.float64)).astype(jnp.bfloat16)
    return np.concatenate([high, low, high], axis=1)


def constants(own, inst_count):
    rows = row_map(own)
    own_pad = up8(own)
    count = len(rows)
    derive = np.zeros((count, count))
    restrict = np.zeros((MODES, count))
    prolong = np.zeros((count, MODES))
    for i, left in enumerate(rows):
        if left is None:
            continue
        n, c = left
        phase = 2.0 * np.pi * n / NI
        shape = (1.0, np.cos(phase), np.sin(phase))
        for h in range(3):
            restrict[mode_row(h, c), i] = shape[h] * (1.0 if h == 0 else 2.0) / NI
            prolong[i, mode_row(h, c)] = shape[h]
        for j, right in enumerate(rows):
            if right is not None and right[1] == c and right[0] != n:
                gap = n - right[0]
                derive[i, j] = 0.5 * (-1.0) ** gap / np.tan(np.pi * gap / NI)
    other = prolong[own_pad:]
    lifts = []
    for k in range(1, inst_count):
        lift = np.zeros((own_pad, MODES))
        lift[:own] = other[(k - 1) * own : k * own]
        lifts.append(lift)
    parts = [derive[:, :own_pad], np.concatenate([derive, restrict]), restrict[:, :own_pad], prolong]
    parts += lifts
    width = -(-3 * count // LANES) * LANES
    blocks, starts, at = [], [], 0
    for part in parts:
        wide = split_matrix(part)
        height = -(-wide.shape[0] // 16) * 16
        blocks.append(np.pad(wide, ((0, height - wide.shape[0]), (0, width - wide.shape[1]))))
        starts.append(at)
        at += height
    return np.concatenate(blocks), starts, count


def split3(values):
    high = values.astype(jnp.bfloat16).astype(jnp.float32)
    return jnp.concatenate([values, values, values - high], axis=0).astype(jnp.bfloat16)


def dot(matrix, values):
    return jnp.dot(matrix, split3(values), preferred_element_type=jnp.float32)


def matrix_of(ref, start, height, depth):
    return ref[start : start + height, 0 : 3 * depth]


def lanes(start, count=1):
    return slice(start * LANES, (start + count) * LANES)


def lane_ds(block):
    return pl.ds(pl.multiple_of(block * LANES, LANES), LANES)


def build_table(idx_ref, wt_ref, at, near, bw, bf):
    target = near + lax.broadcasted_iota(jnp.int32, near.shape, 1)
    slot = lax.broadcasted_iota(jnp.int32, near.shape, 0)
    base = (target >> 7) + jnp.where((slot & 1) == 0, PB, 0)
    idx_ref[at, 0:NEIGH, :] = target & (LANES - 1)
    for j in range(PB + 1):
        wt_ref[at, NEIGH * j : NEIGH * (j + 1), :] = jnp.where(base == j, bw, 0.0)
    wt_ref[at, NEIGH * (PB + 1) : NEIGH * (PB + 1) + 1, :] = bf


def stencil(src_ref, center, idx_ref, wt_ref, at, groups):
    sources = [
        [src_ref[8 * g : 8 * g + 8, lane_ds(center + j - PB)] for j in range(2 * PB + 1)]
        for g in groups
    ]
    sums = [None] * len(groups)
    for k in range(NEIGH):
        index = idx_ref[at, pl.ds(k, 8, stride=0), :]
        for j in range(PB + 1):
            weight = wt_ref[at, pl.ds(NEIGH * j + k, 8, stride=0), :]
            for g in range(len(groups)):
                source = sources[g][j + (PB if k % 2 else 0)]
                term = weight * jnp.take_along_axis(source, index, axis=1)
                sums[g] = term if sums[g] is None else sums[g] + term
    return sums


def chunks(groups, most=5):
    return [groups[i : i + most] for i in range(0, len(groups), most)]


def coefficient(wt_ref, at):
    return wt_ref[at, pl.ds(NEIGH * (PB + 1), 8, stride=0), :]


def blocks_loop(count, body, unroll):
    def step(i, carry):
        body(i)
        return carry

    lax.fori_loop(0, count, step, 0, unroll=min(unroll, count))


def pack_kernel(own_pad, starts, init_hbm, src_hbm, near_hbm, face_hbm, damp_hbm, matrix_hbm,
                a_ref, b_ref, init_ref, scaled_ref, near_ref, coef_ref, mode_ref, matrix_ref,
                src_ref, face_ref, damp_ref, sems):
    cells = init_ref.shape[1]
    nblk = cells // LANES
    half = own_pad // 16 * 8
    copies = [
        pltpu.make_async_copy(face_hbm, face_ref, sems.at[0]),
        pltpu.make_async_copy(damp_hbm, damp_ref, sems.at[1]),
        pltpu.make_async_copy(src_hbm.at[0:half], src_ref.at[0:half], sems.at[2]),
        pltpu.make_async_copy(src_hbm.at[half:own_pad], src_ref.at[half:own_pad], sems.at[3]),
        pltpu.make_async_copy(init_hbm.at[0:half], init_ref.at[0:half], sems.at[4]),
        pltpu.make_async_copy(init_hbm.at[half:own_pad], init_ref.at[half:own_pad], sems.at[5]),
        pltpu.make_async_copy(near_hbm, near_ref, sems.at[6]),
        pltpu.make_async_copy(matrix_hbm, matrix_ref, sems.at[7]),
    ]
    for copy in copies:
        copy.start()
    copies[0].wait()
    copies[1].wait()
    face = face_ref[...]
    inverse = RELAX / (damp_ref[...] + jnp.sum(face, axis=0, keepdims=True))
    coef_ref[0:NEIGH, :] = inverse * face
    coef_ref[NEIGH : NEIGH + 1, :] = FREQ * inverse
    copies[2].wait()
    copies[3].wait()
    groups = own_pad // 8
    for g in range(groups):
        scaled_ref[8 * g : 8 * g + 8, :] = src_ref[8 * g : 8 * g + 8, :] * inverse
    for copy in copies[4:]:
        copy.wait()
    restrict = matrix_of(matrix_ref, starts[2], MODES, own_pad)
    for d in range(0, nblk, 2):
        mode_ref[:, lanes(d, 2)] = dot(restrict, scaled_ref[:, lanes(d, 2)])
    low_modes = [
        dot(restrict, init_ref[:, lanes(d, 2)]) for d in range(FV, nblk - FV, 2)
    ]
    near = near_ref[...].astype(jnp.float32)

    def low_mode(block):
        chunk = low_modes[(block - FV) // 2]
        return chunk[:, lanes((block - FV) % 2)]

    def pack(out, high):
        t = 0
        first = nblk - FV if high else 0
        for g in range(groups):
            for d in range(FV):
                out[t] = init_ref[8 * g : 8 * g + 8, lanes(first + d)]
                t += 1
        first = nblk - FS if high else 0
        for g in range(groups):
            for d in range(FS):
                out[t] = scaled_ref[8 * g : 8 * g + 8, lanes(first + d)]
                t += 1
        first = nblk - MV if high else FV
        for g in range(MODES // 8):
            for d in range(MV - FV):
                out[t] = low_mode(first + d)[8 * g : 8 * g + 8]
                t += 1
        first = nblk - MS if high else FS
        for g in range(MODES // 8):
            for d in range(MS - FS):
                out[t] = mode_ref[8 * g : 8 * g + 8, lanes(first + d)]
                t += 1
        first = nblk - MS if high else 0
        for d in range(MS):
            out[t, 0:NEIGH, :] = coef_ref[0:NEIGH, lanes(first + d)]
            out[t, NEIGH : 2 * NEIGH, :] = near[:, lanes(first + d)]
            t += 1
        for d in range(MS):
            out[t, d : d + 1, :] = coef_ref[NEIGH : NEIGH + 1, lanes(first + d)]

    odd = lax.axis_index("cell") & 1

    @pl.when(odd == 0)
    def _():
        pack(a_ref, True)
        pack(b_ref, False)

    @pl.when(odd == 1)
    def _():
        pack(a_ref, False)
        pack(b_ref, True)


def halo_tiles(own_pad):
    groups = own_pad // 8
    return groups * (FV + FS) + (MODES // 8) * (MV - FV + MS - FS) + MS + 1


def inner_kernel(own_pad, rows, starts, init_ref, scaled_ref, near_ref, coef_ref, matrix_ref,
                 own_ref, cross_ref, v1_ref, m1_ref, m2_ref, idx_ref, wt_ref,
                 first, deriv):
    cells = init_ref.shape[1]
    nblk = cells // LANES
    own_groups = list(range(own_pad // 8))
    all_groups = list(range(rows // 8))
    for b in range(nblk):
        build_table(idx_ref, wt_ref, b, near_ref[:, lanes(b)],
                    coef_ref[0:NEIGH, lanes(b)], coef_ref[NEIGH : NEIGH + 1, lanes(b)])
    width1 = nblk - 2 * PB
    derive = matrix_of(matrix_ref, starts[0], rows, own_pad)
    for d in range(0, width1, 2):
        deriv[:, lanes(d, 2)] = dot(derive, init_ref[:, lanes(PB + d, 2)])

    def sweep1(i):
        b = i + PB
        bf = coefficient(wt_ref, b)
        sums = stencil(init_ref, b, idx_ref, wt_ref, b, own_groups)
        for g in all_groups:
            part = slice(8 * g, 8 * g + 8)
            value = -bf * deriv[part, lane_ds(i)]
            if g in own_groups:
                value = value + (KEEP * init_ref[part, lane_ds(b)] + scaled_ref[part, lane_ds(b)] + sums[g])
            first[part, lane_ds(i)] = value

    blocks_loop(width1, sweep1, 2)
    width2 = nblk - 4 * PB
    both = matrix_of(matrix_ref, starts[1], rows + MODES, rows)
    for d in range(0, width1, 2):
        mixed = dot(both, first[:, lanes(d, 2)])
        deriv[:, lanes(d, 2)] = mixed[0:rows]
        m1_ref[:, lanes(d, 2)] = mixed[rows:]

    def sweep2(i):
        b = i + 2 * PB
        bf = coefficient(wt_ref, b)
        for groups in chunks(all_groups):
            sums = stencil(first, i + PB, idx_ref, wt_ref, b, groups)
            for g, total in zip(groups, sums):
                part = slice(8 * g, 8 * g + 8)
                value = KEEP * first[part, lane_ds(i + PB)] - bf * deriv[part, lane_ds(i + PB)] + total
                if g in own_groups:
                    own_ref[part, lane_ds(i)] = value + scaled_ref[part, lane_ds(b)]
                else:
                    cross_ref[8 * g - own_pad : 8 * g + 8 - own_pad, lane_ds(i)] = value

    blocks_loop(width2, sweep2, 2)
    v1_ref[:, lanes(0, 2 * PB)] = first[:, lanes(0, 2 * PB)]
    v1_ref[:, lanes(2 * PB, 2 * PB)] = first[:, lanes(width1 - 2 * PB, 2 * PB)]
    restrict = matrix_of(matrix_ref, starts[1] + rows, MODES, rows)
    for d in range(0, width2, 2):
        values = jnp.concatenate([own_ref[:, lanes(d, 2)], cross_ref[:, lanes(d, 2)]], axis=0)
        m2_ref[:, lanes(d, 2)] = dot(restrict, values)


def outer_kernel(own_pad, rows, starts, a_ref, b_ref, init_ref, scaled_ref, smode_ref, own_ref,
                 v1_ref, m1i_ref, m2i_ref, idx_in, wt_in, matrix_ref,
                 edge_ref, mid_ref, send_ref,
                 v0e, se, v1e, v2e, deriv, m0x, sx, m1x, m2x, rx, c1x, c2x, idx, wt):
    cells = init_ref.shape[1]
    nblk = cells // LANES
    own_groups = list(range(own_pad // 8))
    all_groups = list(range(rows // 8))
    idx[MS : MS + nblk] = idx_in[...]
    wt[MS : MS + nblk] = wt_in[...]
    v0e[:, lanes(FV, 2 * PB)] = init_ref[:, lanes(0, 2 * PB)]
    v0e[:, lanes(FV + 2 * PB, 2 * PB)] = init_ref[:, lanes(nblk - 2 * PB, 2 * PB)]
    se[:, lanes(FS, 2 * PB)] = scaled_ref[:, lanes(0, 2 * PB)]
    se[:, lanes(FS + 2 * PB, 2 * PB)] = scaled_ref[:, lanes(nblk - 2 * PB, 2 * PB)]
    sx[:, lanes(MS, nblk)] = smode_ref[...]
    v1e[:, lanes(2 * PB, 2 * PB)] = v1_ref[:, lanes(0, 2 * PB)]
    v1e[:, lanes(4 * PB, 2 * PB)] = v1_ref[:, lanes(2 * PB, 2 * PB)]
    m1x[:, lanes(MS + PB, nblk - 2 * PB)] = m1i_ref[...]
    far2 = MS - PB
    m2x[:, lanes(far2 + 2 * PB, nblk - 4 * PB)] = m2i_ref[...]

    def unpack(tiles, right):
        t = 0
        at = FV + 4 * PB if right else 0
        for g in own_groups:
            for d in range(FV):
                v0e[8 * g : 8 * g + 8, lanes(at + d)] = tiles[t]
                t += 1
        at = FS + 4 * PB if right else 0
        for g in own_groups:
            for d in range(FS):
                se[8 * g : 8 * g + 8, lanes(at + d)] = tiles[t]
                t += 1
        at = MV + FV if right else 0
        for g in range(MODES // 8):
            for d in range(MV - FV):
                m0x[8 * g : 8 * g + 8, lanes(at + d)] = tiles[t]
                t += 1
        at = MS + nblk + FS if right else 0
        for g in range(MODES // 8):
            for d in range(MS - FS):
                sx[8 * g : 8 * g + 8, lanes(at + d)] = tiles[t]
                t += 1
        at = MS + nblk if right else 0
        for d in range(MS):
            near = tiles[t + d, NEIGH : 2 * NEIGH, :].astype(jnp.int32)
            build_table(idx, wt, at + d, near, tiles[t + d, 0:NEIGH, :],
                        tiles[t + MS, d : d + 1, :])

    odd = lax.axis_index("cell") & 1

    @pl.when(odd == 0)
    def _():
        unpack(a_ref, True)
        unpack(b_ref, False)

    @pl.when(odd == 1)
    def _():
        unpack(a_ref, False)
        unpack(b_ref, True)

    restrict = matrix_of(matrix_ref, starts[2], MODES, own_pad)
    for d in range(0, FV, 2):
        m0x[:, lanes(MV - FV + d, 2)] = dot(restrict, v0e[:, lanes(d, 2)])
        m0x[:, lanes(MV + d, 2)] = dot(restrict, v0e[:, lanes(FV + 4 * PB + d, 2)])
    for d in range(0, FS, 2):
        sx[:, lanes(MS - FS + d, 2)] = dot(restrict, se[:, lanes(d, 2)])
        sx[:, lanes(MS + nblk + d, 2)] = dot(restrict, se[:, lanes(FS + 4 * PB + d, 2)])

    span = 2 * PB
    derive = matrix_of(matrix_ref, starts[0], rows, own_pad)
    for side in range(2):
        for d in range(0, span, 2):
            deriv[:, lanes(side * span + d, 2)] = dot(
                derive, v0e[:, lanes(side * (FV + 2 * PB) + PB + d, 2)]
            )
    for side in range(2):
        from0 = side * (FV + 2 * PB) + PB
        from_s = side * (FS + 3 * PB)
        table = MS - PB + side * nblk
        to = side * 6 * PB

        def sweep1(i, from0=from0, from_s=from_s, table=table, to=to, side=side):
            bf = coefficient(wt, i + table)
            sums = stencil(v0e, i + from0, idx, wt, i + table, own_groups)
            for g in all_groups:
                part = slice(8 * g, 8 * g + 8)
                value = -bf * deriv[part, lane_ds(i + side * span)]
                if g in own_groups:
                    value = value + (
                        KEEP * v0e[part, lane_ds(i + from0)] + se[part, lane_ds(i + from_s)] + sums[g]
                    )
                v1e[part, lane_ds(i + to)] = value

        blocks_loop(span, sweep1, 2)
    both = matrix_of(matrix_ref, starts[1], rows + MODES, rows)
    for side in range(2):
        for d in range(0, 3 * PB, 2):
            mixed = dot(both, v1e[:, lanes(side * 5 * PB + d, 2)])
            deriv[:, lanes(side * 3 * PB + d, 2)] = mixed[0:rows]
            m1x[:, lanes(MS - PB + side * (nblk - PB) + d, 2)] = mixed[rows:]

    top = lax.broadcasted_iota(jnp.int32, (8, LANES), 0) >= 3

    def relax(src, from_, out, to, table, count, source):
        rhs_ref, rhs_at, keep = source
        low, high = slice(0, 8), slice(8, 16)

        def body(i):
            bf = jnp.where(top, coefficient(wt, i + table), 0.0)
            sums = stencil(src, i + from_, idx, wt, i + table, range(MODES // 8))
            here = lane_ds(i + from_)
            src0, src1 = src[low, here], src[high, here]
            rhs, at = lane_ds(i + rhs_at), lane_ds(i + to)
            out[low, at] = keep * src0 + rhs_ref[low, rhs] - bf * src1 + sums[0]
            out[high, at] = keep * src1 + rhs_ref[high, rhs] + bf * src0 + sums[1]

        blocks_loop(count, body, 4)

    far = MS - PB
    relax(m0x, PB, m1x, 0, 0, far, (sx, 0, KEEP))
    right = MS + nblk + PB
    relax(m0x, MV + PB, m1x, right, right, far, (sx, right, KEEP))

    for side in range(2):
        from1 = PB + side * 4 * PB
        from_d = PB + side * 2 * PB
        from_s = FS + side * 2 * PB
        table = MS + side * (nblk - 2 * PB)

        def sweep2(i, from1=from1, from_d=from_d, from_s=from_s, table=table, side=side):
            bf = coefficient(wt, i + table)
            for groups in chunks(all_groups):
                sums = stencil(v1e, i + from1, idx, wt, i + table, groups)
                for g, total in zip(groups, sums):
                    part = slice(8 * g, 8 * g + 8)
                    value = (
                        KEEP * v1e[part, lane_ds(i + from1)] - bf * deriv[part, lane_ds(i + from_d)] + total
                    )
                    if g in own_groups:
                        value = value + se[part, lane_ds(i + from_s)]
                    v2e[part, lane_ds(i + side * span)] = value

        blocks_loop(span, sweep2, 2)
    restrict_all = matrix_of(matrix_ref, starts[1] + rows, MODES, rows)
    for side in range(2):
        for d in range(0, span, 2):
            m2x[:, lanes(far2 + side * (nblk - 2 * PB) + d, 2)] = dot(
                restrict_all, v2e[:, lanes(side * span + d, 2)]
            )

    relax(m1x, PB, m2x, 0, PB, far2, (sx, PB, KEEP))
    relax(m1x, MS + nblk, m2x, far2 + nblk, MS + nblk, far2, (sx, MS + nblk, KEEP))

    deep = MS - 2 * PB
    relax(m2x, PB, rx, 0, 2 * PB, nblk + 2 * deep, (sx, 2 * PB, -RELAX))
    relax(rx, PB, c1x, 0, 3 * PB, nblk + 2 * PB, (rx, PB, KEEP))
    relax(c1x, PB, c2x, 0, 4 * PB, nblk, (rx, 2 * PB, KEEP))

    prolong = matrix_of(matrix_ref, starts[3], rows, MODES)
    lead = rows - own_pad
    for side in range(2):
        for d in range(0, span, 2):
            part = lanes(side * span + d, 2)
            lifted = v2e[:, part] + dot(prolong, c2x[:, lanes(side * (nblk - 2 * PB) + d, 2)])
            edge_ref[:, part] = lifted[0:own_pad, :]
            send_ref[0:lead, part] = lifted[own_pad:, :]
    prolong_own = matrix_of(matrix_ref, starts[3], own_pad, MODES)
    for d in range(0, nblk - 4 * PB, 2):
        modes = c2x[:, lanes(2 * PB + d, 2)]
        send_ref[lead:, lanes(d, 2)] = modes
        mid_ref[:, lanes(d, 2)] = own_ref[:, lanes(d, 2)] + dot(prolong_own, modes)


def final_kernel(count, starts, edge_ref, mid_ref, matrix_ref, *refs):
    out_ref = refs[-1]
    own_pad = edge_ref.shape[0]
    nblk = out_ref.shape[1] // LANES
    span = 2 * PB
    early, late = refs[0 : 2 * count : 2], refs[1 : 2 * count : 2]
    for d in range(0, 2 * span, 2):
        edge = edge_ref[:, lanes(d, 2)]
        for k in range(count):
            edge = edge + late[k][0:own_pad, lanes(d, 2)]
        out_ref[:, lanes(d if d < span else nblk - 2 * span + d, 2)] = edge
    for d in range(0, nblk - 2 * span, 2):
        mid = mid_ref[:, lanes(d, 2)]
        for k in range(count):
            lift = matrix_of(matrix_ref, starts[4 + k], own_pad, MODES)
            mid = mid + early[k][:, lanes(d, 2)] + dot(lift, late[k][own_pad:, lanes(d, 2)])
        out_ref[:, lanes(span + d, 2)] = mid


def vm(*shape):
    return pltpu.VMEM(shape, jnp.float32)


def f32(*shape):
    return jax.ShapeDtypeStruct(shape, jnp.float32)


def call(kernel, out_shape, scratch, cost_us, *args, fetch=False):
    whole = pl.BlockSpec(memory_space=pltpu.VMEM)
    single = not isinstance(out_shape, (tuple, list))
    return pl.pallas_call(
        kernel,
        out_shape=out_shape,
        in_specs=[pl.BlockSpec(memory_space=pltpu.HBM) if fetch else whole] * len(args),
        out_specs=whole if single else [whole] * len(out_shape),
        scratch_shapes=scratch,
        compiler_params=pltpu.CompilerParams(vmem_limit_bytes=16 * 1024 * 1024),
        cost_estimate=pl.CostEstimate(
            flops=int(cost_us * 1e8), bytes_accessed=int(cost_us * 3e6), transcendentals=0
        ),
    )(*args)


def per_device(initial, source, neighbors, face_weights, damping):
    own, cells = initial.shape
    nblk = cells // LANES
    inst_count = lax.axis_size("inst")
    cell_count = lax.axis_size("cell")
    own_pad = up8(own)
    matrices, starts, rows = constants(own, inst_count)
    matrices = jnp.asarray(matrices)
    cross = rows - own_pad
    if own_pad != own:
        initial = jnp.pad(initial, ((0, own_pad - own), (0, 0)))
        source = jnp.pad(source, ((0, own_pad - own), (0, 0)))
    tiles = halo_tiles(own_pad)
    span = 2 * PB
    mid_blocks = nblk - 2 * span
    slots = NEIGH * (PB + 1) + 4

    def int32(*shape):
        return jax.ShapeDtypeStruct(shape, jnp.int32)

    pack_a, pack_b, initial, scaled, neighbors, coef, smode, matrices = call(
        functools.partial(pack_kernel, own_pad, starts),
        [f32(tiles, 8, LANES), f32(tiles, 8, LANES), f32(own_pad, cells), f32(own_pad, cells),
         int32(NEIGH, cells), f32(8, cells), f32(MODES, cells),
         jax.ShapeDtypeStruct(matrices.shape, matrices.dtype)],
        [vm(own_pad, cells), vm(NEIGH, cells), vm(1, cells), pltpu.SemaphoreType.DMA((8,))], 2,
        *[
            pltpu.with_memory_space_constraint(x, pltpu.HBM)
            for x in (initial, source, neighbors, face_weights, damping.reshape(1, cells), matrices)
        ],
        fetch=True,
    )
    near_pairs = [(i, i ^ 1) for i in range(cell_count) if i ^ 1 < cell_count]
    far_pairs = []
    for i in range(1, cell_count - 1, 2):
        far_pairs += [(i, i + 1), (i + 1, i)]
    halo_b = lax.ppermute(pack_b, "cell", far_pairs)
    halo_a = lax.ppermute(pack_a, "cell", near_pairs)

    own_mid, cross_mid, v1, m1, m2, idx, wt = call(
        functools.partial(inner_kernel, own_pad, rows, starts),
        [f32(own_pad, mid_blocks * LANES), f32(cross, mid_blocks * LANES),
         f32(rows, 4 * PB * LANES), f32(MODES, (nblk - 2 * PB) * LANES),
         f32(MODES, mid_blocks * LANES), int32(nblk, 8, LANES), f32(nblk, slots, LANES)],
        [vm(rows, (nblk - 2 * PB) * LANES), vm(rows, (nblk - 2 * PB) * LANES)], 5,
        initial, scaled, neighbors, coef, matrices,
    )

    def share(array, k):
        if cross == own_pad:
            return array
        part = lax.slice_in_dim(array, (k - 1) * own, k * own, axis=0)
        return jnp.pad(part, ((0, own_pad - own), (0, 0)))

    def shift(k):
        return [(i, (i + k) % inst_count) for i in range(inst_count)]

    early = [lax.ppermute(share(cross_mid, k), "inst", shift(k)) for k in range(1, inst_count)]

    ext = nblk + 2 * MS
    edge, mid, send = call(
        functools.partial(outer_kernel, own_pad, rows, starts),
        [f32(own_pad, 2 * span * LANES), f32(own_pad, mid_blocks * LANES),
         f32(cross + MODES, 2 * span * LANES)],
        [vm(own_pad, 2 * (FV + 2 * PB) * LANES), vm(own_pad, 2 * (FS + 2 * PB) * LANES),
         vm(rows, 8 * PB * LANES), vm(rows, 2 * span * LANES), vm(rows, 6 * PB * LANES),
         vm(MODES, 2 * MV * LANES), vm(MODES, ext * LANES), vm(MODES, ext * LANES),
         vm(MODES, (ext - 2 * PB) * LANES), vm(MODES, (ext - 4 * PB) * LANES),
         vm(MODES, (nblk + 2 * PB) * LANES), vm(MODES, cells),
         pltpu.VMEM((ext, 8, LANES), jnp.int32), vm(ext, slots, LANES)],
        8, halo_a, halo_b, initial, scaled, smode, own_mid, v1, m1, m2, idx, wt, matrices,
    )

    def share_late(k):
        if cross == own_pad:
            return send
        return jnp.concatenate([share(send[:cross], k), send[cross:]], axis=0)

    late = [lax.ppermute(share_late(k), "inst", shift(k)) for k in range(1, inst_count)]
    received = [r for pair in zip(early, late) for r in pair]
    out = call(
        functools.partial(final_kernel, inst_count - 1, starts), f32(own_pad, cells), [], 1,
        edge, mid, matrices, *received,
    )
    return out[:own] if own_pad != own else out


def solution(mesh):
    return jax.shard_map(
        per_device,
        mesh=mesh,
        in_specs=(
            P("inst", "cell"),
            P("inst", "cell"),
            P(None, "cell"),
            P(None, "cell"),
            P("cell"),
        ),
        out_specs=P("inst", "cell"),
        check_vma=False,
    )
```

time: 37.7 us -> 31.5 us (0.84)
  local copies, waits for them, and re-layouts: 4.87 us -> 0 us
  Pallas kernels: 15.9 us -> 14.1 us
  waiting for transfers between devices: 11.2 us -> 11.9 us
    unnamed x22 -> x0, local copies, waits for them, and re-layouts: 4.87 us -> none
    pallas_call x4, Pallas kernels: 15.9 us -> 14.1 us  [call(): pl.pallas_call(kernel, out_shape=out_shape, in_specs=[pl.BlockSpec(memory...]
    ppermute x1, waiting for transfers between devices: 3.11 us -> 3.83 us  [per_device(): halo_b = lax.ppermute(pack_b, 'cell', far_pairs)]
where the time goes in v2:
time: 31.5 us; the launch traced here: 31.3 us
  Pallas kernels  14.1 us (45%)
  waiting for transfers between devices  11.9 us (38%)
  starting transfers between devices  5.28 us (17%)
    pallas_call x4, Pallas kernels, call(): pl.pallas_call(kernel, out_shape=out_shape, in_specs=[pl.BlockSpec(memory...  14.1 us
    ppermute x1, waiting for transfers between devices, per_device(): lax.ppermute(share(cross_mid, k), 'inst', shift(k))  8.09 us
    ppermute x1, waiting for transfers between devices, per_device(): halo_b = lax.ppermute(pack_b, 'cell', far_pairs)  3.83 us
    ppermute x1, starting transfers between devices, per_device(): halo_b = lax.ppermute(pack_b, 'cell', far_pairs)  3.05 us
    ppermute x1, starting transfers between devices, per_device(): lax.ppermute(share(cross_mid, k), 'inst', shift(k))  1.21 us
    ppermute x1, starting transfers between devices, per_device(): halo_a = lax.ppermute(pack_a, 'cell', near_pairs)  0.7 us
  transfers between devices with their start and end apart: 4, of which 2 were waited for; matrix products, arithmetic and copies ran while one was open for 0% of the time, Pallas kernels for 11%

profile of v2, /device:TPU:19, one launch (start us, length us, event | category | flops | bytes accessed | tf_op | source)
XLA Modules:
  0.0 31.3 jit_solution(1790676181282453612)
XLA Ops:
  0.0 1.6 %shard_map.64 = (f32[63,8,128]{2,1,0:T(8,128)S(1)}, f32[63,8,128]{2,1,0:T(8,128)S(1)}, f32[40,2048]{1,0:T(8,128)S(1)}, f32[40,2048]{1,0:T(8,128)S(1)}, s32[4,204...) custom-call(f32[40,2048]{1,0:T(8,128)} %init_hbm.1, ...), custom_call_target="tpu_custom_call" | custom-call | flops 200000000 | bytes 6000000 | tf_op jit(solution)/shard_map/pallas_call | solution.py:511
  1.6 0.7 %collective-permute-start = (f32[63,8,128]{2,1,0:T(8,128)S(1)}, f32[63,8,128]{2,1,0:T(8,128)S(1)}, u32[]{:S(2)}, u32[]{:S(2)}) collective-permute-start(f32[63,8,128]{2,1,0:T(8,128)S(1)} %get-tuple-element.23), channel_id=1, source_target_pairs={{0,2},{2,0},{4,6},{6,4},{8,10},{10,8},{12,14},{14,12},{16,18},{18,... | collective-permute-start | bytes 774152 | tf_op jit(solution)/shard_map/ppermute | solution.py:561
  2.3 3.0 %collective-permute-start.1 = (f32[63,8,128]{2,1,0:T(8,128)S(1)}, f32[63,8,128]{2,1,0:T(8,128)S(1)}, u32[]{:S(2)}, u32[]{:S(2)}) collective-permute-start(f32[63,8,128]{2,1,0:T(8,128)S(1)} %get-tuple-element.24), channel_id=1, source_target_pairs={{2,4},{4,2},{6,8},{8,6},{10,12},{12,10},{14,16},{16,14},{18,20},{2... | collective-permute-start | bytes 774152 | tf_op jit(solution)/shard_map/ppermute | solution.py:560
  5.4 3.5 %shard_map.65 = (f32[40,1024]{1,0:T(8,128)S(1)}, f32[40,1024]{1,0:T(8,128)S(1)}, f32[80,1024]{1,0:T(8,128)S(1)}, f32[16,1536]{1,0:T(8,128)S(1)}, f32[16,1024]{1,...) custom-call(f32[40,2048]{1,0:T(8,128)S(1)} %get-tuple-element.25.init_ref, ...), custom_call_target="tpu_custom_call" | custom-call | flops 500000000 | bytes 15000000 | tf_op jit(solution)/shard_map/pallas_call | solution.py:511
  8.9 0.0 collective-permute-done.a_ref
  8.9 3.8 %collective-permute-done.1.b_ref = f32[63,8,128]{2,1,0:T(8,128)S(1)} collective-permute-done((f32[63,8,128]{2,1,0:T(8,128)S(1)}, f32[63,8,128]{2,1,0:T(8,128)S(1)}, u32[]{:S(2)}, u32[]{:S(2)}) %collective-permute-start.1) | collective-permute-done | bytes 258080 | tf_op jit(solution)/shard_map/ppermute | solution.py:560
  12.7 8.1 %shard_map.66 = (f32[40,1024]{1,0:T(8,128)S(1)}, f32[40,1024]{1,0:T(8,128)S(1)}, f32[56,1024]{1,0:T(8,128)S(1)}) custom-call(f32[63,8,128]{2,1,0:T(8,128)S(1)} %collective-permute-done.a_ref, f32[63,8,128]{2,1,0:T(8,128)S(1)} %collective-permute-done.1.b_ref, f32[40,2048]{1,0:T(8,128)S(1)} %get-tuple-element.25.init_ref, ...), custom_call_target="tpu_custom_call" | custom-call | flops 800000000 | bytes 24000000 | tf_op jit(solution)/shard_map/pallas_call | solution.py:511
  20.8 0.3 %collective-permute-start.3 = (f32[56,1024]{1,0:T(8,128)S(1)}, f32[56,1024]{1,0:T(8,128)S(1)}, u32[]{:S(2)}, u32[]{:S(2)}) collective-permute-start(f32[56,1024]{1,0:T(8,128)S(1)} %get-tuple-element.40), channel_id=1, source_target_pairs={{0,1},{1,0},{2,3},{3,2},{4,5},{5,4},{6,7},{7,6},{8,9},{9,8},{10,11... | collective-permute-start | bytes 688136 | tf_op jit(solution)/shard_map/ppermute | solution.py:602
  21.1 1.2 %collective-permute-start.2 = (f32[40,1024]{1,0:T(8,128)S(1)}, f32[40,1024]{1,0:T(8,128)S(1)}, u32[]{:S(2)}, u32[]{:S(2)}) collective-permute-start(f32[40,1024]{1,0:T(8,128)S(1)} %get-tuple-element.39), channel_id=1, source_target_pairs={{0,1},{1,0},{2,3},{3,2},{4,5},{5,4},{6,7},{7,6},{8,9},{9,8},{10,11... | collective-permute-start | bytes 491528 | tf_op jit(solution)/shard_map/ppermute | solution.py:581
  22.3 8.1 %collective-permute-done.2.refs_0_ = f32[40,1024]{1,0:T(8,128)S(1)} collective-permute-done((f32[40,1024]{1,0:T(8,128)S(1)}, f32[40,1024]{1,0:T(8,128)S(1)}, u32[]{:S(2)}, u32[]{:S(2)}) %collective-permute-start.2) | collective-permute-done | bytes 163872 | tf_op jit(solution)/shard_map/ppermute | solution.py:581
  30.4 0.0 collective-permute-done.3.refs_1_
  30.4 0.9 %shard_map.67 = f32[40,2048]{1,0:T(8,128)} custom-call(f32[40,1024]{1,0:T(8,128)S(1)} %get-tuple-element.37.edge_ref, f32[40,1024]{1,0:T(8,128)S(1)} %get-tuple-element.38.mid_ref, bf16[320,256]{1,0:T(8,128)(2,1)S(1)} %get-tuple-element.30.matrix_ref, f32[40,1024]{1,0:T(8,128)S(1)} %collective-permute-done.2.refs_0_, ...), custom_call_target="tpu_custom_call" | custom-call | flops 100000000 | bytes 3000000 | tf_op jit(solution)/shard_map/pallas_call | solution.py:511
Async XLA Ops:
  1.6 7.3 %collective-permute-start = (f32[63,8,128]{2,1,0:T(8,128)S(1)}, f32[63,8,128]{2,1,0:T(8,128)S(1)}, u32[]{:S(2)}, u32[]{:S(2)}) collective-permute-start(f32[63,8,128]{2,1,0:T(8,128)S(1)} %get-tuple-element.23), channel_id=1, source_target_pairs={{0,2},{2,0},{4,6},{6,4},{8,10},{10,8},{12,14},{14,12},{16,18},{18,... | collective-permute-start | bytes 774152 | tf_op jit(solution)/shard_map/ppermute | solution.py:561
  2.3 10.4 %collective-permute-start.1 = (f32[63,8,128]{2,1,0:T(8,128)S(1)}, f32[63,8,128]{2,1,0:T(8,128)S(1)}, u32[]{:S(2)}, u32[]{:S(2)}) collective-permute-start(f32[63,8,128]{2,1,0:T(8,128)S(1)} %get-tuple-element.24), channel_id=1, source_target_pairs={{2,4},{4,2},{6,8},{8,6},{10,12},{12,10},{14,16},{16,14},{18,20},{2... | collective-permute-start | bytes 774152 | tf_op jit(solution)/shard_map/ppermute | solution.py:560
  20.8 9.6 %collective-permute-start.3 = (f32[56,1024]{1,0:T(8,128)S(1)}, f32[56,1024]{1,0:T(8,128)S(1)}, u32[]{:S(2)}, u32[]{:S(2)}) collective-permute-start(f32[56,1024]{1,0:T(8,128)S(1)} %get-tuple-element.40), channel_id=1, source_target_pairs={{0,1},{1,0},{2,3},{3,2},{4,5},{5,4},{6,7},{7,6},{8,9},{9,8},{10,11... | collective-permute-start | bytes 688136 | tf_op jit(solution)/shard_map/ppermute | solution.py:602
  21.1 9.3 %collective-permute-start.2 = (f32[40,1024]{1,0:T(8,128)S(1)}, f32[40,1024]{1,0:T(8,128)S(1)}, u32[]{:S(2)}, u32[]{:S(2)}) collective-permute-start(f32[40,1024]{1,0:T(8,128)S(1)} %get-tuple-element.39), channel_id=1, source_target_pairs={{0,1},{1,0},{2,3},{3,2},{4,5},{5,4},{6,7},{7,6},{8,9},{9,8},{10,11... | collective-permute-start | bytes 491528 | tf_op jit(solution)/shard_map/ppermute | solution.py:581

commit v3 on v0

v3 whole, which is shorter than its diff:
```python
import functools

import jax
import jax.numpy as jnp
import numpy as np
from jax import lax
from jax.experimental import pallas as pl
from jax.experimental.pallas import tpu as pltpu
from jax.sharding import PartitionSpec as P


NI = 16
COMP = 5
NEIGH = 4
PLANE = 256
FREQ = 0.15
RELAX = 0.6
KEEP = 1.0 - RELAX

LANES = 128
PB = PLANE // LANES
MODES = 16


def up8(count):
    return -(-count // 8) * 8


def row_map(own):
    rows = [divmod(r, COMP) for r in range(own)]
    rows += [None] * (up8(own) - own)
    other = NI * COMP - own
    rows += [divmod(own + r, COMP) for r in range(other)]
    rows += [None] * (up8(other) - other)
    return rows


def mode_row(h, c):
    if h:
        return 8 * (h - 1) + 3 + c
    return c if c < 3 else 5 + c


def split_matrix(matrix):
    high = matrix.astype(jnp.bfloat16)
    low = (matrix - high.astype(np.float64)).astype(jnp.bfloat16)
    return np.concatenate([high, low, high], axis=1)


def constants(own, inst_count):
    rows = row_map(own)
    own_pad = up8(own)
    count = len(rows)
    derive = np.zeros((count, count))
    restrict = np.zeros((MODES, count))
    prolong = np.zeros((count, MODES))
    for i, left in enumerate(rows):
        if left is None:
            continue
        n, c = left
        phase = 2.0 * np.pi * n / NI
        shape = (1.0, np.cos(phase), np.sin(phase))
        for h in range(3):
            restrict[mode_row(h, c), i] = shape[h] * (1.0 if h == 0 else 2.0) / NI
            prolong[i, mode_row(h, c)] = shape[h]
        for j, right in enumerate(rows):
            if right is not None and right[1] == c and right[0] != n:
                gap = n - right[0]
                derive[i, j] = 0.5 * (-1.0) ** gap / np.tan(np.pi * gap / NI)
    other = prolong[own_pad:]
    lifts = []
    for k in range(1, inst_count):
        lift = np.zeros((own_pad, MODES))
        lift[:own] = other[(k - 1) * own : k * own]
        lifts.append(lift)
    parts = [derive[:, :own_pad], np.concatenate([derive, restrict]), restrict[:, :own_pad], prolong]
    parts += lifts
    width = -(-3 * count // LANES) * LANES
    blocks, starts, at = [], [], 0
    for part in parts:
        wide = split_matrix(part)
        height = -(-wide.shape[0] // 16) * 16
        blocks.append(np.pad(wide, ((0, height - wide.shape[0]), (0, width - wide.shape[1]))))
        starts.append(at)
        at += height
    return np.concatenate(blocks), starts, count


def split3(values):
    high = values.astype(jnp.bfloat16).astype(jnp.float32)
    return jnp.concatenate([values, values, values - high], axis=0).astype(jnp.bfloat16)


def dot(matrix, values):
    return jnp.dot(matrix, split3(values), preferred_element_type=jnp.float32)


def matrix_of(ref, start, height, depth):
    return ref[start : start + height, 0 : 3 * depth]


def lanes(start, count=1):
    return slice(start * LANES, (start + count) * LANES)


def build_table(idx_ref, wt_ref, at, near, bw, bf):
    target = near + lax.broadcasted_iota(jnp.int32, near.shape, 1)
    slot = lax.broadcasted_iota(jnp.int32, near.shape, 0)
    base = (target >> 7) + jnp.where((slot & 1) == 0, PB, 0)
    idx_ref[at, 0:NEIGH, :] = target & (LANES - 1)
    for j in range(PB + 1):
        wt_ref[at, NEIGH * j : NEIGH * (j + 1), :] = jnp.where(base == j, bw, 0.0)
    wt_ref[at, NEIGH * (PB + 1) : NEIGH * (PB + 1) + 1, :] = bf


def coefficient(table):
    _, wt_ref, at = table
    return wt_ref[at, pl.ds(NEIGH * (PB + 1), 8, stride=0), :]


def stencil(read, block, table, groups, known=None):
    idx_ref, wt_ref, at = table
    sums, cache = [None] * len(groups), {}

    def source(g, b):
        if (g, b) not in cache:
            cache[g, b] = read(g, b)
        return cache[g, b]

    for k in range(NEIGH):
        index = None
        for j in range(PB + 1):
            b = block + j - (0 if k % 2 else PB)
            if known is not None and not known(b):
                continue
            if index is None:
                index = idx_ref[at, pl.ds(k, 8, stride=0), :]
            weight = wt_ref[at, pl.ds(NEIGH * j + k, 8, stride=0), :]
            for i, g in enumerate(groups):
                term = weight * jnp.take_along_axis(source(g, b), index, axis=1)
                sums[i] = term if sums[i] is None else sums[i] + term
    return [0.0 if total is None else total for total in sums]


def turned(values, table, keep):
    top = lax.broadcasted_iota(jnp.int32, (8, LANES), 0) >= 3
    bf = jnp.where(top, coefficient(table), 0.0)
    low, high = values
    return keep * low - bf * high, keep * high + bf * low


def rows8(g):
    return slice(8 * g, 8 * g + 8)


MODE_GROUPS = list(range(MODES // 8))
NEAR, FAR, DEEP = range(PB), range(PB, 2 * PB), range(2 * PB, 3 * PB)


def halo_layout(own_pad):
    fine, mode = own_pad // 8 * PB, MODES // 8 * PB
    sizes = [fine, fine, mode, mode, mode, mode, 2 * PB, 1]
    starts = [sum(sizes[:i]) for i in range(len(sizes))]
    return starts, sum(sizes)


def pack_kernel(own_pad, starts, init_hbm, src_hbm, near_hbm, face_hbm, damp_hbm, matrix_hbm,
                a_ref, b_ref, init_ref, scaled_ref, mode_ref, edge_ref, idx_ref, wt_ref, matrix_ref,
                src_ref, near_ref, face_ref, damp_ref, coef_ref, m0, m1, m2, rp, sems):
    cells = init_ref.shape[1]
    nblk = cells // LANES
    half = own_pad // 16 * 8
    copies = [
        pltpu.make_async_copy(face_hbm, face_ref, sems.at[0]),
        pltpu.make_async_copy(damp_hbm, damp_ref, sems.at[1]),
        pltpu.make_async_copy(near_hbm, near_ref, sems.at[2]),
        pltpu.make_async_copy(src_hbm.at[0:half], src_ref.at[0:half], sems.at[3]),
        pltpu.make_async_copy(src_hbm.at[half:own_pad], src_ref.at[half:own_pad], sems.at[4]),
        pltpu.make_async_copy(init_hbm.at[0:half], init_ref.at[0:half], sems.at[5]),
        pltpu.make_async_copy(init_hbm.at[half:own_pad], init_ref.at[half:own_pad], sems.at[6]),
        pltpu.make_async_copy(matrix_hbm, matrix_ref, sems.at[7]),
    ]
    for copy in copies:
        copy.start()
    for copy in copies[0:3]:
        copy.wait()
    face = face_ref[...]
    inverse = RELAX / (damp_ref[...] + jnp.sum(face, axis=0, keepdims=True))
    coef_ref[0:NEIGH, :] = inverse * face
    coef_ref[NEIGH : NEIGH + 1, :] = FREQ * inverse
    for b in range(nblk):
        build_table(idx_ref, wt_ref, b, near_ref[:, lanes(b)],
                    coef_ref[0:NEIGH, lanes(b)], coef_ref[NEIGH : NEIGH + 1, lanes(b)])
    for copy in copies[3:]:
        copy.wait()
    groups = list(range(own_pad // 8))
    for g in groups:
        scaled_ref[rows8(g), :] = src_ref[rows8(g), :] * inverse
    restrict = matrix_of(matrix_ref, starts[2], MODES, own_pad)
    for d in range(0, nblk, 2):
        m0[:, lanes(d, 2)] = dot(restrict, init_ref[:, lanes(d, 2)])
    for d in range(0, nblk, 2):
        mode_ref[:, lanes(d, 2)] = dot(restrict, scaled_ref[:, lanes(d, 2)])

    def table(b):
        return idx_ref, wt_ref, b

    def reader(ref, first=0):
        return lambda g, b: ref[rows8(g), lanes(b - first)]

    derive = matrix_of(matrix_ref, starts[0], own_pad, own_pad)
    for side in range(2):
        at = side * (nblk - PB)
        deriv = dot(derive, init_ref[:, lanes(at, PB)])
        for i in NEAR:
            b = at + i
            sums = stencil(reader(init_ref), b, table(b), groups, lambda s: 0 <= s < nblk)
            bf = coefficient(table(b))
            for g in groups:
                edge_ref[rows8(g), lanes(side * PB + i)] = (
                    KEEP * init_ref[rows8(g), lanes(b)]
                    + scaled_ref[rows8(g), lanes(b)]
                    - bf * deriv[rows8(g), lanes(i)]
                    + sums[g]
                )

    def modes(src, first, out, to, b, known, keep):
        sums = stencil(reader(src, first), b, table(b), MODE_GROUPS, known)
        parts = (0.0, 0.0)
        if keep is not None:
            parts = turned([src[rows8(g), lanes(b - first)] for g in MODE_GROUPS], table(b), keep)
        for g in MODE_GROUPS:
            out[rows8(g), lanes(to)] = parts[g] + sums[g] + mode_ref[rows8(g), lanes(b)]

    for b in range(PB, nblk - PB):
        modes(m0, 0, m1, b - PB, b, None, KEEP)
    for side in range(2):
        for d in list(FAR) + list(DEEP):
            b = nblk - 1 - d if side else d
            modes(m1, PB, m2, b - PB, b, lambda s: PB <= s < nblk - PB, KEEP)
    for side in range(2):
        for d in FAR:
            b = nblk - 1 - d if side else d
            deep = [nblk - 1 - e if side else e for e in DEEP]
            modes(m2, PB, rp, b - PB, b, lambda s, deep=deep: s in deep, None)

    near = near_ref[...].astype(jnp.float32)
    first_tiles, _ = halo_layout(own_pad)

    def pack(out, high):
        near_at = nblk - PB if high else 0
        far_at = nblk - 2 * PB if high else PB
        edge_at = PB if high else 0
        all_at = nblk - 2 * PB if high else 0
        for i in range(PB):
            for g in groups:
                out[first_tiles[0] + g * PB + i] = init_ref[rows8(g), lanes(near_at + i)]
                out[first_tiles[1] + g * PB + i] = edge_ref[rows8(g), lanes(edge_at + i)]
            for g in MODE_GROUPS:
                t = g * PB + i
                out[first_tiles[2] + t] = mode_ref[rows8(g), lanes(near_at + i)]
                out[first_tiles[3] + t] = m1[rows8(g), lanes(far_at + i - PB)]
                out[first_tiles[4] + t] = m2[rows8(g), lanes(far_at + i - PB)]
                out[first_tiles[5] + t] = rp[rows8(g), lanes(far_at + i - PB)]
        for i in range(2 * PB):
            out[first_tiles[6] + i, 0:NEIGH, :] = coef_ref[0:NEIGH, lanes(all_at + i)]
            out[first_tiles[6] + i, NEIGH : 2 * NEIGH, :] = near[:, lanes(all_at + i)]
            out[first_tiles[7], i : i + 1, :] = coef_ref[NEIGH : NEIGH + 1, lanes(all_at + i)]

    odd = lax.axis_index("cell") & 1

    @pl.when(odd == 0)
    def _():
        pack(a_ref, True)
        pack(b_ref, False)

    @pl.when(odd == 1)
    def _():
        pack(a_ref, False)
        pack(b_ref, True)


def inner_kernel(own_pad, rows, starts, init_ref, scaled_ref, smode_ref, idx_ref, wt_ref, matrix_ref,
                 own_ref, cross_ref, part_ref, cpart_ref, cend_ref, m2_ref, rp_ref,
                 first, deriv):
    cells = init_ref.shape[1]
    nblk = cells // LANES
    own_groups = list(range(own_pad // 8))
    cross_groups = list(range(own_pad // 8, rows // 8))

    def table(b):
        return idx_ref, wt_ref, b

    derive = matrix_of(matrix_ref, starts[0], rows, own_pad)
    for d in range(0, nblk, 2):
        deriv[:, lanes(d, 2)] = dot(derive, init_ref[:, lanes(d, 2)])

    def read_init(g, b):
        return init_ref[rows8(g), lanes(b)]

    def read_first(g, b):
        return first[rows8(g), lanes(b)]

    inside = range(PB, nblk - PB)
    for b in range(nblk):
        bf = coefficient(table(b))
        for g in cross_groups:
            first[rows8(g), lanes(b)] = -bf * deriv[rows8(g), lanes(b)]
        if b in inside:
            sums = stencil(read_init, b, table(b), own_groups)
            for g in own_groups:
                first[rows8(g), lanes(b)] = (
                    KEEP * init_ref[rows8(g), lanes(b)]
                    + scaled_ref[rows8(g), lanes(b)]
                    - bf * deriv[rows8(g), lanes(b)]
                    + sums[g]
                )
    derive = matrix_of(matrix_ref, starts[1], rows, rows)
    for d in range(PB, nblk - PB, 2):
        deriv[:, lanes(d, 2)] = dot(derive, first[:, lanes(d, 2)])

    def local(g, b):
        bf = coefficient(table(b))
        return KEEP * first[rows8(g), lanes(b)] - bf * deriv[rows8(g), lanes(b)]

    for b in range(nblk):
        sums = stencil(read_first, b, table(b), cross_groups, lambda s: 0 <= s < nblk)
        for g, total in zip(cross_groups, sums):
            part = rows8(g - len(own_groups))
            if b in inside:
                cross_ref[part, lanes(b - PB)] = local(g, b) + total
            else:
                at = lanes(b if b < PB else b - nblk + 2 * PB)
                cpart_ref[part, at] = total
                cend_ref[part, at] = first[rows8(g), lanes(b)]
    middle = range(2 * PB, nblk - 2 * PB)
    for b in range(nblk):
        sums = stencil(read_first, b, table(b), own_groups, lambda s: s in inside)
        for g, total in zip(own_groups, sums):
            if b in inside:
                total = total + local(g, b) + scaled_ref[rows8(g), lanes(b)]
            if b in middle:
                own_ref[rows8(g), lanes(b - 2 * PB)] = total
            else:
                part_ref[rows8(g), lanes(b if b < 2 * PB else b - nblk + 4 * PB)] = total
    restrict = matrix_of(matrix_ref, starts[1] + rows, MODES, rows)
    for d in range(0, nblk - 4 * PB, 2):
        values = jnp.concatenate([own_ref[:, lanes(d, 2)], cross_ref[:, lanes(PB + d, 2)]], axis=0)
        m2_ref[:, lanes(d, 2)] = dot(restrict, values)

    def read_m2(g, b):
        return m2_ref[rows8(g), lanes(b - 2 * PB)]

    for b in range(nblk):
        sums = stencil(read_m2, b, table(b), MODE_GROUPS, lambda s: s in middle)
        if b in middle:
            parts = turned([read_m2(g, b) for g in MODE_GROUPS], table(b), -RELAX)
            sums = [total + part for total, part in zip(sums, parts)]
        for g in MODE_GROUPS:
            rp_ref[rows8(g), lanes(b)] = sums[g] + smode_ref[rows8(g), lanes(b)]


def outer_kernel(own_pad, rows, starts, a_ref, b_ref, init_ref, scaled_ref, smode_ref, edge_ref,
                 own_ref, cross_ref, part_ref, cpart_ref, cend_ref, m2i_ref, rp_ref, idx_in, wt_in,
                 matrix_ref, base_ref, send_ref,
                 halo, v1, v2, deriv, m1x, m2x, rx, c1x, c2x, idx, wt):
    cells = init_ref.shape[1]
    nblk = cells // LANES
    lead = own_pad // 8
    own_groups = list(range(lead))
    cross_groups = list(range(lead, rows // 8))
    tiles, _ = halo_layout(own_pad)
    odd = lax.axis_index("cell") & 1

    @pl.when(odd == 0)
    def _():
        halo[1] = a_ref[...]
        halo[0] = b_ref[...]

    @pl.when(odd == 1)
    def _():
        halo[0] = a_ref[...]
        halo[1] = b_ref[...]

    def side_of(b):
        return (0, b + 2 * PB) if b < 0 else (1, b - nblk)

    for side in range(2):
        for i in range(2 * PB):
            tile = tiles[6] + i
            build_table(idx, wt, side * 2 * PB + i, halo[side, tile, NEIGH : 2 * NEIGH, :].astype(jnp.int32),
                        halo[side, tile, 0:NEIGH, :], halo[side, tiles[7], i : i + 1, :])

    def table(b):
        if 0 <= b < nblk:
            return idx_in, wt_in, b
        side, i = side_of(b)
        return idx, wt, side * 2 * PB + i

    def section(number, g, b, far=False):
        side, i = side_of(b)
        if (side == 1) == far:
            i -= PB
        return halo[side, tiles[number] + g * PB + i]

    def own(b):
        return 0 <= b < nblk

    def read_init(g, b):
        return init_ref[rows8(g), lanes(b)] if own(b) else section(0, g, b)

    ring = list(range(-PB, PB)) + list(range(nblk - PB, nblk + PB))
    place = {b: i for i, b in enumerate(ring)}

    def read_v1(g, b):
        return v1[rows8(g), lanes(place[b])]

    derive_cross = matrix_of(matrix_ref, starts[0], rows, own_pad)
    for side in range(2):
        first = nblk if side else -PB
        values = jnp.concatenate(
            [
                jnp.concatenate([section(0, g, first + i) for i in range(PB)], axis=1)
                for g in own_groups
            ],
            axis=0,
        )
        turn = dot(derive_cross, values)
        for i in range(PB):
            b = first + i
            bf = coefficient(table(b))
            for g in cross_groups:
                v1[rows8(g), lanes(place[b])] = -bf * turn[rows8(g), lanes(i)]
            sums = stencil(read_init, b, table(b), own_groups, own)
            for g in own_groups:
                v1[rows8(g), lanes(place[b])] = section(1, g, b) + sums[g]
        for i in range(PB):
            b = nblk - PB + i if side else i
            at = lanes(side * PB + i)
            sums = stencil(read_init, b, table(b), own_groups, lambda s: not own(s))
            for g in own_groups:
                v1[rows8(g), lanes(place[b])] = edge_ref[rows8(g), at] + sums[g]
            for g in cross_groups:
                v1[rows8(g), lanes(place[b])] = cend_ref[rows8(g - lead), at]
    both = matrix_of(matrix_ref, starts[1], rows + MODES, rows)
    restrict = matrix_of(matrix_ref, starts[1] + rows, MODES, rows)
    low = -2 * PB
    for side in range(2):
        b = nblk if side else -PB
        m1x[:, lanes(b - low, PB)] = dot(restrict, v1[:, lanes(place[b], PB)])
        b = nblk - PB if side else 0
        mixed = dot(both, v1[:, lanes(place[b], PB)])
        deriv[:, lanes(side * PB, PB)] = mixed[0:rows]
        m1x[:, lanes(b - low, PB)] = mixed[rows:]
    for b in list(range(-2 * PB, -PB)) + list(range(nblk + PB, nblk + 2 * PB)):
        for g in MODE_GROUPS:
            m1x[rows8(g), lanes(b - low)] = section(3, g, b, True)

    outer_own = list(range(2 * PB)) + list(range(nblk - 2 * PB, nblk))
    place2 = {b: i for i, b in enumerate(outer_own)}
    ends = list(range(PB)) + list(range(nblk - PB, nblk))
    for b in outer_own:
        at = lanes(place2[b])
        sums = stencil(read_v1, b, table(b), own_groups, lambda s: s in place)
        bf = coefficient(table(b))
        for g in own_groups:
            total = part_ref[rows8(g), at] + sums[g]
            if b in ends:
                total = total + (
                    KEEP * read_v1(g, b)
                    + scaled_ref[rows8(g), lanes(b)]
                    - bf * deriv[rows8(g), lanes(ends.index(b))]
                )
            v2[rows8(g), at] = total
        if b in ends:
            sums = stencil(read_v1, b, table(b), cross_groups, lambda s: not own(s))
        for i, g in enumerate(cross_groups):
            if b in ends:
                end = lanes(ends.index(b))
                v2[rows8(g), at] = (
                    cpart_ref[rows8(i), end] + sums[i] + KEEP * read_v1(g, b) - bf * deriv[rows8(g), end]
                )
            else:
                v2[rows8(g), at] = cross_ref[rows8(i), lanes(b - PB)]
    for d in range(0, 4 * PB, 2):
        m2x[:, lanes(outer_own[d] - low, 2)] = dot(restrict, v2[:, lanes(d, 2)])
    m2x[:, lanes(2 * PB - low, nblk - 4 * PB)] = m2i_ref[...]

    def reader(ref, first):
        return lambda g, b: ref[rows8(g), lanes(b - first)]

    def modes(src, first, b, keep, known=None):
        read = reader(src, first)
        sums = stencil(read, b, table(b), MODE_GROUPS, known)
        if keep is None:
            return sums
        parts = turned([read(g, b) for g in MODE_GROUPS], table(b), keep)
        return [total + part for total, part in zip(sums, parts)]

    near = list(range(-PB, 0)) + list(range(nblk, nblk + PB))
    far = list(range(-2 * PB, -PB)) + list(range(nblk + PB, nblk + 2 * PB))
    for b in far:
        sums = modes(m1x, low, b, None, lambda s: s in place)
        for g in MODE_GROUPS:
            m2x[rows8(g), lanes(b - low)] = section(4, g, b, True) + sums[g]
    for b in near:
        sums = modes(m1x, low, b, KEEP)
        for g in MODE_GROUPS:
            m2x[rows8(g), lanes(b - low)] = section(2, g, b) + sums[g]

    middle = range(2 * PB, nblk - 2 * PB)
    for b in range(-2 * PB, nblk + 2 * PB):
        if b in middle:
            sums = modes(m2x, low, b, None, lambda s: s not in middle)
        elif own(b):
            sums = modes(m2x, low, b, -RELAX, lambda s: s not in middle)
        else:
            sums = modes(m2x, low, b, -RELAX, lambda s: -2 * PB <= s < nblk + 2 * PB)
        for g in MODE_GROUPS:
            if own(b):
                ready = rp_ref[rows8(g), lanes(b)]
            else:
                ready = section(5, g, b, True) if b in far else section(2, g, b)
            rx[rows8(g), lanes(b - low)] = ready + sums[g]
    for b in range(-PB, nblk + PB):
        sums = modes(rx, low, b, KEEP)
        for g in MODE_GROUPS:
            c1x[rows8(g), lanes(b + PB)] = sums[g] + rx[rows8(g), lanes(b - low)]
    for b in range(nblk):
        sums = modes(c1x, -PB, b, KEEP)
        for g in MODE_GROUPS:
            c2x[rows8(g), lanes(b)] = sums[g] + rx[rows8(g), lanes(b - low)]

    prolong = matrix_of(matrix_ref, starts[3], rows, MODES)
    prolong_own = matrix_of(matrix_ref, starts[3], own_pad, MODES)
    cross = rows - own_pad
    for b in range(0, nblk, 2):
        values = c2x[:, lanes(b, 2)]
        if b in middle:
            base_ref[:, lanes(b, 2)] = own_ref[:, lanes(b - 2 * PB, 2)] + dot(prolong_own, values)
        elif b in ends:
            lifted = v2[:, lanes(place2[b], 2)] + dot(prolong, values)
            base_ref[:, lanes(b, 2)] = lifted[0:own_pad]
            send_ref[0:cross, lanes(ends.index(b), 2)] = lifted[own_pad:]
        else:
            base_ref[:, lanes(b, 2)] = v2[0:own_pad, lanes(place2[b], 2)] + dot(prolong_own, values)
        if b not in ends:
            fold, at = divmod(b - PB, 2 * PB)
            send_ref[cross + fold * MODES : cross + (fold + 1) * MODES, lanes(at, 2)] = values


def final_kernel(count, starts, base_ref, matrix_ref, *refs):
    out_ref = refs[-1]
    own_pad = base_ref.shape[0]
    nblk = out_ref.shape[1] // LANES
    early, late = refs[0 : 2 * count : 2], refs[1 : 2 * count : 2]
    ends = list(range(PB)) + list(range(nblk - PB, nblk))
    for b in range(0, nblk, 2):
        total = base_ref[:, lanes(b, 2)]
        for k in range(count):
            if b in ends:
                total = total + late[k][0:own_pad, lanes(ends.index(b), 2)]
            else:
                fold, at = divmod(b - PB, 2 * PB)
                lift = matrix_of(matrix_ref, starts[4 + k], own_pad, MODES)
                first = own_pad + fold * MODES
                total = (
                    total
                    + early[k][:, lanes(b - PB, 2)]
                    + dot(lift, late[k][first : first + MODES, lanes(at, 2)])
                )
        out_ref[:, lanes(b, 2)] = total


def vm(*shape):
    return pltpu.VMEM(shape, jnp.float32)


def f32(*shape):
    return jax.ShapeDtypeStruct(shape, jnp.float32)


def call(kernel, out_shape, scratch, cost_us, *args, fetch=False):
    whole = pl.BlockSpec(memory_space=pltpu.VMEM)
    single = not isinstance(out_shape, (tuple, list))
    return pl.pallas_call(
        kernel,
        out_shape=out_shape,
        in_specs=[pl.BlockSpec(memory_space=pltpu.HBM) if fetch else whole] * len(args),
        out_specs=whole if single else [whole] * len(out_shape),
        scratch_shapes=scratch,
        compiler_params=pltpu.CompilerParams(vmem_limit_bytes=16 * 1024 * 1024),
        cost_estimate=pl.CostEstimate(
            flops=int(cost_us * 1e8), bytes_accessed=int(cost_us * 3e6), transcendentals=0
        ),
    )(*args)


def per_device(initial, source, neighbors, face_weights, damping):
    own, cells = initial.shape
    nblk = cells // LANES
    inst_count = lax.axis_size("inst")
    cell_count = lax.axis_size("cell")
    own_pad = up8(own)
    matrices, starts, rows = constants(own, inst_count)
    matrices = jnp.asarray(matrices)
    cross = rows - own_pad
    if own_pad != own:
        initial = jnp.pad(initial, ((0, own_pad - own), (0, 0)))
        source = jnp.pad(source, ((0, own_pad - own), (0, 0)))
    _, tiles = halo_layout(own_pad)
    assert nblk >= 8 * PB and nblk % 2 == 0
    slots = NEIGH * (PB + 1) + 4
    folds = -(-(nblk - 2 * PB) // (2 * PB))

    def wide(height, blocks):
        return f32(height, blocks * LANES)

    def scratch(height, blocks):
        return vm(height, blocks * LANES)

    def int32(*shape):
        return jax.ShapeDtypeStruct(shape, jnp.int32)

    pack_a, pack_b, initial, scaled, smode, ends, idx, wt, matrices = call(
        functools.partial(pack_kernel, own_pad, starts),
        [f32(tiles, 8, LANES), f32(tiles, 8, LANES), wide(own_pad, nblk), wide(own_pad, nblk),
         wide(MODES, nblk), wide(own_pad, 2 * PB), int32(nblk, 8, LANES), f32(nblk, slots, LANES),
         jax.ShapeDtypeStruct(matrices.shape, matrices.dtype)],
        [scratch(own_pad, nblk), pltpu.VMEM((NEIGH, cells), jnp.int32), vm(NEIGH, cells), vm(1, cells),
         vm(8, cells), scratch(MODES, nblk), scratch(MODES, nblk - 2 * PB),
         scratch(MODES, nblk - 2 * PB), scratch(MODES, nblk - 2 * PB), pltpu.SemaphoreType.DMA((8,))],
        2,
        *[
            pltpu.with_memory_space_constraint(x, pltpu.HBM)
            for x in (initial, source, neighbors, face_weights, damping.reshape(1, cells), matrices)
        ],
        fetch=True,
    )
    near_pairs = [(i, i ^ 1) for i in range(cell_count) if i ^ 1 < cell_count]
    far_pairs = []
    for i in range(1, cell_count - 1, 2):
        far_pairs += [(i, i + 1), (i + 1, i)]
    halo_b = lax.ppermute(pack_b, "cell", far_pairs)
    halo_a = lax.ppermute(pack_a, "cell", near_pairs)

    own_mid, cross_mid, part, cpart, cend, m2, rp = call(
        functools.partial(inner_kernel, own_pad, rows, starts),
        [wide(own_pad, nblk - 4 * PB), wide(cross, nblk - 2 * PB), wide(own_pad, 4 * PB),
         wide(cross, 2 * PB), wide(cross, 2 * PB), wide(MODES, nblk - 4 * PB), wide(MODES, nblk)],
        [scratch(rows, nblk), scratch(rows, nblk)], 5,
        initial, scaled, smode, idx, wt, matrices,
    )

    def share(array, k):
        if cross == own_pad:
            return array
        part = lax.slice_in_dim(array, (k - 1) * own, k * own, axis=0)
        return jnp.pad(part, ((0, own_pad - own), (0, 0)))

    def shift(k):
        return [(i, (i + k) % inst_count) for i in range(inst_count)]

    early = [lax.ppermute(share(cross_mid, k), "inst", shift(k)) for k in range(1, inst_count)]

    base, send = call(
        functools.partial(outer_kernel, own_pad, rows, starts),
        [wide(own_pad, nblk), wide(cross + folds * MODES, 2 * PB)],
        [pltpu.VMEM((2, tiles, 8, LANES), jnp.float32), scratch(rows, 4 * PB), scratch(rows, 4 * PB),
         scratch(rows, 2 * PB), scratch(MODES, nblk + 4 * PB), scratch(MODES, nblk + 4 * PB),
         scratch(MODES, nblk + 4 * PB), scratch(MODES, nblk + 2 * PB), scratch(MODES, nblk),
         pltpu.VMEM((4 * PB, 8, LANES), jnp.int32), vm(4 * PB, slots, LANES)],
        8, halo_a, halo_b, initial, scaled, smode, ends, own_mid, cross_mid, part, cpart, cend, m2, rp,
        idx, wt, matrices,
    )

    def share_late(k):
        if cross == own_pad:
            return send
        return jnp.concatenate([share(send[:cross], k), send[cross:]], axis=0)

    late = [lax.ppermute(share_late(k), "inst", shift(k)) for k in range(1, inst_count)]
    received = [r for pair in zip(early, late) for r in pair]
    out = call(
        functools.partial(final_kernel, inst_count - 1, starts), f32(own_pad, cells), [], 1,
        base, matrices, *received,
    )
    return out[:own] if own_pad != own else out


def solution(mesh):
    return jax.shard_map(
        per_device,
        mesh=mesh,
        in_specs=(
            P("inst", "cell"),
            P("inst", "cell"),
            P(None, "cell"),
            P(None, "cell"),
            P("cell"),
        ),
        out_specs=P("inst", "cell"),
        check_vma=False,
    )
```

time: 244 us -> 22.6 us (0.09)
  local copies, waits for them, and re-layouts: 109 us -> 0 us
  other arithmetic: 34.9 us -> 0 us
  blocking collectives: 29.9 us -> 0 us
  starting transfers between devices: 32.2 us -> 4.4 us
  between operations: 13.9 us -> 0.03 us
  Pallas kernels: 0 us -> 10.1 us
  waiting for transfers between devices: 17.6 us -> 7.9 us
  matrix products: 4.44 us -> 0 us
    gather x5 -> x0, local copies, waits for them, and re-layouts: 105 us -> none  [neighbour_terms(): jnp.take(padded, flat_index, axis=1).reshape(padded.shape[0], NEIGH, cells)]
    all_gather x4 -> x0, blocking collectives: 29.9 us -> none  [the longest x3 25.5 us: derivative(): gathered = lax.all_gather(values, 'inst', axis=0, tiled=True)]
    ppermute x10 -> x4, starting transfers between devices: 32.2 us -> 4.4 us  [the longest x1 3.05 us: per_device(): halo_b = lax.ppermute(pack_b, 'cell', far_pairs)]
    select_n x7 -> x0, other arithmetic: 23.1 us -> none  [the longest x5 22.9 us: neighbour_terms(): jnp.take(padded, flat_index, axis=1).reshape(padded.shape[0], NEIGH, cells)]
    reduce_scatter x1 -> x0, waiting for transfers between devices: 10.7 us -> none  [per_device(): lax.psum_scatter(partial_terms, 'inst', scatter_dimension=1, tiled=True)]
    pallas_call x0 -> x4, Pallas kernels: none -> 10.1 us  [call(): pl.pallas_call(kernel, out_shape=out_shape, in_specs=[pl.BlockSpec(memory...]
    reduce_sum x6 -> x0, other arithmetic: 7.01 us -> none  [the longest x5 6.23 us: neighbour_terms(): return jnp.sum(face_weights[None, :, :] * picked, axis=1)]
    dot_general x7 -> x0, matrix products: 4.44 us -> none  [the longest x3 1.6 us: derivative(): return jnp.dot(own_rows, gathered, precision=highest)]
  transfers between devices with their start and end apart: 11 -> 4, of which waited for: 3 -> 3; matrix products, arithmetic and copies ran while one was open for 2% -> 0% of each run, Pallas kernels for 0% -> 30%
where the time goes in v3:
time: 22.6 us; the launch traced here: 22.4 us
  Pallas kernels  10.1 us (45%)
  waiting for transfers between devices  7.9 us (35%)
  starting transfers between devices  4.4 us (19%)
    pallas_call x4, Pallas kernels, call(): pl.pallas_call(kernel, out_shape=out_shape, in_specs=[pl.BlockSpec(memory...  10.1 us
    ppermute x1, waiting for transfers between devices, per_device(): lax.ppermute(share_late(k), 'inst', shift(k))  4.48 us
    ppermute x1, starting transfers between devices, per_device(): halo_b = lax.ppermute(pack_b, 'cell', far_pairs)  3.05 us
    ppermute x1, waiting for transfers between devices, per_device(): lax.ppermute(share(cross_mid, k), 'inst', shift(k))  1.83 us
    ppermute x1, waiting for transfers between devices, per_device(): halo_b = lax.ppermute(pack_b, 'cell', far_pairs)  1.59 us
    ppermute x1, starting transfers between devices, per_device(): halo_a = lax.ppermute(pack_a, 'cell', near_pairs)  0.72 us
  transfers between devices with their start and end apart: 4, of which 3 were waited for; matrix products, arithmetic and copies ran while one was open for 0% of the time, Pallas kernels for 30%

profile of v3, /device:TPU:19, one launch (start us, length us, event | category | flops | bytes accessed | tf_op | source)
XLA Modules:
  0.0 22.4 jit_solution(16653810262281731250)
XLA Ops:
  0.0 2.5 %shard_map.64 = (f32[41,8,128]{2,1,0:T(8,128)S(1)}, f32[41,8,128]{2,1,0:T(8,128)S(1)}, f32[40,2048]{1,0:T(8,128)S(1)}, f32[40,2048]{1,0:T(8,128)S(1)}, f32[16,20...) custom-call(f32[40,2048]{1,0:T(8,128)} %init_hbm.1, ...), custom_call_target="tpu_custom_call" | custom-call | flops 200000000 | bytes 6000000 | tf_op jit(solution)/shard_map/pallas_call | solution.py:586
  2.6 0.7 %collective-permute-start = (f32[41,8,128]{2,1,0:T(8,128)S(1)}, f32[41,8,128]{2,1,0:T(8,128)S(1)}, u32[]{:S(2)}, u32[]{:S(2)}) collective-permute-start(f32[41,8,128]{2,1,0:T(8,128)S(1)} %get-tuple-element.23), channel_id=1, source_target_pairs={{0,2},{2,0},{4,6},{6,4},{8,10},{10,8},{12,14},{14,12},{16,18},{18,... | collective-permute-start | bytes 503816 | tf_op jit(solution)/shard_map/ppermute | solution.py:645
  3.3 3.0 %collective-permute-start.1 = (f32[41,8,128]{2,1,0:T(8,128)S(1)}, f32[41,8,128]{2,1,0:T(8,128)S(1)}, u32[]{:S(2)}, u32[]{:S(2)}) collective-permute-start(f32[41,8,128]{2,1,0:T(8,128)S(1)} %get-tuple-element.24), channel_id=1, source_target_pairs={{2,4},{4,2},{6,8},{8,6},{10,12},{12,10},{14,16},{16,14},{18,20},{2... | collective-permute-start | bytes 503816 | tf_op jit(solution)/shard_map/ppermute | solution.py:644
  6.3 3.5 %shard_map.65 = (f32[40,1024]{1,0:T(8,128)S(1)}, f32[40,1536]{1,0:T(8,128)S(1)}, f32[40,1024]{1,0:T(8,128)S(1)}, f32[40,512]{1,0:T(8,128)S(1)}, f32[40,512]{1,0:...) custom-call(f32[40,2048]{1,0:T(8,128)S(1)} %get-tuple-element.25.init_ref, ...), custom_call_target="tpu_custom_call" | custom-call | flops 500000000 | bytes 15000000 | tf_op jit(solution)/shard_map/pallas_call | solution.py:586
  9.8 0.3 %collective-permute-start.2 = (f32[40,1536]{1,0:T(8,128)S(1)}, f32[40,1536]{1,0:T(8,128)S(1)}, u32[]{:S(2)}, u32[]{:S(2)}) collective-permute-start(f32[40,1536]{1,0:T(8,128)S(1)} %get-tuple-element.33.cross_ref), channel_id=1, source_target_pairs={{0,1},{1,0},{2,3},{3,2},{4,5},{5,4},{6,7},{7,6},{8,9},{9,8},{10,11... | collective-permute-start | bytes 737288 | tf_op jit(solution)/shard_map/ppermute | solution.py:664
  10.1 0.0 collective-permute-done.a_ref
  10.2 1.6 %collective-permute-done.1.b_ref = f32[41,8,128]{2,1,0:T(8,128)S(1)} collective-permute-done((f32[41,8,128]{2,1,0:T(8,128)S(1)}, f32[41,8,128]{2,1,0:T(8,128)S(1)}, u32[]{:S(2)}, u32[]{:S(2)}) %collective-permute-start.1) | collective-permute-done | bytes 167968 | tf_op jit(solution)/shard_map/ppermute | solution.py:644
  11.7 3.1 %shard_map.66 = (f32[40,2048]{1,0:T(8,128)S(1)}, f32[88,512]{1,0:T(8,128)S(1)}) custom-call(f32[41,8,128]{2,1,0:T(8,128)S(1)} %collective-permute-done.a_ref, f32[41,8,128]{2,1,0:T(8,128)S(1)} %collective-permute-done.1.b_ref, f32[40,2048]{1,0:T(8,128)S(1)} %get-tuple-element.25.init_ref, f32[40,2048]{1,0:T(8,128)S(1)} %get-tuple-element.26.scaled_ref, ...), custom_call_target="tpu_custom_call" | custom-call | flops 800000000 | bytes 24000000 | tf_op jit(solution)/shard_map/pallas_call | solution.py:586
  14.9 0.3 %collective-permute-start.3 = (f32[88,512]{1,0:T(8,128)S(1)}, f32[88,512]{1,0:T(8,128)S(1)}, u32[]{:S(2)}, u32[]{:S(2)}) collective-permute-start(f32[88,512]{1,0:T(8,128)S(1)} %get-tuple-element.40), channel_id=1, source_target_pairs={{0,1},{1,0},{2,3},{3,2},{4,5},{5,4},{6,7},{7,6},{8,9},{9,8},{10,11... | collective-permute-start | bytes 540680 | tf_op jit(solution)/shard_map/ppermute | solution.py:682
  15.2 1.8 %collective-permute-done.2.refs_0_ = f32[40,1536]{1,0:T(8,128)S(1)} collective-permute-done((f32[40,1536]{1,0:T(8,128)S(1)}, f32[40,1536]{1,0:T(8,128)S(1)}, u32[]{:S(2)}, u32[]{:S(2)}) %collective-permute-start.2) | collective-permute-done | bytes 245792 | tf_op jit(solution)/shard_map/ppermute | solution.py:664
  17.0 4.5 %collective-permute-done.3.refs_1_ = f32[88,512]{1,0:T(8,128)S(1)} collective-permute-done((f32[88,512]{1,0:T(8,128)S(1)}, f32[88,512]{1,0:T(8,128)S(1)}, u32[]{:S(2)}, u32[]{:S(2)}) %collective-permute-start.3) | collective-permute-done | bytes 180256 | tf_op jit(solution)/shard_map/ppermute | solution.py:682
  21.5 0.9 %shard_map.67 = f32[40,2048]{1,0:T(8,128)} custom-call(f32[40,2048]{1,0:T(8,128)S(1)} %get-tuple-element.39.base_ref, bf16[320,256]{1,0:T(8,128)(2,1)S(1)} %get-tuple-element.31.matrix_ref, f32[40,1536]{1,0:T(8,128)S(1)} %collective-permute-done.2.refs_0_, f32[88,512]{1,0:T(8,128)S(1)} %collective-permute-done.3.refs_1_), custom_call_target="tpu_custom_call" | custom-call | flops 100000000 | bytes 3000000 | tf_op jit(solution)/shard_map/pallas_call | solution.py:586
Async XLA Ops:
  2.6 7.6 %collective-permute-start = (f32[41,8,128]{2,1,0:T(8,128)S(1)}, f32[41,8,128]{2,1,0:T(8,128)S(1)}, u32[]{:S(2)}, u32[]{:S(2)}) collective-permute-start(f32[41,8,128]{2,1,0:T(8,128)S(1)} %get-tuple-element.23), channel_id=1, source_target_pairs={{0,2},{2,0},{4,6},{6,4},{8,10},{10,8},{12,14},{14,12},{16,18},{18,... | collective-permute-start | bytes 503816 | tf_op jit(solution)/shard_map/ppermute | solution.py:645
  3.3 8.5 %collective-permute-start.1 = (f32[41,8,128]{2,1,0:T(8,128)S(1)}, f32[41,8,128]{2,1,0:T(8,128)S(1)}, u32[]{:S(2)}, u32[]{:S(2)}) collective-permute-start(f32[41,8,128]{2,1,0:T(8,128)S(1)} %get-tuple-element.24), channel_id=1, source_target_pairs={{2,4},{4,2},{6,8},{8,6},{10,12},{12,10},{14,16},{16,14},{18,20},{2... | collective-permute-start | bytes 503816 | tf_op jit(solution)/shard_map/ppermute | solution.py:644
  9.8 7.2 %collective-permute-start.2 = (f32[40,1536]{1,0:T(8,128)S(1)}, f32[40,1536]{1,0:T(8,128)S(1)}, u32[]{:S(2)}, u32[]{:S(2)}) collective-permute-start(f32[40,1536]{1,0:T(8,128)S(1)} %get-tuple-element.33.cross_ref), channel_id=1, source_target_pairs={{0,1},{1,0},{2,3},{3,2},{4,5},{5,4},{6,7},{7,6},{8,9},{9,8},{10,11... | collective-permute-start | bytes 737288 | tf_op jit(solution)/shard_map/ppermute | solution.py:664
  14.9 6.6 %collective-permute-start.3 = (f32[88,512]{1,0:T(8,128)S(1)}, f32[88,512]{1,0:T(8,128)S(1)}, u32[]{:S(2)}, u32[]{:S(2)}) collective-permute-start(f32[88,512]{1,0:T(8,128)S(1)} %get-tuple-element.40), channel_id=1, source_target_pairs={{0,1},{1,0},{2,3},{3,2},{4,5},{5,4},{6,7},{7,6},{8,9},{9,8},{10,11... | collective-permute-start | bytes 540680 | tf_op jit(solution)/shard_map/ppermute | solution.py:682

commit v4 on v3

--- a/solution.py
+++ b/solution.py
@@ -280,9 +280,8 @@
         pack(b_ref, True)
 
 
-def inner_kernel(own_pad, rows, starts, init_ref, scaled_ref, smode_ref, idx_ref, wt_ref, matrix_ref,
-                 own_ref, cross_ref, part_ref, cpart_ref, cend_ref, m2_ref, rp_ref,
-                 first, deriv):
+def cross_kernel(own_pad, rows, starts, init_ref, scaled_ref, idx_ref, wt_ref, matrix_ref,
+                 cross_ref, first, deriv):
     cells = init_ref.shape[1]
     nblk = cells // LANES
     own_groups = list(range(own_pad // 8))
@@ -318,27 +317,38 @@
     derive = matrix_of(matrix_ref, starts[1], rows, rows)
     for d in range(PB, nblk - PB, 2):
         deriv[:, lanes(d, 2)] = dot(derive, first[:, lanes(d, 2)])
-
-    def local(g, b):
+    for b in inside:
+        sums = stencil(read_first, b, table(b), cross_groups)
         bf = coefficient(table(b))
-        return KEEP * first[rows8(g), lanes(b)] - bf * deriv[rows8(g), lanes(b)]
+        for g, total in zip(cross_groups, sums):
+            cross_ref[rows8(g - len(own_groups)), lanes(b - PB)] = (
+                KEEP * read_first(g, b) - bf * deriv[rows8(g), lanes(b)] + total
+            )
+
+
+def inner_kernel(own_pad, rows, starts, first, deriv, scaled_ref, smode_ref, cross_ref, idx_ref, wt_ref,
+                 matrix_ref, own_ref, part_ref, cpart_ref, m2_ref, rp_ref):
+    cells = scaled_ref.shape[1]
+    nblk = cells // LANES
+    own_groups = list(range(own_pad // 8))
+    cross_groups = list(range(own_pad // 8, rows // 8))
+    inside = range(PB, nblk - PB)
+    middle = range(2 * PB, nblk - 2 * PB)
+
+    def table(b):
+        return idx_ref, wt_ref, b
+
+    def read_first(g, b):
+        return first[rows8(g), lanes(b)]
 
     for b in range(nblk):
-        sums = stencil(read_first, b, table(b), cross_groups, lambda s: 0 <= s < nblk)
-        for g, total in zip(cross_groups, sums):
-            part = rows8(g - len(own_groups))
-            if b in inside:
-                cross_ref[part, lanes(b - PB)] = local(g, b) + total
-            else:
-                at = lanes(b if b < PB else b - nblk + 2 * PB)
-                cpart_ref[part, at] = total
-                cend_ref[part, at] = first[rows8(g), lanes(b)]
-    middle = range(2 * PB, nblk - 2 * PB)
-    for b in range(nblk):
+        bf = coefficient(table(b))
         sums = stencil(read_first, b, table(b), own_groups, lambda s: s in inside)
         for g, total in zip(own_groups, sums):
             if b in inside:
-                total = total + local(g, b) + scaled_ref[rows8(g), lanes(b)]
+                total = total + (
+                    KEEP * read_first(g, b) - bf * deriv[rows8(g), lanes(b)] + scaled_ref[rows8(g), lanes(b)]
+                )
             if b in middle:
                 own_ref[rows8(g), lanes(b - 2 * PB)] = total
             else:
@@ -347,6 +357,11 @@
     for d in range(0, nblk - 4 * PB, 2):
         values = jnp.concatenate([own_ref[:, lanes(d, 2)], cross_ref[:, lanes(PB + d, 2)]], axis=0)
         m2_ref[:, lanes(d, 2)] = dot(restrict, values)
+    for b in list(range(PB)) + list(range(nblk - PB, nblk)):
+        sums = stencil(read_first, b, table(b), cross_groups, lambda s: 0 <= s < nblk)
+        for g, total in zip(cross_groups, sums):
+            part = rows8(g - len(own_groups))
+            cpart_ref[part, lanes(b if b < PB else b - nblk + 2 * PB)] = total
 
     def read_m2(g, b):
         return m2_ref[rows8(g), lanes(b - 2 * PB)]
@@ -361,7 +376,7 @@
 
 
 def outer_kernel(own_pad, rows, starts, a_ref, b_ref, init_ref, scaled_ref, smode_ref, edge_ref,
-                 own_ref, cross_ref, part_ref, cpart_ref, cend_ref, m2i_ref, rp_ref, idx_in, wt_in,
+                 own_ref, cross_ref, part_ref, cpart_ref, first_ref, m2i_ref, rp_ref, idx_in, wt_in,
                  matrix_ref, base_ref, send_ref,
                  halo, v1, v2, deriv, m1x, m2x, rx, c1x, c2x, idx, wt):
     cells = init_ref.shape[1]
@@ -441,7 +456,7 @@
             for g in own_groups:
                 v1[rows8(g), lanes(place[b])] = edge_ref[rows8(g), at] + sums[g]
             for g in cross_groups:
-                v1[rows8(g), lanes(place[b])] = cend_ref[rows8(g - lead), at]
+                v1[rows8(g), lanes(place[b])] = first_ref[rows8(g), lanes(b)]
     both = matrix_of(matrix_ref, starts[1], rows + MODES, rows)
     restrict = matrix_of(matrix_ref, starts[1] + rows, MODES, rows)
     low = -2 * PB
@@ -550,10 +565,11 @@
 
 
 def final_kernel(count, starts, base_ref, matrix_ref, *refs):
-    out_ref = refs[-1]
+    out_hbm, out_ref, sems = refs[2 * count :]
     own_pad = base_ref.shape[0]
     nblk = out_ref.shape[1] // LANES
     early, late = refs[0 : 2 * count : 2], refs[1 : 2 * count : 2]
+    copies = []
     ends = list(range(PB)) + list(range(nblk - PB, nblk))
     for b in range(0, nblk, 2):
         total = base_ref[:, lanes(b, 2)]
@@ -570,6 +586,12 @@
                     + dot(lift, late[k][first : first + MODES, lanes(at, 2)])
                 )
         out_ref[:, lanes(b, 2)] = total
+        if b % 4 == 2:
+            piece = (slice(None), lanes(b - 2, 4))
+            copies.append(pltpu.make_async_copy(out_ref.at[piece], out_hbm.at[piece], sems.at[b // 4]))
+            copies[-1].start()
+    for copy in copies:
+        copy.wait()
 
 
 def vm(*shape):
@@ -580,14 +602,14 @@
     return jax.ShapeDtypeStruct(shape, jnp.float32)
 
 
-def call(kernel, out_shape, scratch, cost_us, *args, fetch=False):
+def call(kernel, out_shape, scratch, cost_us, *args, fetch=False, store=False):
     whole = pl.BlockSpec(memory_space=pltpu.VMEM)
     single = not isinstance(out_shape, (tuple, list))
     return pl.pallas_call(
         kernel,
         out_shape=out_shape,
         in_specs=[pl.BlockSpec(memory_space=pltpu.HBM) if fetch else whole] * len(args),
-        out_specs=whole if single else [whole] * len(out_shape),
+        out_specs=(pl.BlockSpec(memory_space=pltpu.HBM) if store else whole) if single else [whole] * len(out_shape),
         scratch_shapes=scratch,
         compiler_params=pltpu.CompilerParams(vmem_limit_bytes=16 * 1024 * 1024),
         cost_estimate=pl.CostEstimate(
@@ -609,7 +631,7 @@
         initial = jnp.pad(initial, ((0, own_pad - own), (0, 0)))
         source = jnp.pad(source, ((0, own_pad - own), (0, 0)))
     _, tiles = halo_layout(own_pad)
-    assert nblk >= 8 * PB and nblk % 2 == 0
+    assert nblk >= 8 * PB and nblk % 4 == 0
     slots = NEIGH * (PB + 1) + 4
     folds = -(-(nblk - 2 * PB) // (2 * PB))
 
@@ -644,12 +666,10 @@
     halo_b = lax.ppermute(pack_b, "cell", far_pairs)
     halo_a = lax.ppermute(pack_a, "cell", near_pairs)
 
-    own_mid, cross_mid, part, cpart, cend, m2, rp = call(
-        functools.partial(inner_kernel, own_pad, rows, starts),
-        [wide(own_pad, nblk - 4 * PB), wide(cross, nblk - 2 * PB), wide(own_pad, 4 * PB),
-         wide(cross, 2 * PB), wide(cross, 2 * PB), wide(MODES, nblk - 4 * PB), wide(MODES, nblk)],
-        [scratch(rows, nblk), scratch(rows, nblk)], 5,
-        initial, scaled, smode, idx, wt, matrices,
+    cross_mid, first, deriv = call(
+        functools.partial(cross_kernel, own_pad, rows, starts),
+        [wide(cross, nblk - 2 * PB), wide(rows, nblk), wide(rows, nblk)], [], 3,
+        initial, scaled, idx, wt, matrices,
     )
 
     def share(array, k):
@@ -663,6 +683,12 @@
 
     early = [lax.ppermute(share(cross_mid, k), "inst", shift(k)) for k in range(1, inst_count)]
 
+    own_mid, part, cpart, m2, rp = call(
+        functools.partial(inner_kernel, own_pad, rows, starts),
+        [wide(own_pad, nblk - 4 * PB), wide(own_pad, 4 * PB), wide(cross, 2 * PB),
+         wide(MODES, nblk - 4 * PB), wide(MODES, nblk)], [], 3,
+        first, deriv, scaled, smode, cross_mid, idx, wt, matrices,
+    )
     base, send = call(
         functools.partial(outer_kernel, own_pad, rows, starts),
         [wide(own_pad, nblk), wide(cross + folds * MODES, 2 * PB)],
@@ -670,7 +696,7 @@
          scratch(rows, 2 * PB), scratch(MODES, nblk + 4 * PB), scratch(MODES, nblk + 4 * PB),
          scratch(MODES, nblk + 4 * PB), scratch(MODES, nblk + 2 * PB), scratch(MODES, nblk),
          pltpu.VMEM((4 * PB, 8, LANES), jnp.int32), vm(4 * PB, slots, LANES)],
-        8, halo_a, halo_b, initial, scaled, smode, ends, own_mid, cross_mid, part, cpart, cend, m2, rp,
+        8, halo_a, halo_b, initial, scaled, smode, ends, own_mid, cross_mid, part, cpart, first, m2, rp,
         idx, wt, matrices,
     )
 
@@ -682,8 +708,9 @@
     late = [lax.ppermute(share_late(k), "inst", shift(k)) for k in range(1, inst_count)]
     received = [r for pair in zip(early, late) for r in pair]
     out = call(
-        functools.partial(final_kernel, inst_count - 1, starts), f32(own_pad, cells), [], 1,
-        base, matrices, *received,
+        functools.partial(final_kernel, inst_count - 1, starts), f32(own_pad, cells),
+        [vm(own_pad, cells), pltpu.SemaphoreType.DMA((nblk // 4,))], 1,
+        base, matrices, *received, store=True,
     )
     return out[:own] if own_pad != own else out
 

time: 22.6 us -> 22.6 us (level)
  the two profiles are of different devices: /device:TPU:19 before, /device:TPU:24 now
where the time goes in v4:
time: 22.6 us; the launch traced here: 22.4 us
  Pallas kernels  10.2 us (45%)
  waiting for transfers between devices  6.54 us (29%)
  starting transfers between devices  5.68 us (25%)
    pallas_call x5, Pallas kernels, call(): pl.pallas_call(kernel, out_shape=out_shape, in_specs=[pl.BlockSpec(memory...  10.2 us
    ppermute x1, waiting for transfers between devices, per_device(): lax.ppermute(share_late(k), 'inst', shift(k))  5.49 us
    ppermute x1, starting transfers between devices, per_device(): halo_b = lax.ppermute(pack_b, 'cell', far_pairs)  3.4 us
    ppermute x1, starting transfers between devices, per_device(): lax.ppermute(share(cross_mid, k), 'inst', shift(k))  1.56 us
    ppermute x1, waiting for transfers between devices, per_device(): lax.ppermute(share(cross_mid, k), 'inst', shift(k))  1.05 us
    ppermute x1, starting transfers between devices, per_device(): lax.ppermute(share_late(k), 'inst', shift(k))  0.64 us
  transfers between devices with their start and end apart: 4, of which 2 were waited for; matrix products, arithmetic and copies ran while one was open for 0% of the time, Pallas kernels for 30%

profile of v4, /device:TPU:24, one launch (start us, length us, event | category | flops | bytes accessed | tf_op | source)
XLA Modules:
  0.0 22.4 jit_solution(5195696128955444559)
XLA Ops:
  0.0 2.5 %shard_map.64 = (f32[41,8,128]{2,1,0:T(8,128)S(1)}, f32[41,8,128]{2,1,0:T(8,128)S(1)}, f32[40,2048]{1,0:T(8,128)S(1)}, f32[40,2048]{1,0:T(8,128)S(1)}, f32[16,20...) custom-call(f32[40,2048]{1,0:T(8,128)} %init_hbm.1, ...), custom_call_target="tpu_custom_call" | custom-call | flops 200000000 | bytes 6000000 | tf_op jit(solution)/shard_map/pallas_call | solution.py:608
  2.5 0.1 collective-permute-start
  2.6 3.4 %collective-permute-start.1 = (f32[41,8,128]{2,1,0:T(8,128)S(1)}, f32[41,8,128]{2,1,0:T(8,128)S(1)}, u32[]{:S(2)}, u32[]{:S(2)}) collective-permute-start(f32[41,8,128]{2,1,0:T(8,128)S(1)} %get-tuple-element.25), channel_id=1, source_target_pairs={{2,4},{4,2},{6,8},{8,6},{10,12},{12,10},{14,16},{16,14},{18,20},{2... | collective-permute-start | bytes 503816 | tf_op jit(solution)/shard_map/ppermute | solution.py:666
  6.0 2.0 %shard_map.65 = (f32[40,1536]{1,0:T(8,128)S(1)}, f32[80,2048]{1,0:T(8,128)S(1)}, f32[80,2048]{1,0:T(8,128)S(1)}) custom-call(f32[40,2048]{1,0:T(8,128)S(1)} %get-tuple-element.26.init_ref, f32[40,2048]{1,0:T(8,128)S(1)} %get-tuple-element.27.scaled_ref, s32[16,8,128]{2,1,0:T(8,128)S(1)} %get-tuple-element.30.idx_ref.idx_in, ...), custom_call_target="tpu_custom_call" | custom-call | flops 300000000 | bytes 9000000 | tf_op jit(solution)/shard_map/pallas_call | solution.py:608
  8.0 1.6 %collective-permute-start.2 = (f32[40,1536]{1,0:T(8,128)S(1)}, f32[40,1536]{1,0:T(8,128)S(1)}, u32[]{:S(2)}, u32[]{:S(2)}) collective-permute-start(f32[40,1536]{1,0:T(8,128)S(1)} %get-tuple-element.35.cross_ref), channel_id=1, source_target_pairs={{0,1},{1,0},{2,3},{3,2},{4,5},{5,4},{6,7},{7,6},{8,9},{9,8},{10,11... | collective-permute-start | bytes 737288 | tf_op jit(solution)/shard_map/ppermute | solution.py:684
  9.6 1.6 %shard_map.66 = (f32[40,1024]{1,0:T(8,128)S(1)}, f32[40,1024]{1,0:T(8,128)S(1)}, f32[40,512]{1,0:T(8,128)S(1)}, f32[16,1024]{1,0:T(8,128)S(1)}, f32[16,2048]{1,0:T(8,128)S(1)}) custom-call(f32[80,2048]{1,0:T(8,128)S(1)} %get-tuple-element.33.first.first_ref, f32[80,2048]{1,0:T(8,128)S(1)} %get-tuple-element.34.deriv, ...), custom_call_target="tpu_custom_call" | custom-call | flops 300000000 | bytes 9000000 | tf_op jit(solution)/shard_map/pallas_call | solution.py:608
  11.2 0.0 collective-permute-done.a_ref
  11.2 0.0 collective-permute-done.1.b_ref
  11.2 3.2 %shard_map.67 = (f32[40,2048]{1,0:T(8,128)S(1)}, f32[88,512]{1,0:T(8,128)S(1)}) custom-call(f32[41,8,128]{2,1,0:T(8,128)S(1)} %collective-permute-done.a_ref, f32[41,8,128]{2,1,0:T(8,128)S(1)} %collective-permute-done.1.b_ref, f32[40,2048]{1,0:T(8,128)S(1)} %get-tuple-element.26.init_ref, f32[40,2048]{1,0:T(8,128)S(1)} %get-tuple-element.27.scaled_ref, ...), custom_call_target="tpu_custom_call" | custom-call | flops 800000000 | bytes 24000000 | tf_op jit(solution)/shard_map/pallas_call | solution.py:608
  14.4 0.6 %collective-permute-start.3 = (f32[88,512]{1,0:T(8,128)S(1)}, f32[88,512]{1,0:T(8,128)S(1)}, u32[]{:S(2)}, u32[]{:S(2)}) collective-permute-start(f32[88,512]{1,0:T(8,128)S(1)} %get-tuple-element.42), channel_id=1, source_target_pairs={{0,1},{1,0},{2,3},{3,2},{4,5},{5,4},{6,7},{7,6},{8,9},{9,8},{10,11... | collective-permute-start | bytes 540680 | tf_op jit(solution)/shard_map/ppermute | solution.py:708
  15.0 1.0 %collective-permute-done.2.refs_0_ = f32[40,1536]{1,0:T(8,128)S(1)} collective-permute-done((f32[40,1536]{1,0:T(8,128)S(1)}, f32[40,1536]{1,0:T(8,128)S(1)}, u32[]{:S(2)}, u32[]{:S(2)}) %collective-permute-start.2) | collective-permute-done | bytes 245792 | tf_op jit(solution)/shard_map/ppermute | solution.py:684
  16.1 5.5 %collective-permute-done.3.refs_1_ = f32[88,512]{1,0:T(8,128)S(1)} collective-permute-done((f32[88,512]{1,0:T(8,128)S(1)}, f32[88,512]{1,0:T(8,128)S(1)}, u32[]{:S(2)}, u32[]{:S(2)}) %collective-permute-start.3) | collective-permute-done | bytes 180256 | tf_op jit(solution)/shard_map/ppermute | solution.py:708
  21.6 0.9 %shard_map.68 = f32[40,2048]{1,0:T(8,128)} custom-call(f32[40,2048]{1,0:T(8,128)S(1)} %get-tuple-element.41.base_ref, bf16[320,256]{1,0:T(8,128)(2,1)S(1)} %get-tuple-element.32.matrix_ref, f32[40,1536]{1,0:T(8,128)S(1)} %collective-permute-done.2.refs_0_, f32[88,512]{1,0:T(8,128)S(1)} %collective-permute-done.3.refs_1_), custom_call_target="tpu_custom_call" | custom-call | flops 100000000 | bytes 3000000 | tf_op jit(solution)/shard_map/pallas_call | solution.py:608
Async XLA Ops:
  2.5 8.6 %collective-permute-start = (f32[41,8,128]{2,1,0:T(8,128)S(1)}, f32[41,8,128]{2,1,0:T(8,128)S(1)}, u32[]{:S(2)}, u32[]{:S(2)}) collective-permute-start(f32[41,8,128]{2,1,0:T(8,128)S(1)} %get-tuple-element.24), channel_id=1, source_target_pairs={{0,2},{2,0},{4,6},{6,4},{8,10},{10,8},{12,14},{14,12},{16,18},{18,... | collective-permute-start | bytes 503816 | tf_op jit(solution)/shard_map/ppermute | solution.py:667
  2.6 8.6 %collective-permute-start.1 = (f32[41,8,128]{2,1,0:T(8,128)S(1)}, f32[41,8,128]{2,1,0:T(8,128)S(1)}, u32[]{:S(2)}, u32[]{:S(2)}) collective-permute-start(f32[41,8,128]{2,1,0:T(8,128)S(1)} %get-tuple-element.25), channel_id=1, source_target_pairs={{2,4},{4,2},{6,8},{8,6},{10,12},{12,10},{14,16},{16,14},{18,20},{2... | collective-permute-start | bytes 503816 | tf_op jit(solution)/shard_map/ppermute | solution.py:666
  8.0 8.1 %collective-permute-start.2 = (f32[40,1536]{1,0:T(8,128)S(1)}, f32[40,1536]{1,0:T(8,128)S(1)}, u32[]{:S(2)}, u32[]{:S(2)}) collective-permute-start(f32[40,1536]{1,0:T(8,128)S(1)} %get-tuple-element.35.cross_ref), channel_id=1, source_target_pairs={{0,1},{1,0},{2,3},{3,2},{4,5},{5,4},{6,7},{7,6},{8,9},{9,8},{10,11... | collective-permute-start | bytes 737288 | tf_op jit(solution)/shard_map/ppermute | solution.py:684
  14.4 7.2 %collective-permute-start.3 = (f32[88,512]{1,0:T(8,128)S(1)}, f32[88,512]{1,0:T(8,128)S(1)}, u32[]{:S(2)}, u32[]{:S(2)}) collective-permute-start(f32[88,512]{1,0:T(8,128)S(1)} %get-tuple-element.42), channel_id=1, source_target_pairs={{0,1},{1,0},{2,3},{3,2},{4,5},{5,4},{6,7},{7,6},{8,9},{9,8},{10,11... | collective-permute-start | bytes 540680 | tf_op jit(solution)/shard_map/ppermute | solution.py:708

commit v5 on v4

--- a/solution.py
+++ b/solution.py
@@ -165,8 +165,8 @@
 
 
 def pack_kernel(own_pad, starts, init_hbm, src_hbm, near_hbm, face_hbm, damp_hbm, matrix_hbm,
-                a_ref, b_ref, init_ref, scaled_ref, mode_ref, edge_ref, idx_ref, wt_ref, matrix_ref,
-                src_ref, near_ref, face_ref, damp_ref, coef_ref, m0, m1, m2, rp, sems):
+                a_ref, b_ref, init_ref, scaled_ref, mode_ref, edge_ref, m1, m2, idx_ref, wt_ref, matrix_ref,
+                src_ref, near_ref, face_ref, damp_ref, coef_ref, m0, rp, sems):
     cells = init_ref.shape[1]
     nblk = cells // LANES
     half = own_pad // 16 * 8
@@ -326,14 +326,14 @@
             )
 
 
-def inner_kernel(own_pad, rows, starts, first, deriv, scaled_ref, smode_ref, cross_ref, idx_ref, wt_ref,
-                 matrix_ref, own_ref, part_ref, cpart_ref, m2_ref, rp_ref):
-    cells = scaled_ref.shape[1]
+def inner_kernel(own_pad, rows, first, smode_ref, m1_ref, m2_ref, idx_ref, wt_ref,
+                 cpart_ref, mpart_ref, m2_out, rp_ref):
+    cells = smode_ref.shape[1]
     nblk = cells // LANES
-    own_groups = list(range(own_pad // 8))
     cross_groups = list(range(own_pad // 8, rows // 8))
     inside = range(PB, nblk - PB)
     middle = range(2 * PB, nblk - 2 * PB)
+    ends = list(range(PB)) + list(range(nblk - PB, nblk))
 
     def table(b):
         return idx_ref, wt_ref, b
@@ -341,31 +341,26 @@
     def read_first(g, b):
         return first[rows8(g), lanes(b)]
 
-    for b in range(nblk):
-        bf = coefficient(table(b))
-        sums = stencil(read_first, b, table(b), own_groups, lambda s: s in inside)
-        for g, total in zip(own_groups, sums):
-            if b in inside:
-                total = total + (
-                    KEEP * read_first(g, b) - bf * deriv[rows8(g), lanes(b)] + scaled_ref[rows8(g), lanes(b)]
-                )
-            if b in middle:
-                own_ref[rows8(g), lanes(b - 2 * PB)] = total
-            else:
-                part_ref[rows8(g), lanes(b if b < 2 * PB else b - nblk + 4 * PB)] = total
-    restrict = matrix_of(matrix_ref, starts[1] + rows, MODES, rows)
-    for d in range(0, nblk - 4 * PB, 2):
-        values = jnp.concatenate([own_ref[:, lanes(d, 2)], cross_ref[:, lanes(PB + d, 2)]], axis=0)
-        m2_ref[:, lanes(d, 2)] = dot(restrict, values)
-    for b in list(range(PB)) + list(range(nblk - PB, nblk)):
+    def read_m1(g, b):
+        return m1_ref[rows8(g), lanes(b - PB)]
+
+    def read_m2(g, b):
+        return m2_out[rows8(g), lanes(b - PB)]
+
+    m2_out[...] = m2_ref[...]
+    for b in range(3 * PB, nblk - 3 * PB):
+        sums = stencil(read_m1, b, table(b), MODE_GROUPS)
+        parts = turned([read_m1(g, b) for g in MODE_GROUPS], table(b), KEEP)
+        for g in MODE_GROUPS:
+            m2_out[rows8(g), lanes(b - PB)] = parts[g] + sums[g] + smode_ref[rows8(g), lanes(b)]
+    for i, b in enumerate(ends):
+        sums = stencil(read_m1, b, table(b), MODE_GROUPS, lambda s: s in inside)
+        for g in MODE_GROUPS:
+            mpart_ref[rows8(g), lanes(i)] = sums[g] + smode_ref[rows8(g), lanes(b)]
+    for i, b in enumerate(ends):
         sums = stencil(read_first, b, table(b), cross_groups, lambda s: 0 <= s < nblk)
         for g, total in zip(cross_groups, sums):
-            part = rows8(g - len(own_groups))
-            cpart_ref[part, lanes(b if b < PB else b - nblk + 2 * PB)] = total
-
-    def read_m2(g, b):
-        return m2_ref[rows8(g), lanes(b - 2 * PB)]
-
+            cpart_ref[rows8(g - own_pad // 8), lanes(i)] = total
     for b in range(nblk):
         sums = stencil(read_m2, b, table(b), MODE_GROUPS, lambda s: s in middle)
         if b in middle:
@@ -375,10 +370,10 @@
             rp_ref[rows8(g), lanes(b)] = sums[g] + smode_ref[rows8(g), lanes(b)]
 
 
-def outer_kernel(own_pad, rows, starts, a_ref, b_ref, init_ref, scaled_ref, smode_ref, edge_ref,
-                 own_ref, cross_ref, part_ref, cpart_ref, first_ref, m2i_ref, rp_ref, idx_in, wt_in,
-                 matrix_ref, base_ref, send_ref,
-                 halo, v1, v2, deriv, m1x, m2x, rx, c1x, c2x, idx, wt):
+def outer_kernel(own_pad, rows, starts, a_ref, b_ref, init_ref, smode_ref, edge_ref,
+                 cpart_ref, mpart_ref, first_ref, m1i_ref, m2i_ref, rp_ref, idx_in, wt_in,
+                 matrix_ref, send_ref, v1, deriv, c2x,
+                 halo, v2, m1x, m2x, rx, c1x, idx, wt):
     cells = init_ref.shape[1]
     nblk = cells // LANES
     lead = own_pad // 8
@@ -467,39 +462,19 @@
         mixed = dot(both, v1[:, lanes(place[b], PB)])
         deriv[:, lanes(side * PB, PB)] = mixed[0:rows]
         m1x[:, lanes(b - low, PB)] = mixed[rows:]
+    m1x[:, lanes(PB - low, nblk - 2 * PB)] = m1i_ref[...]
     for b in list(range(-2 * PB, -PB)) + list(range(nblk + PB, nblk + 2 * PB)):
         for g in MODE_GROUPS:
             m1x[rows8(g), lanes(b - low)] = section(3, g, b, True)
 
-    outer_own = list(range(2 * PB)) + list(range(nblk - 2 * PB, nblk))
-    place2 = {b: i for i, b in enumerate(outer_own)}
     ends = list(range(PB)) + list(range(nblk - PB, nblk))
-    for b in outer_own:
-        at = lanes(place2[b])
-        sums = stencil(read_v1, b, table(b), own_groups, lambda s: s in place)
+    for i, b in enumerate(ends):
+        at = lanes(i)
+        sums = stencil(read_v1, b, table(b), cross_groups, lambda s: not own(s))
         bf = coefficient(table(b))
-        for g in own_groups:
-            total = part_ref[rows8(g), at] + sums[g]
-            if b in ends:
-                total = total + (
-                    KEEP * read_v1(g, b)
-                    + scaled_ref[rows8(g), lanes(b)]
-                    - bf * deriv[rows8(g), lanes(ends.index(b))]
-                )
-            v2[rows8(g), at] = total
-        if b in ends:
-            sums = stencil(read_v1, b, table(b), cross_groups, lambda s: not own(s))
-        for i, g in enumerate(cross_groups):
-            if b in ends:
-                end = lanes(ends.index(b))
-                v2[rows8(g), at] = (
-                    cpart_ref[rows8(i), end] + sums[i] + KEEP * read_v1(g, b) - bf * deriv[rows8(g), end]
-                )
-            else:
-                v2[rows8(g), at] = cross_ref[rows8(i), lanes(b - PB)]
-    for d in range(0, 4 * PB, 2):
-        m2x[:, lanes(outer_own[d] - low, 2)] = dot(restrict, v2[:, lanes(d, 2)])
-    m2x[:, lanes(2 * PB - low, nblk - 4 * PB)] = m2i_ref[...]
+        for g, total in zip(cross_groups, sums):
+            part = rows8(g - lead)
+            v2[part, at] = cpart_ref[part, at] + total + KEEP * read_v1(g, b) - bf * deriv[rows8(g), at]
 
     def reader(ref, first):
         return lambda g, b: ref[rows8(g), lanes(b - first)]
@@ -522,6 +497,15 @@
         sums = modes(m1x, low, b, KEEP)
         for g in MODE_GROUPS:
             m2x[rows8(g), lanes(b - low)] = section(2, g, b) + sums[g]
+    for i, b in enumerate(ends):
+        sums = modes(m1x, low, b, KEEP, lambda s: s in place)
+        for g in MODE_GROUPS:
+            m2x[rows8(g), lanes(b - low)] = mpart_ref[rows8(g), lanes(i)] + sums[g]
+    m2x[:, lanes(2 * PB - low, nblk - 4 * PB)] = m2i_ref[:, lanes(PB, nblk - 4 * PB)]
+    for b in list(range(PB, 2 * PB)) + list(range(nblk - 2 * PB, nblk - PB)):
+        sums = modes(m1x, low, b, None, lambda s: s in place)
+        for g in MODE_GROUPS:
+            m2x[rows8(g), lanes(b - low)] = m2i_ref[rows8(g), lanes(b - PB)] + sums[g]
 
     middle = range(2 * PB, nblk - 2 * PB)
     for b in range(-2 * PB, nblk + 2 * PB):
@@ -546,22 +530,50 @@
         for g in MODE_GROUPS:
             c2x[rows8(g), lanes(b)] = sums[g] + rx[rows8(g), lanes(b - low)]
 
-    prolong = matrix_of(matrix_ref, starts[3], rows, MODES)
-    prolong_own = matrix_of(matrix_ref, starts[3], own_pad, MODES)
     cross = rows - own_pad
+    prolong = matrix_of(matrix_ref, starts[3] + own_pad, cross, MODES)
     for b in range(0, nblk, 2):
         values = c2x[:, lanes(b, 2)]
-        if b in middle:
-            base_ref[:, lanes(b, 2)] = own_ref[:, lanes(b - 2 * PB, 2)] + dot(prolong_own, values)
-        elif b in ends:
-            lifted = v2[:, lanes(place2[b], 2)] + dot(prolong, values)
-            base_ref[:, lanes(b, 2)] = lifted[0:own_pad]
-            send_ref[0:cross, lanes(ends.index(b), 2)] = lifted[own_pad:]
+        if b in ends:
+            at = lanes(ends.index(b), 2)
+            send_ref[0:cross, at] = v2[:, at] + dot(prolong, values)
         else:
-            base_ref[:, lanes(b, 2)] = v2[0:own_pad, lanes(place2[b], 2)] + dot(prolong_own, values)
-        if b not in ends:
             fold, at = divmod(b - PB, 2 * PB)
             send_ref[cross + fold * MODES : cross + (fold + 1) * MODES, lanes(at, 2)] = values
+
+
+def own_kernel(own_pad, starts, first, deriv, v1_ref, ends_ref, scaled_ref, c2_ref, idx_ref, wt_ref,
+               matrix_ref, base_ref):
+    cells = scaled_ref.shape[1]
+    nblk = cells // LANES
+    groups = list(range(own_pad // 8))
+    ring = list(range(-PB, PB)) + list(range(nblk - PB, nblk + PB))
+    ends = list(range(PB)) + list(range(nblk - PB, nblk))
+    prolong = matrix_of(matrix_ref, starts[3], own_pad, MODES)
+
+    def read(g, b):
+        if b in ring:
+            return v1_ref[rows8(g), lanes(ring.index(b))]
+        return first[rows8(g), lanes(b)]
+
+    for d in range(0, nblk, 2):
+        lifted = dot(prolong, c2_ref[:, lanes(d, 2)])
+        for b in range(d, d + 2):
+            table = (idx_ref, wt_ref, b)
+            bf = coefficient(table)
+            sums = stencil(read, b, table, groups)
+            for g in groups:
+                if b in ends:
+                    turn = ends_ref[rows8(g), lanes(ends.index(b))]
+                else:
+                    turn = deriv[rows8(g), lanes(b)]
+                base_ref[rows8(g), lanes(b)] = (
+                    KEEP * read(g, b)
+                    + scaled_ref[rows8(g), lanes(b)]
+                    - bf * turn
+                    + sums[g]
+                    + lifted[rows8(g), lanes(b - d)]
+                )
 
 
 def final_kernel(count, starts, base_ref, matrix_ref, *refs):
@@ -644,14 +656,14 @@
     def int32(*shape):
         return jax.ShapeDtypeStruct(shape, jnp.int32)
 
-    pack_a, pack_b, initial, scaled, smode, ends, idx, wt, matrices = call(
+    pack_a, pack_b, initial, scaled, smode, ends, m1, m2, idx, wt, matrices = call(
         functools.partial(pack_kernel, own_pad, starts),
         [f32(tiles, 8, LANES), f32(tiles, 8, LANES), wide(own_pad, nblk), wide(own_pad, nblk),
-         wide(MODES, nblk), wide(own_pad, 2 * PB), int32(nblk, 8, LANES), f32(nblk, slots, LANES),
+         wide(MODES, nblk), wide(own_pad, 2 * PB), wide(MODES, nblk - 2 * PB), wide(MODES, nblk - 2 * PB),
+         int32(nblk, 8, LANES), f32(nblk, slots, LANES),
          jax.ShapeDtypeStruct(matrices.shape, matrices.dtype)],
         [scratch(own_pad, nblk), pltpu.VMEM((NEIGH, cells), jnp.int32), vm(NEIGH, cells), vm(1, cells),
-         vm(8, cells), scratch(MODES, nblk), scratch(MODES, nblk - 2 * PB),
-         scratch(MODES, nblk - 2 * PB), scratch(MODES, nblk - 2 * PB), pltpu.SemaphoreType.DMA((8,))],
+         vm(8, cells), scratch(MODES, nblk), scratch(MODES, nblk - 2 * PB), pltpu.SemaphoreType.DMA((8,))],
         2,
         *[
             pltpu.with_memory_space_constraint(x, pltpu.HBM)
@@ -683,21 +695,19 @@
 
     early = [lax.ppermute(share(cross_mid, k), "inst", shift(k)) for k in range(1, inst_count)]
 
-    own_mid, part, cpart, m2, rp = call(
-        functools.partial(inner_kernel, own_pad, rows, starts),
-        [wide(own_pad, nblk - 4 * PB), wide(own_pad, 4 * PB), wide(cross, 2 * PB),
-         wide(MODES, nblk - 4 * PB), wide(MODES, nblk)], [], 3,
-        first, deriv, scaled, smode, cross_mid, idx, wt, matrices,
+    cpart, mpart, m2, rp = call(
+        functools.partial(inner_kernel, own_pad, rows),
+        [wide(cross, 2 * PB), wide(MODES, 2 * PB), wide(MODES, nblk - 2 * PB), wide(MODES, nblk)], [], 3,
+        first, smode, m1, m2, idx, wt,
     )
-    base, send = call(
+    send, v1, dends, c2 = call(
         functools.partial(outer_kernel, own_pad, rows, starts),
-        [wide(own_pad, nblk), wide(cross + folds * MODES, 2 * PB)],
-        [pltpu.VMEM((2, tiles, 8, LANES), jnp.float32), scratch(rows, 4 * PB), scratch(rows, 4 * PB),
-         scratch(rows, 2 * PB), scratch(MODES, nblk + 4 * PB), scratch(MODES, nblk + 4 * PB),
-         scratch(MODES, nblk + 4 * PB), scratch(MODES, nblk + 2 * PB), scratch(MODES, nblk),
+        [wide(cross + folds * MODES, 2 * PB), wide(rows, 4 * PB), wide(rows, 2 * PB), wide(MODES, nblk)],
+        [pltpu.VMEM((2, tiles, 8, LANES), jnp.float32), scratch(cross, 2 * PB),
+         scratch(MODES, nblk + 4 * PB), scratch(MODES, nblk + 4 * PB),
+         scratch(MODES, nblk + 4 * PB), scratch(MODES, nblk + 2 * PB),
          pltpu.VMEM((4 * PB, 8, LANES), jnp.int32), vm(4 * PB, slots, LANES)],
-        8, halo_a, halo_b, initial, scaled, smode, ends, own_mid, cross_mid, part, cpart, first, m2, rp,
-        idx, wt, matrices,
+        8, halo_a, halo_b, initial, smode, ends, cpart, mpart, first, m1, m2, rp, idx, wt, matrices,
     )
 
     def share_late(k):
@@ -706,6 +716,10 @@
         return jnp.concatenate([share(send[:cross], k), send[cross:]], axis=0)
 
     late = [lax.ppermute(share_late(k), "inst", shift(k)) for k in range(1, inst_count)]
+    base = call(
+        functools.partial(own_kernel, own_pad, starts), wide(own_pad, nblk), [], 2,
+        first, deriv, v1, dends, scaled, c2, idx, wt, matrices,
+    )
     received = [r for pair in zip(early, late) for r in pair]
     out = call(
         functools.partial(final_kernel, inst_count - 1, starts), f32(own_pad, cells),

time: 22.6 us -> 22 us (0.973)
  the two profiles are of different devices: /device:TPU:24 before, /device:TPU:19 now
where the time goes in v5:
time: 22 us; the launch traced here: 21.7 us
  Pallas kernels  10.5 us (48%)
  waiting for transfers between devices  6.65 us (30%)
  starting transfers between devices  4.41 us (20%)
    pallas_call x6, Pallas kernels, call(): pl.pallas_call(kernel, out_shape=out_shape, in_specs=[pl.BlockSpec(memory...  10.5 us
    ppermute x1, waiting for transfers between devices, per_device(): lax.ppermute(share_late(k), 'inst', shift(k))  4.08 us
    ppermute x1, starting transfers between devices, per_device(): halo_b = lax.ppermute(pack_b, 'cell', far_pairs)  3.05 us
    ppermute x1, waiting for transfers between devices, per_device(): halo_b = lax.ppermute(pack_b, 'cell', far_pairs)  2.56 us
    ppermute x1, starting transfers between devices, per_device(): halo_a = lax.ppermute(pack_a, 'cell', near_pairs)  0.72 us
  transfers between devices with their start and end apart: 4, of which 2 were waited for; matrix products, arithmetic and copies ran while one was open for 0% of the time, Pallas kernels for 33%

profile of v5, /device:TPU:19, one launch (start us, length us, event | category | flops | bytes accessed | tf_op | source)
XLA Modules:
  0.0 21.7 jit_solution(1945435861219265508)
XLA Ops:
  0.0 2.5 %shard_map.64 = (f32[41,8,128]{2,1,0:T(8,128)S(1)}, f32[41,8,128]{2,1,0:T(8,128)S(1)}, f32[40,2048]{1,0:T(8,128)S(1)}, f32[40,2048]{1,0:T(8,128)S(1)}, f32[16,20...) custom-call(f32[40,2048]{1,0:T(8,128)} %init_hbm.1, ...), custom_call_target="tpu_custom_call" | custom-call | flops 200000000 | bytes 6000000 | tf_op jit(solution)/shard_map/pallas_call | solution.py:620
  2.5 0.7 %collective-permute-start = (f32[41,8,128]{2,1,0:T(8,128)S(1)}, f32[41,8,128]{2,1,0:T(8,128)S(1)}, u32[]{:S(2)}, u32[]{:S(2)}) collective-permute-start(f32[41,8,128]{2,1,0:T(8,128)S(1)} %get-tuple-element.34), channel_id=1, source_target_pairs={{0,2},{2,0},{4,6},{6,4},{8,10},{10,8},{12,14},{14,12},{16,18},{18,... | collective-permute-start | bytes 503816 | tf_op jit(solution)/shard_map/ppermute | solution.py:679
  3.3 3.0 %collective-permute-start.1 = (f32[41,8,128]{2,1,0:T(8,128)S(1)}, f32[41,8,128]{2,1,0:T(8,128)S(1)}, u32[]{:S(2)}, u32[]{:S(2)}) collective-permute-start(f32[41,8,128]{2,1,0:T(8,128)S(1)} %get-tuple-element.35), channel_id=1, source_target_pairs={{2,4},{4,2},{6,8},{8,6},{10,12},{12,10},{14,16},{16,14},{18,20},{2... | collective-permute-start | bytes 503816 | tf_op jit(solution)/shard_map/ppermute | solution.py:678
  6.3 2.0 %shard_map.65 = (f32[40,1536]{1,0:T(8,128)S(1)}, f32[80,2048]{1,0:T(8,128)S(1)}, f32[80,2048]{1,0:T(8,128)S(1)}) custom-call(f32[40,2048]{1,0:T(8,128)S(1)} %get-tuple-element.27.init_ref, f32[40,2048]{1,0:T(8,128)S(1)} %get-tuple-element.28.scaled_ref, s32[16,8,128]{2,1,0:T(8,128)S(1)} %get-tuple-element.29.idx_ref.idx_in, ...), custom_call_target="tpu_custom_call" | custom-call | flops 300000000 | bytes 9000000 | tf_op jit(solution)/shard_map/pallas_call | solution.py:620
  8.3 0.3 %collective-permute-start.2 = (f32[40,1536]{1,0:T(8,128)S(1)}, f32[40,1536]{1,0:T(8,128)S(1)}, u32[]{:S(2)}, u32[]{:S(2)}) collective-permute-start(f32[40,1536]{1,0:T(8,128)S(1)} %get-tuple-element.47), channel_id=1, source_target_pairs={{0,1},{1,0},{2,3},{3,2},{4,5},{5,4},{6,7},{7,6},{8,9},{9,8},{10,11... | collective-permute-start | bytes 737288 | tf_op jit(solution)/shard_map/ppermute | solution.py:696
  8.6 0.8 %shard_map.66 = (f32[40,512]{1,0:T(8,128)S(1)}, f32[16,512]{1,0:T(8,128)S(1)}, f32[16,1536]{1,0:T(8,128)S(1)}, f32[16,2048]{1,0:T(8,128)S(1)}) custom-call(f32[80,2048]{1,0:T(8,128)S(1)} %get-tuple-element.32.first.first_ref, f32[16,2048]{1,0:T(8,128)S(1)} %get-tuple-element.36.smode_ref, f32[16,1536]{1,0:T(8,128)S(1)} %get-tuple-element.38.m1_ref.m1i_ref, ...), custom_call_target="tpu_custom_call" | custom-call | flops 300000000 | bytes 9000000 | tf_op jit(solution)/shard_map/pallas_call | solution.py:620
  9.5 0.0 collective-permute-done.a_ref
  9.5 2.6 %collective-permute-done.1.b_ref = f32[41,8,128]{2,1,0:T(8,128)S(1)} collective-permute-done((f32[41,8,128]{2,1,0:T(8,128)S(1)}, f32[41,8,128]{2,1,0:T(8,128)S(1)}, u32[]{:S(2)}, u32[]{:S(2)}) %collective-permute-start.1) | collective-permute-done | bytes 167968 | tf_op jit(solution)/shard_map/ppermute | solution.py:678
  12.0 3.0 %shard_map.67 = (f32[88,512]{1,0:T(8,128)S(1)}, f32[80,1024]{1,0:T(8,128)S(1)}, f32[80,512]{1,0:T(8,128)S(1)}, f32[16,2048]{1,0:T(8,128)S(1)}) custom-call(f32[41,8,128]{2,1,0:T(8,128)S(1)} %collective-permute-done.a_ref, f32[41,8,128]{2,1,0:T(8,128)S(1)} %collective-permute-done.1.b_ref, f32[40,2048]{1,0:T(8,128)S(1)} %get-tuple-element.27.init_ref, ...), custom_call_target="tpu_custom_call" | custom-call | flops 800000000 | bytes 24000000 | tf_op jit(solution)/shard_map/pallas_call | solution.py:620
  15.0 0.3 %collective-permute-start.3 = (f32[88,512]{1,0:T(8,128)S(1)}, f32[88,512]{1,0:T(8,128)S(1)}, u32[]{:S(2)}, u32[]{:S(2)}) collective-permute-start(f32[88,512]{1,0:T(8,128)S(1)} %get-tuple-element.48), channel_id=1, source_target_pairs={{0,1},{1,0},{2,3},{3,2},{4,5},{5,4},{6,7},{7,6},{8,9},{9,8},{10,11... | collective-permute-start | bytes 540680 | tf_op jit(solution)/shard_map/ppermute | solution.py:718
  15.4 1.3 %shard_map.68.base_ref = f32[40,2048]{1,0:T(8,128)S(1)} custom-call(f32[80,2048]{1,0:T(8,128)S(1)} %get-tuple-element.32.first.first_ref, f32[80,2048]{1,0:T(8,128)S(1)} %get-tuple-element.33.deriv, f32[80,1024]{1,0:T(8,128)S(1)} %get-tuple-element.44.v1_ref, f32[80,512]{1,0:T(8,128)S(1)} %get-tuple-element.45.ends_ref, ...), custom_call_target="tpu_custom_call" | custom-call | flops 200000000 | bytes 6000000 | tf_op jit(solution)/shard_map/pallas_call | solution.py:620
  16.7 0.0 collective-permute-done.2.refs_0_
  16.7 4.1 %collective-permute-done.3.refs_1_ = f32[88,512]{1,0:T(8,128)S(1)} collective-permute-done((f32[88,512]{1,0:T(8,128)S(1)}, f32[88,512]{1,0:T(8,128)S(1)}, u32[]{:S(2)}, u32[]{:S(2)}) %collective-permute-start.3) | collective-permute-done | bytes 180256 | tf_op jit(solution)/shard_map/ppermute | solution.py:718
  20.8 0.9 %shard_map.69 = f32[40,2048]{1,0:T(8,128)} custom-call(f32[40,2048]{1,0:T(8,128)S(1)} %shard_map.68.base_ref, bf16[320,256]{1,0:T(8,128)(2,1)S(1)} %get-tuple-element.31.matrix_ref, f32[40,1536]{1,0:T(8,128)S(1)} %collective-permute-done.2.refs_0_, f32[88,512]{1,0:T(8,128)S(1)} %collective-permute-done.3.refs_1_), custom_call_target="tpu_custom_call" | custom-call | flops 100000000 | bytes 3000000 | tf_op jit(solution)/shard_map/pallas_call | solution.py:620
Async XLA Ops:
  2.5 6.9 %collective-permute-start = (f32[41,8,128]{2,1,0:T(8,128)S(1)}, f32[41,8,128]{2,1,0:T(8,128)S(1)}, u32[]{:S(2)}, u32[]{:S(2)}) collective-permute-start(f32[41,8,128]{2,1,0:T(8,128)S(1)} %get-tuple-element.34), channel_id=1, source_target_pairs={{0,2},{2,0},{4,6},{6,4},{8,10},{10,8},{12,14},{14,12},{16,18},{18,... | collective-permute-start | bytes 503816 | tf_op jit(solution)/shard_map/ppermute | solution.py:679
  3.3 8.8 %collective-permute-start.1 = (f32[41,8,128]{2,1,0:T(8,128)S(1)}, f32[41,8,128]{2,1,0:T(8,128)S(1)}, u32[]{:S(2)}, u32[]{:S(2)}) collective-permute-start(f32[41,8,128]{2,1,0:T(8,128)S(1)} %get-tuple-element.35), channel_id=1, source_target_pairs={{2,4},{4,2},{6,8},{8,6},{10,12},{12,10},{14,16},{16,14},{18,20},{2... | collective-permute-start | bytes 503816 | tf_op jit(solution)/shard_map/ppermute | solution.py:678
  8.3 8.4 %collective-permute-start.2 = (f32[40,1536]{1,0:T(8,128)S(1)}, f32[40,1536]{1,0:T(8,128)S(1)}, u32[]{:S(2)}, u32[]{:S(2)}) collective-permute-start(f32[40,1536]{1,0:T(8,128)S(1)} %get-tuple-element.47), channel_id=1, source_target_pairs={{0,1},{1,0},{2,3},{3,2},{4,5},{5,4},{6,7},{7,6},{8,9},{9,8},{10,11... | collective-permute-start | bytes 737288 | tf_op jit(solution)/shard_map/ppermute | solution.py:696
  15.0 5.7 %collective-permute-start.3 = (f32[88,512]{1,0:T(8,128)S(1)}, f32[88,512]{1,0:T(8,128)S(1)}, u32[]{:S(2)}, u32[]{:S(2)}) collective-permute-start(f32[88,512]{1,0:T(8,128)S(1)} %get-tuple-element.48), channel_id=1, source_target_pairs={{0,1},{1,0},{2,3},{3,2},{4,5},{5,4},{6,7},{7,6},{8,9},{9,8},{10,11... | collective-permute-start | bytes 540680 | tf_op jit(solution)/shard_map/ppermute | solution.py:718

commit v6 on v5

--- a/solution.py
+++ b/solution.py
@@ -108,19 +108,31 @@
     slot = lax.broadcasted_iota(jnp.int32, near.shape, 0)
     base = (target >> 7) + jnp.where((slot & 1) == 0, PB, 0)
     idx_ref[at, 0:NEIGH, :] = target & (LANES - 1)
+    idx_ref[at, NEIGH : 2 * NEIGH, :] = target & (LANES - 1)
     for j in range(PB + 1):
         wt_ref[at, NEIGH * j : NEIGH * (j + 1), :] = jnp.where(base == j, bw, 0.0)
     wt_ref[at, NEIGH * (PB + 1) : NEIGH * (PB + 1) + 1, :] = bf
 
 
+def build_product(ut_ref, at, table, block, coefs):
+    idx_ref, wt_ref, to = table
+    even = (lax.broadcasted_iota(jnp.int32, (8, LANES), 0) & 1) == 0
+    for j in range(PB + 1):
+        low = jnp.broadcast_to(coefs(block + j - PB), (8, LANES))
+        high = jnp.broadcast_to(coefs(block + j), (8, LANES))
+        taken = jnp.take_along_axis(jnp.where(even, low, high), idx_ref[to], axis=1)
+        part = slice(NEIGH * j, NEIGH * (j + 1))
+        ut_ref[at, part, :] = wt_ref[to, part, :] * taken[0:NEIGH]
+
+
 def coefficient(table):
     _, wt_ref, at = table
     return wt_ref[at, pl.ds(NEIGH * (PB + 1), 8, stride=0), :]
 
 
-def stencil(read, block, table, groups, known=None):
+def stencil(read, block, table, groups, known=None, product=None):
     idx_ref, wt_ref, at = table
-    sums, cache = [None] * len(groups), {}
+    sums, others, cache = [0.0] * len(groups), [0.0] * len(groups), {}
 
     def source(g, b):
         if (g, b) not in cache:
@@ -135,11 +147,16 @@
                 continue
             if index is None:
                 index = idx_ref[at, pl.ds(k, 8, stride=0), :]
-            weight = wt_ref[at, pl.ds(NEIGH * j + k, 8, stride=0), :]
+            row = pl.ds(NEIGH * j + k, 8, stride=0)
+            weight = wt_ref[at, row, :]
+            if product is not None:
+                other = product[0][product[1], row, :]
             for i, g in enumerate(groups):
-                term = weight * jnp.take_along_axis(source(g, b), index, axis=1)
-                sums[i] = term if sums[i] is None else sums[i] + term
-    return [0.0 if total is None else total for total in sums]
+                taken = jnp.take_along_axis(source(g, b), index, axis=1)
+                sums[i] = sums[i] + weight * taken
+                if product is not None:
+                    others[i] = others[i] + other * taken
+    return sums if product is None else (sums, others)
 
 
 def turned(values, table, keep):
@@ -165,8 +182,8 @@
 
 
 def pack_kernel(own_pad, starts, init_hbm, src_hbm, near_hbm, face_hbm, damp_hbm, matrix_hbm,
-                a_ref, b_ref, init_ref, scaled_ref, mode_ref, edge_ref, m1, m2, idx_ref, wt_ref, matrix_ref,
-                src_ref, near_ref, face_ref, damp_ref, coef_ref, m0, rp, sems):
+                a_ref, b_ref, init_ref, scaled_ref, mode_ref, edge_ref, push_ref, m1, m2, idx_ref, wt_ref, matrix_ref,
+                src_ref, near_ref, face_ref, damp_ref, coef_ref, m0, rp, ut, sems):
     cells = init_ref.shape[1]
     nblk = cells // LANES
     half = own_pad // 16 * 8
@@ -214,9 +231,20 @@
         deriv = dot(derive, init_ref[:, lanes(at, PB)])
         for i in NEAR:
             b = at + i
-            sums = stencil(reader(init_ref), b, table(b), groups, lambda s: 0 <= s < nblk)
+            at2 = side * PB + i
+
+            def coefs(s):
+                if not 0 <= s < nblk:
+                    return jnp.zeros((1, LANES), jnp.float32)
+                return coef_ref[NEIGH : NEIGH + 1, lanes(s)]
+
+            build_product(ut, at2, table(b), b, coefs)
+            sums, pushes = stencil(
+                reader(init_ref), b, table(b), groups, lambda s: 0 <= s < nblk, (ut, at2)
+            )
             bf = coefficient(table(b))
             for g in groups:
+                push_ref[rows8(g), lanes(at2)] = pushes[g]
                 edge_ref[rows8(g), lanes(side * PB + i)] = (
                     KEEP * init_ref[rows8(g), lanes(b)]
                     + scaled_ref[rows8(g), lanes(b)]
@@ -281,7 +309,7 @@
 
 
 def cross_kernel(own_pad, rows, starts, init_ref, scaled_ref, idx_ref, wt_ref, matrix_ref,
-                 cross_ref, first, deriv):
+                 cross_ref, first, deriv, push, ut):
     cells = init_ref.shape[1]
     nblk = cells // LANES
     own_groups = list(range(own_pad // 8))
@@ -301,13 +329,19 @@
         return first[rows8(g), lanes(b)]
 
     inside = range(PB, nblk - PB)
+
+    def coefs(s):
+        return wt_ref[s, NEIGH * (PB + 1) : NEIGH * (PB + 1) + 1, :]
+
     for b in range(nblk):
         bf = coefficient(table(b))
         for g in cross_groups:
             first[rows8(g), lanes(b)] = -bf * deriv[rows8(g), lanes(b)]
         if b in inside:
-            sums = stencil(read_init, b, table(b), own_groups)
+            build_product(ut, b - PB, table(b), b, coefs)
+            sums, pushes = stencil(read_init, b, table(b), own_groups, None, (ut, b - PB))
             for g in own_groups:
+                push[rows8(g), lanes(b - PB)] = pushes[g]
                 first[rows8(g), lanes(b)] = (
                     KEEP * init_ref[rows8(g), lanes(b)]
                     + scaled_ref[rows8(g), lanes(b)]
@@ -315,31 +349,28 @@
                     + sums[g]
                 )
     derive = matrix_of(matrix_ref, starts[1], rows, rows)
+    couple = matrix_of(matrix_ref, starts[0] + own_pad, rows - own_pad, own_pad)
     for d in range(PB, nblk - PB, 2):
         deriv[:, lanes(d, 2)] = dot(derive, first[:, lanes(d, 2)])
-    for b in inside:
-        sums = stencil(read_first, b, table(b), cross_groups)
-        bf = coefficient(table(b))
-        for g, total in zip(cross_groups, sums):
-            cross_ref[rows8(g - len(own_groups)), lanes(b - PB)] = (
-                KEEP * read_first(g, b) - bf * deriv[rows8(g), lanes(b)] + total
-            )
-
-
-def inner_kernel(own_pad, rows, first, smode_ref, m1_ref, m2_ref, idx_ref, wt_ref,
-                 cpart_ref, mpart_ref, m2_out, rp_ref):
+        turn = dot(couple, push[:, lanes(d - PB, 2)])
+        for b in range(d, d + 2):
+            bf = coefficient(table(b))
+            for g in cross_groups:
+                part = rows8(g - len(own_groups))
+                cross_ref[part, lanes(b - PB)] = (
+                    KEEP * read_first(g, b) - bf * deriv[rows8(g), lanes(b)] - turn[part, lanes(b - d)]
+                )
+
+
+def inner_kernel(smode_ref, m1_ref, m2_ref, idx_ref, wt_ref, mpart_ref, m2_out, rp_ref):
     cells = smode_ref.shape[1]
     nblk = cells // LANES
-    cross_groups = list(range(own_pad // 8, rows // 8))
     inside = range(PB, nblk - PB)
     middle = range(2 * PB, nblk - 2 * PB)
     ends = list(range(PB)) + list(range(nblk - PB, nblk))
 
     def table(b):
         return idx_ref, wt_ref, b
-
-    def read_first(g, b):
-        return first[rows8(g), lanes(b)]
 
     def read_m1(g, b):
         return m1_ref[rows8(g), lanes(b - PB)]
@@ -357,10 +388,6 @@
         sums = stencil(read_m1, b, table(b), MODE_GROUPS, lambda s: s in inside)
         for g in MODE_GROUPS:
             mpart_ref[rows8(g), lanes(i)] = sums[g] + smode_ref[rows8(g), lanes(b)]
-    for i, b in enumerate(ends):
-        sums = stencil(read_first, b, table(b), cross_groups, lambda s: 0 <= s < nblk)
-        for g, total in zip(cross_groups, sums):
-            cpart_ref[rows8(g - own_pad // 8), lanes(i)] = total
     for b in range(nblk):
         sums = stencil(read_m2, b, table(b), MODE_GROUPS, lambda s: s in middle)
         if b in middle:
@@ -371,9 +398,9 @@
 
 
 def outer_kernel(own_pad, rows, starts, a_ref, b_ref, init_ref, smode_ref, edge_ref,
-                 cpart_ref, mpart_ref, first_ref, m1i_ref, m2i_ref, rp_ref, idx_in, wt_in,
+                 push_ref, mpart_ref, first_ref, m1i_ref, m2i_ref, rp_ref, idx_in, wt_in,
                  matrix_ref, send_ref, v1, deriv, c2x,
-                 halo, v2, m1x, m2x, rx, c1x, idx, wt):
+                 halo, v2, push, m1x, m2x, rx, c1x, idx, wt, ut):
     cells = init_ref.shape[1]
     nblk = cells // LANES
     lead = own_pad // 8
@@ -424,6 +451,12 @@
 
     def read_v1(g, b):
         return v1[rows8(g), lanes(place[b])]
+
+    def coefs(b):
+        if own(b):
+            return jnp.zeros((1, LANES), jnp.float32)
+        side, i = side_of(b)
+        return halo[side, tiles[7], i : i + 1, :]
 
     derive_cross = matrix_of(matrix_ref, starts[0], rows, own_pad)
     for side in range(2):
@@ -447,8 +480,12 @@
         for i in range(PB):
             b = nblk - PB + i if side else i
             at = lanes(side * PB + i)
-            sums = stencil(read_init, b, table(b), own_groups, lambda s: not own(s))
+            build_product(ut, side * PB + i, table(b), b, coefs)
+            sums, pushes = stencil(
+                read_init, b, table(b), own_groups, lambda s: not own(s), (ut, side * PB + i)
+            )
             for g in own_groups:
+                push[rows8(g), at] = push_ref[rows8(g), at] + pushes[g]
                 v1[rows8(g), lanes(place[b])] = edge_ref[rows8(g), at] + sums[g]
             for g in cross_groups:
                 v1[rows8(g), lanes(place[b])] = first_ref[rows8(g), lanes(b)]
@@ -468,13 +505,15 @@
             m1x[rows8(g), lanes(b - low)] = section(3, g, b, True)
 
     ends = list(range(PB)) + list(range(nblk - PB, nblk))
-    for i, b in enumerate(ends):
-        at = lanes(i)
-        sums = stencil(read_v1, b, table(b), cross_groups, lambda s: not own(s))
-        bf = coefficient(table(b))
-        for g, total in zip(cross_groups, sums):
-            part = rows8(g - lead)
-            v2[part, at] = cpart_ref[part, at] + total + KEEP * read_v1(g, b) - bf * deriv[rows8(g), at]
+    couple = matrix_of(matrix_ref, starts[0] + own_pad, rows - own_pad, own_pad)
+    for side in range(2):
+        turn = dot(couple, push[:, lanes(side * PB, PB)])
+        for i in range(PB):
+            b, at = ends[side * PB + i], lanes(side * PB + i)
+            bf = coefficient(table(b))
+            for g in cross_groups:
+                part = rows8(g - lead)
+                v2[part, at] = KEEP * read_v1(g, b) - bf * deriv[rows8(g), at] - turn[part, lanes(i)]
 
     def reader(ref, first):
         return lambda g, b: ref[rows8(g), lanes(b - first)]
@@ -656,14 +695,16 @@
     def int32(*shape):
         return jax.ShapeDtypeStruct(shape, jnp.int32)
 
-    pack_a, pack_b, initial, scaled, smode, ends, m1, m2, idx, wt, matrices = call(
+    pack_a, pack_b, initial, scaled, smode, ends, push, m1, m2, idx, wt, matrices = call(
         functools.partial(pack_kernel, own_pad, starts),
         [f32(tiles, 8, LANES), f32(tiles, 8, LANES), wide(own_pad, nblk), wide(own_pad, nblk),
-         wide(MODES, nblk), wide(own_pad, 2 * PB), wide(MODES, nblk - 2 * PB), wide(MODES, nblk - 2 * PB),
+         wide(MODES, nblk), wide(own_pad, 2 * PB), wide(own_pad, 2 * PB), wide(MODES, nblk - 2 * PB),
+         wide(MODES, nblk - 2 * PB),
          int32(nblk, 8, LANES), f32(nblk, slots, LANES),
          jax.ShapeDtypeStruct(matrices.shape, matrices.dtype)],
         [scratch(own_pad, nblk), pltpu.VMEM((NEIGH, cells), jnp.int32), vm(NEIGH, cells), vm(1, cells),
-         vm(8, cells), scratch(MODES, nblk), scratch(MODES, nblk - 2 * PB), pltpu.SemaphoreType.DMA((8,))],
+         vm(8, cells), scratch(MODES, nblk), scratch(MODES, nblk - 2 * PB), vm(2 * PB, slots, LANES),
+         pltpu.SemaphoreType.DMA((8,))],
         2,
         *[
             pltpu.with_memory_space_constraint(x, pltpu.HBM)
@@ -680,7 +721,8 @@
 
     cross_mid, first, deriv = call(
         functools.partial(cross_kernel, own_pad, rows, starts),
-        [wide(cross, nblk - 2 * PB), wide(rows, nblk), wide(rows, nblk)], [], 3,
+        [wide(cross, nblk - 2 * PB), wide(rows, nblk), wide(rows, nblk)],
+        [scratch(own_pad, nblk - 2 * PB), vm(nblk - 2 * PB, slots, LANES)], 3,
         initial, scaled, idx, wt, matrices,
     )
 
@@ -695,19 +737,19 @@
 
     early = [lax.ppermute(share(cross_mid, k), "inst", shift(k)) for k in range(1, inst_count)]
 
-    cpart, mpart, m2, rp = call(
-        functools.partial(inner_kernel, own_pad, rows),
-        [wide(cross, 2 * PB), wide(MODES, 2 * PB), wide(MODES, nblk - 2 * PB), wide(MODES, nblk)], [], 3,
-        first, smode, m1, m2, idx, wt,
+    mpart, m2, rp = call(
+        inner_kernel,
+        [wide(MODES, 2 * PB), wide(MODES, nblk - 2 * PB), wide(MODES, nblk)], [], 3,
+        smode, m1, m2, idx, wt,
     )
     send, v1, dends, c2 = call(
         functools.partial(outer_kernel, own_pad, rows, starts),
         [wide(cross + folds * MODES, 2 * PB), wide(rows, 4 * PB), wide(rows, 2 * PB), wide(MODES, nblk)],
         [pltpu.VMEM((2, tiles, 8, LANES), jnp.float32), scratch(cross, 2 * PB),
-         scratch(MODES, nblk + 4 * PB), scratch(MODES, nblk + 4 * PB),
+         scratch(own_pad, 2 * PB), scratch(MODES, nblk + 4 * PB), scratch(MODES, nblk + 4 * PB),
          scratch(MODES, nblk + 4 * PB), scratch(MODES, nblk + 2 * PB),
-         pltpu.VMEM((4 * PB, 8, LANES), jnp.int32), vm(4 * PB, slots, LANES)],
-        8, halo_a, halo_b, initial, smode, ends, cpart, mpart, first, m1, m2, rp, idx, wt, matrices,
+         pltpu.VMEM((4 * PB, 8, LANES), jnp.int32), vm(4 * PB, slots, LANES), vm(2 * PB, slots, LANES)],
+        8, halo_a, halo_b, initial, smode, ends, push, mpart, first, m1, m2, rp, idx, wt, matrices,
     )
 
     def share_late(k):

time: 22 us -> 21.8 us (level)
  waiting for transfers between devices: 6.65 us -> 7.38 us
  Pallas kernels: 10.5 us -> 9.89 us
    ppermute x1, waiting for transfers between devices: 2.56 us -> 3.29 us  [per_device(): halo_b = lax.ppermute(pack_b, 'cell', far_pairs)]
    pallas_call x6, Pallas kernels: 10.5 us -> 9.89 us  [call(): pl.pallas_call(kernel, out_shape=out_shape, in_specs=[pl.BlockSpec(memory...]
  transfers between devices with their start and end apart: 4 -> 4, of which waited for: 2 -> 2; matrix products, arithmetic and copies ran while one was open for 0% -> 0% of each run, Pallas kernels for 33% -> 30%
where the time goes in v6:
time: 21.8 us; the launch traced here: 21.7 us
  Pallas kernels  9.89 us (45%)
  waiting for transfers between devices  7.38 us (34%)
  starting transfers between devices  4.35 us (20%)
    pallas_call x6, Pallas kernels, call(): pl.pallas_call(kernel, out_shape=out_shape, in_specs=[pl.BlockSpec(memory...  9.89 us
    ppermute x1, waiting for transfers between devices, per_device(): lax.ppermute(share_late(k), 'inst', shift(k))  4.08 us
    ppermute x1, waiting for transfers between devices, per_device(): halo_b = lax.ppermute(pack_b, 'cell', far_pairs)  3.29 us
    ppermute x1, starting transfers between devices, per_device(): halo_b = lax.ppermute(pack_b, 'cell', far_pairs)  3.05 us
    ppermute x1, starting transfers between devices, per_device(): halo_a = lax.ppermute(pack_a, 'cell', near_pairs)  0.72 us
  transfers between devices with their start and end apart: 4, of which 2 were waited for; matrix products, arithmetic and copies ran while one was open for 0% of the time, Pallas kernels for 30%

profile of v6, /device:TPU:19, one launch (start us, length us, event | category | flops | bytes accessed | tf_op | source)
XLA Modules:
  0.0 21.7 jit_solution(7750796334215874332)
XLA Ops:
  0.0 2.6 %shard_map.64 = (f32[41,8,128]{2,1,0:T(8,128)S(1)}, f32[41,8,128]{2,1,0:T(8,128)S(1)}, f32[40,2048]{1,0:T(8,128)S(1)}, f32[40,2048]{1,0:T(8,128)S(1)}, f32[16,20...) custom-call(f32[40,2048]{1,0:T(8,128)} %init_hbm.1, ...), custom_call_target="tpu_custom_call" | custom-call | flops 200000000 | bytes 6000000 | tf_op jit(solution)/shard_map/pallas_call | solution.py:659
  2.6 0.7 %collective-permute-start = (f32[41,8,128]{2,1,0:T(8,128)S(1)}, f32[41,8,128]{2,1,0:T(8,128)S(1)}, u32[]{:S(2)}, u32[]{:S(2)}) collective-permute-start(f32[41,8,128]{2,1,0:T(8,128)S(1)} %get-tuple-element.34), channel_id=1, source_target_pairs={{0,2},{2,0},{4,6},{6,4},{8,10},{10,8},{12,14},{14,12},{16,18},{18,... | collective-permute-start | bytes 503816 | tf_op jit(solution)/shard_map/ppermute | solution.py:720
  3.3 3.0 %collective-permute-start.1 = (f32[41,8,128]{2,1,0:T(8,128)S(1)}, f32[41,8,128]{2,1,0:T(8,128)S(1)}, u32[]{:S(2)}, u32[]{:S(2)}) collective-permute-start(f32[41,8,128]{2,1,0:T(8,128)S(1)} %get-tuple-element.35), channel_id=1, source_target_pairs={{2,4},{4,2},{6,8},{8,6},{10,12},{12,10},{14,16},{16,14},{18,20},{2... | collective-permute-start | bytes 503816 | tf_op jit(solution)/shard_map/ppermute | solution.py:719
  6.4 1.5 %shard_map.65 = (f32[40,1536]{1,0:T(8,128)S(1)}, f32[80,2048]{1,0:T(8,128)S(1)}, f32[80,2048]{1,0:T(8,128)S(1)}) custom-call(f32[40,2048]{1,0:T(8,128)S(1)} %get-tuple-element.27.init_ref, f32[40,2048]{1,0:T(8,128)S(1)} %get-tuple-element.28.scaled_ref, s32[16,8,128]{2,1,0:T(8,128)S(1)} %get-tuple-element.29.idx_ref.idx_in, ...), custom_call_target="tpu_custom_call" | custom-call | flops 300000000 | bytes 9000000 | tf_op jit(solution)/shard_map/pallas_call | solution.py:659
  7.8 0.3 %collective-permute-start.2 = (f32[40,1536]{1,0:T(8,128)S(1)}, f32[40,1536]{1,0:T(8,128)S(1)}, u32[]{:S(2)}, u32[]{:S(2)}) collective-permute-start(f32[40,1536]{1,0:T(8,128)S(1)} %get-tuple-element.47), channel_id=1, source_target_pairs={{0,1},{1,0},{2,3},{3,2},{4,5},{5,4},{6,7},{7,6},{8,9},{9,8},{10,11... | collective-permute-start | bytes 737288 | tf_op jit(solution)/shard_map/ppermute | solution.py:738
  8.2 0.6 %shard_map.66 = (f32[16,512]{1,0:T(8,128)S(1)}, f32[16,1536]{1,0:T(8,128)S(1)}, f32[16,2048]{1,0:T(8,128)S(1)}) custom-call(f32[16,2048]{1,0:T(8,128)S(1)} %get-tuple-element.36.smode_ref, f32[16,1536]{1,0:T(8,128)S(1)} %get-tuple-element.39.m1_ref.m1i_ref, f32[16,1536]{1,0:T(8,128)S(1)} %get-tuple-element.40.m2_ref, ...), custom_call_target="tpu_custom_call" | custom-call | flops 300000000 | bytes 9000000 | tf_op jit(solution)/shard_map/pallas_call | solution.py:659
  8.8 0.0 collective-permute-done.a_ref
  8.8 3.3 %collective-permute-done.1.b_ref = f32[41,8,128]{2,1,0:T(8,128)S(1)} collective-permute-done((f32[41,8,128]{2,1,0:T(8,128)S(1)}, f32[41,8,128]{2,1,0:T(8,128)S(1)}, u32[]{:S(2)}, u32[]{:S(2)}) %collective-permute-start.1) | collective-permute-done | bytes 167968 | tf_op jit(solution)/shard_map/ppermute | solution.py:719
  12.1 3.0 %shard_map.67 = (f32[88,512]{1,0:T(8,128)S(1)}, f32[80,1024]{1,0:T(8,128)S(1)}, f32[80,512]{1,0:T(8,128)S(1)}, f32[16,2048]{1,0:T(8,128)S(1)}) custom-call(f32[41,8,128]{2,1,0:T(8,128)S(1)} %collective-permute-done.a_ref, f32[41,8,128]{2,1,0:T(8,128)S(1)} %collective-permute-done.1.b_ref, f32[40,2048]{1,0:T(8,128)S(1)} %get-tuple-element.27.init_ref, ...), custom_call_target="tpu_custom_call" | custom-call | flops 800000000 | bytes 24000000 | tf_op jit(solution)/shard_map/pallas_call | solution.py:659
  15.1 0.3 %collective-permute-start.3 = (f32[88,512]{1,0:T(8,128)S(1)}, f32[88,512]{1,0:T(8,128)S(1)}, u32[]{:S(2)}, u32[]{:S(2)}) collective-permute-start(f32[88,512]{1,0:T(8,128)S(1)} %get-tuple-element.48), channel_id=1, source_target_pairs={{0,1},{1,0},{2,3},{3,2},{4,5},{5,4},{6,7},{7,6},{8,9},{9,8},{10,11... | collective-permute-start | bytes 540680 | tf_op jit(solution)/shard_map/ppermute | solution.py:760
  15.4 1.3 %shard_map.68.base_ref = f32[40,2048]{1,0:T(8,128)S(1)} custom-call(f32[80,2048]{1,0:T(8,128)S(1)} %get-tuple-element.32.first_ref.first, f32[80,2048]{1,0:T(8,128)S(1)} %get-tuple-element.33.deriv, f32[80,1024]{1,0:T(8,128)S(1)} %get-tuple-element.44.v1_ref, f32[80,512]{1,0:T(8,128)S(1)} %get-tuple-element.45.ends_ref, ...), custom_call_target="tpu_custom_call" | custom-call | flops 200000000 | bytes 6000000 | tf_op jit(solution)/shard_map/pallas_call | solution.py:659
  16.7 0.0 collective-permute-done.2.refs_0_
  16.7 4.1 %collective-permute-done.3.refs_1_ = f32[88,512]{1,0:T(8,128)S(1)} collective-permute-done((f32[88,512]{1,0:T(8,128)S(1)}, f32[88,512]{1,0:T(8,128)S(1)}, u32[]{:S(2)}, u32[]{:S(2)}) %collective-permute-start.3) | collective-permute-done | bytes 180256 | tf_op jit(solution)/shard_map/ppermute | solution.py:760
  20.8 0.9 %shard_map.69 = f32[40,2048]{1,0:T(8,128)} custom-call(f32[40,2048]{1,0:T(8,128)S(1)} %shard_map.68.base_ref, bf16[320,256]{1,0:T(8,128)(2,1)S(1)} %get-tuple-element.31.matrix_ref, f32[40,1536]{1,0:T(8,128)S(1)} %collective-permute-done.2.refs_0_, f32[88,512]{1,0:T(8,128)S(1)} %collective-permute-done.3.refs_1_), custom_call_target="tpu_custom_call" | custom-call | flops 100000000 | bytes 3000000 | tf_op jit(solution)/shard_map/pallas_call | solution.py:659
Async XLA Ops:
  2.6 6.2 %collective-permute-start = (f32[41,8,128]{2,1,0:T(8,128)S(1)}, f32[41,8,128]{2,1,0:T(8,128)S(1)}, u32[]{:S(2)}, u32[]{:S(2)}) collective-permute-start(f32[41,8,128]{2,1,0:T(8,128)S(1)} %get-tuple-element.34), channel_id=1, source_target_pairs={{0,2},{2,0},{4,6},{6,4},{8,10},{10,8},{12,14},{14,12},{16,18},{18,... | collective-permute-start | bytes 503816 | tf_op jit(solution)/shard_map/ppermute | solution.py:720
  3.3 8.8 %collective-permute-start.1 = (f32[41,8,128]{2,1,0:T(8,128)S(1)}, f32[41,8,128]{2,1,0:T(8,128)S(1)}, u32[]{:S(2)}, u32[]{:S(2)}) collective-permute-start(f32[41,8,128]{2,1,0:T(8,128)S(1)} %get-tuple-element.35), channel_id=1, source_target_pairs={{2,4},{4,2},{6,8},{8,6},{10,12},{12,10},{14,16},{16,14},{18,20},{2... | collective-permute-start | bytes 503816 | tf_op jit(solution)/shard_map/ppermute | solution.py:719
  7.8 8.8 %collective-permute-start.2 = (f32[40,1536]{1,0:T(8,128)S(1)}, f32[40,1536]{1,0:T(8,128)S(1)}, u32[]{:S(2)}, u32[]{:S(2)}) collective-permute-start(f32[40,1536]{1,0:T(8,128)S(1)} %get-tuple-element.47), channel_id=1, source_target_pairs={{0,1},{1,0},{2,3},{3,2},{4,5},{5,4},{6,7},{7,6},{8,9},{9,8},{10,11... | collective-permute-start | bytes 737288 | tf_op jit(solution)/shard_map/ppermute | solution.py:738
  15.1 5.7 %collective-permute-start.3 = (f32[88,512]{1,0:T(8,128)S(1)}, f32[88,512]{1,0:T(8,128)S(1)}, u32[]{:S(2)}, u32[]{:S(2)}) collective-permute-start(f32[88,512]{1,0:T(8,128)S(1)} %get-tuple-element.48), channel_id=1, source_target_pairs={{0,1},{1,0},{2,3},{3,2},{4,5},{5,4},{6,7},{7,6},{8,9},{9,8},{10,11... | collective-permute-start | bytes 540680 | tf_op jit(solution)/shard_map/ppermute | solution.py:760

commit v7 on v6

--- a/solution.py
+++ b/solution.py
@@ -73,17 +73,23 @@
         lift = np.zeros((own_pad, MODES))
         lift[:own] = other[(k - 1) * own : k * own]
         lifts.append(lift)
-    parts = [derive[:, :own_pad], np.concatenate([derive, restrict]), restrict[:, :own_pad], prolong]
-    parts += lifts
-    width = -(-3 * count // LANES) * LANES
+    early = [derive[:, :own_pad], restrict[:, :own_pad]]
+    late = [np.concatenate([derive, restrict]), prolong] + lifts
+    (lead, lead_starts), (rest, rest_starts) = stack(early), stack(late)
+    starts = [lead_starts[0], rest_starts[0], lead_starts[1]] + rest_starts[1:]
+    return lead, rest, starts, count
+
+
+def stack(parts):
+    wides = [split_matrix(part) for part in parts]
+    width = -(-max(wide.shape[1] for wide in wides) // LANES) * LANES
     blocks, starts, at = [], [], 0
-    for part in parts:
-        wide = split_matrix(part)
+    for wide in wides:
         height = -(-wide.shape[0] // 16) * 16
         blocks.append(np.pad(wide, ((0, height - wide.shape[0]), (0, width - wide.shape[1]))))
         starts.append(at)
         at += height
-    return np.concatenate(blocks), starts, count
+    return np.concatenate(blocks), starts
 
 
 def split3(values):
@@ -171,7 +177,6 @@
 
 
 MODE_GROUPS = list(range(MODES // 8))
-NEAR, FAR, DEEP = range(PB), range(PB, 2 * PB), range(2 * PB, 3 * PB)
 
 
 def halo_layout(own_pad):
@@ -181,8 +186,9 @@
     return starts, sum(sizes)
 
 
-def pack_kernel(own_pad, starts, init_hbm, src_hbm, near_hbm, face_hbm, damp_hbm, matrix_hbm,
-                a_ref, b_ref, init_ref, scaled_ref, mode_ref, edge_ref, push_ref, m1, m2, idx_ref, wt_ref, matrix_ref,
+def pack_kernel(own_pad, starts, init_hbm, src_hbm, near_hbm, face_hbm, damp_hbm, lead_hbm, matrix_hbm,
+                a_ref, b_ref, init_ref, scaled_ref, mode_ref, edge_ref, push_ref, m1, m2, idx_ref, wt_ref,
+                lead_ref, matrix_ref,
                 src_ref, near_ref, face_ref, damp_ref, coef_ref, m0, rp, ut, sems):
     cells = init_ref.shape[1]
     nblk = cells // LANES
@@ -191,11 +197,12 @@
         pltpu.make_async_copy(face_hbm, face_ref, sems.at[0]),
         pltpu.make_async_copy(damp_hbm, damp_ref, sems.at[1]),
         pltpu.make_async_copy(near_hbm, near_ref, sems.at[2]),
-        pltpu.make_async_copy(src_hbm.at[0:half], src_ref.at[0:half], sems.at[3]),
-        pltpu.make_async_copy(src_hbm.at[half:own_pad], src_ref.at[half:own_pad], sems.at[4]),
-        pltpu.make_async_copy(init_hbm.at[0:half], init_ref.at[0:half], sems.at[5]),
-        pltpu.make_async_copy(init_hbm.at[half:own_pad], init_ref.at[half:own_pad], sems.at[6]),
-        pltpu.make_async_copy(matrix_hbm, matrix_ref, sems.at[7]),
+        pltpu.make_async_copy(lead_hbm, lead_ref, sems.at[3]),
+        pltpu.make_async_copy(init_hbm.at[0:half], init_ref.at[0:half], sems.at[4]),
+        pltpu.make_async_copy(init_hbm.at[half:own_pad], init_ref.at[half:own_pad], sems.at[5]),
+        pltpu.make_async_copy(src_hbm.at[0:half], src_ref.at[0:half], sems.at[6]),
+        pltpu.make_async_copy(src_hbm.at[half:own_pad], src_ref.at[half:own_pad], sems.at[7]),
+        pltpu.make_async_copy(matrix_hbm, matrix_ref, sems.at[8]),
     ]
     for copy in copies:
         copy.start()
@@ -208,49 +215,52 @@
     for b in range(nblk):
         build_table(idx_ref, wt_ref, b, near_ref[:, lanes(b)],
                     coef_ref[0:NEIGH, lanes(b)], coef_ref[NEIGH : NEIGH + 1, lanes(b)])
-    for copy in copies[3:]:
+
+    def table(b):
+        return idx_ref, wt_ref, b
+
+    def reader(ref, first=0):
+        return lambda g, b: ref[rows8(g), lanes(b - first)]
+
+    def coefs(s):
+        if not 0 <= s < nblk:
+            return jnp.zeros((1, LANES), jnp.float32)
+        return coef_ref[NEIGH : NEIGH + 1, lanes(s)]
+
+    ends = list(range(PB)) + list(range(nblk - PB, nblk))
+    for i, b in enumerate(ends):
+        build_product(ut, i, table(b), b, coefs)
+    for copy in copies[3:6]:
         copy.wait()
     groups = list(range(own_pad // 8))
-    for g in groups:
-        scaled_ref[rows8(g), :] = src_ref[rows8(g), :] * inverse
-    restrict = matrix_of(matrix_ref, starts[2], MODES, own_pad)
+    restrict = matrix_of(lead_ref, starts[2], MODES, own_pad)
+    derive = matrix_of(lead_ref, starts[0], own_pad, own_pad)
     for d in range(0, nblk, 2):
         m0[:, lanes(d, 2)] = dot(restrict, init_ref[:, lanes(d, 2)])
-    for d in range(0, nblk, 2):
-        mode_ref[:, lanes(d, 2)] = dot(restrict, scaled_ref[:, lanes(d, 2)])
-
-    def table(b):
-        return idx_ref, wt_ref, b
-
-    def reader(ref, first=0):
-        return lambda g, b: ref[rows8(g), lanes(b - first)]
-
-    derive = matrix_of(matrix_ref, starts[0], own_pad, own_pad)
+
     for side in range(2):
         at = side * (nblk - PB)
         deriv = dot(derive, init_ref[:, lanes(at, PB)])
-        for i in NEAR:
-            b = at + i
-            at2 = side * PB + i
-
-            def coefs(s):
-                if not 0 <= s < nblk:
-                    return jnp.zeros((1, LANES), jnp.float32)
-                return coef_ref[NEIGH : NEIGH + 1, lanes(s)]
-
-            build_product(ut, at2, table(b), b, coefs)
+        for i in range(PB):
+            b, here = at + i, lanes(side * PB + i)
             sums, pushes = stencil(
-                reader(init_ref), b, table(b), groups, lambda s: 0 <= s < nblk, (ut, at2)
+                reader(init_ref), b, table(b), groups, lambda s: 0 <= s < nblk, (ut, side * PB + i)
             )
             bf = coefficient(table(b))
             for g in groups:
-                push_ref[rows8(g), lanes(at2)] = pushes[g]
-                edge_ref[rows8(g), lanes(side * PB + i)] = (
-                    KEEP * init_ref[rows8(g), lanes(b)]
-                    + scaled_ref[rows8(g), lanes(b)]
-                    - bf * deriv[rows8(g), lanes(i)]
-                    + sums[g]
+                push_ref[rows8(g), here] = pushes[g]
+                edge_ref[rows8(g), here] = (
+                    KEEP * init_ref[rows8(g), lanes(b)] - bf * deriv[rows8(g), lanes(i)] + sums[g]
                 )
+    for copy in copies[6:8]:
+        copy.wait()
+    for g in groups:
+        scaled_ref[rows8(g), :] = src_ref[rows8(g), :] * inverse
+    for i, b in enumerate(ends):
+        for g in groups:
+            edge_ref[rows8(g), lanes(i)] = edge_ref[rows8(g), lanes(i)] + scaled_ref[rows8(g), lanes(b)]
+    for d in range(0, nblk, 2):
+        mode_ref[:, lanes(d, 2)] = dot(restrict, scaled_ref[:, lanes(d, 2)])
 
     def modes(src, first, out, to, b, known, keep):
         sums = stencil(reader(src, first), b, table(b), MODE_GROUPS, known)
@@ -260,17 +270,18 @@
         for g in MODE_GROUPS:
             out[rows8(g), lanes(to)] = parts[g] + sums[g] + mode_ref[rows8(g), lanes(b)]
 
+    near, far, deep = range(PB), range(PB, 2 * PB), range(2 * PB, 3 * PB)
     for b in range(PB, nblk - PB):
         modes(m0, 0, m1, b - PB, b, None, KEEP)
     for side in range(2):
-        for d in list(FAR) + list(DEEP):
+        for d in list(far) + list(deep):
             b = nblk - 1 - d if side else d
             modes(m1, PB, m2, b - PB, b, lambda s: PB <= s < nblk - PB, KEEP)
     for side in range(2):
-        for d in FAR:
+        for d in far:
             b = nblk - 1 - d if side else d
-            deep = [nblk - 1 - e if side else e for e in DEEP]
-            modes(m2, PB, rp, b - PB, b, lambda s, deep=deep: s in deep, None)
+            known = [nblk - 1 - e if side else e for e in deep]
+            modes(m2, PB, rp, b - PB, b, lambda s, known=known: s in known, None)
 
     near = near_ref[...].astype(jnp.float32)
     first_tiles, _ = halo_layout(own_pad)
@@ -307,8 +318,10 @@
         pack(a_ref, False)
         pack(b_ref, True)
 
-
-def cross_kernel(own_pad, rows, starts, init_ref, scaled_ref, idx_ref, wt_ref, matrix_ref,
+    copies[8].wait()
+
+
+def cross_kernel(own_pad, rows, starts, init_ref, scaled_ref, idx_ref, wt_ref, lead_ref, matrix_ref,
                  cross_ref, first, deriv, push, ut):
     cells = init_ref.shape[1]
     nblk = cells // LANES
@@ -318,7 +331,7 @@
     def table(b):
         return idx_ref, wt_ref, b
 
-    derive = matrix_of(matrix_ref, starts[0], rows, own_pad)
+    derive = matrix_of(lead_ref, starts[0], rows, own_pad)
     for d in range(0, nblk, 2):
         deriv[:, lanes(d, 2)] = dot(derive, init_ref[:, lanes(d, 2)])
 
@@ -349,7 +362,7 @@
                     + sums[g]
                 )
     derive = matrix_of(matrix_ref, starts[1], rows, rows)
-    couple = matrix_of(matrix_ref, starts[0] + own_pad, rows - own_pad, own_pad)
+    couple = matrix_of(lead_ref, starts[0] + own_pad, rows - own_pad, own_pad)
     for d in range(PB, nblk - PB, 2):
         deriv[:, lanes(d, 2)] = dot(derive, first[:, lanes(d, 2)])
         turn = dot(couple, push[:, lanes(d - PB, 2)])
@@ -399,7 +412,7 @@
 
 def outer_kernel(own_pad, rows, starts, a_ref, b_ref, init_ref, smode_ref, edge_ref,
                  push_ref, mpart_ref, first_ref, m1i_ref, m2i_ref, rp_ref, idx_in, wt_in,
-                 matrix_ref, send_ref, v1, deriv, c2x,
+                 lead_ref, matrix_ref, send_ref, v1, deriv, c2x,
                  halo, v2, push, m1x, m2x, rx, c1x, idx, wt, ut):
     cells = init_ref.shape[1]
     nblk = cells // LANES
@@ -458,7 +471,7 @@
         side, i = side_of(b)
         return halo[side, tiles[7], i : i + 1, :]
 
-    derive_cross = matrix_of(matrix_ref, starts[0], rows, own_pad)
+    derive_cross = matrix_of(lead_ref, starts[0], rows, own_pad)
     for side in range(2):
         first = nblk if side else -PB
         values = jnp.concatenate(
@@ -505,7 +518,7 @@
             m1x[rows8(g), lanes(b - low)] = section(3, g, b, True)
 
     ends = list(range(PB)) + list(range(nblk - PB, nblk))
-    couple = matrix_of(matrix_ref, starts[0] + own_pad, rows - own_pad, own_pad)
+    couple = matrix_of(lead_ref, starts[0] + own_pad, rows - own_pad, own_pad)
     for side in range(2):
         turn = dot(couple, push[:, lanes(side * PB, PB)])
         for i in range(PB):
@@ -675,8 +688,8 @@
     inst_count = lax.axis_size("inst")
     cell_count = lax.axis_size("cell")
     own_pad = up8(own)
-    matrices, starts, rows = constants(own, inst_count)
-    matrices = jnp.asarray(matrices)
+    lead, matrices, starts, rows = constants(own, inst_count)
+    lead, matrices = jnp.asarray(lead), jnp.asarray(matrices)
     cross = rows - own_pad
     if own_pad != own:
         initial = jnp.pad(initial, ((0, own_pad - own), (0, 0)))
@@ -695,20 +708,21 @@
     def int32(*shape):
         return jax.ShapeDtypeStruct(shape, jnp.int32)
 
-    pack_a, pack_b, initial, scaled, smode, ends, push, m1, m2, idx, wt, matrices = call(
+    pack_a, pack_b, initial, scaled, smode, ends, push, m1, m2, idx, wt, lead, matrices = call(
         functools.partial(pack_kernel, own_pad, starts),
         [f32(tiles, 8, LANES), f32(tiles, 8, LANES), wide(own_pad, nblk), wide(own_pad, nblk),
          wide(MODES, nblk), wide(own_pad, 2 * PB), wide(own_pad, 2 * PB), wide(MODES, nblk - 2 * PB),
          wide(MODES, nblk - 2 * PB),
          int32(nblk, 8, LANES), f32(nblk, slots, LANES),
+         jax.ShapeDtypeStruct(lead.shape, lead.dtype),
          jax.ShapeDtypeStruct(matrices.shape, matrices.dtype)],
         [scratch(own_pad, nblk), pltpu.VMEM((NEIGH, cells), jnp.int32), vm(NEIGH, cells), vm(1, cells),
          vm(8, cells), scratch(MODES, nblk), scratch(MODES, nblk - 2 * PB), vm(2 * PB, slots, LANES),
-         pltpu.SemaphoreType.DMA((8,))],
+         pltpu.SemaphoreType.DMA((9,))],
         2,
         *[
             pltpu.with_memory_space_constraint(x, pltpu.HBM)
-            for x in (initial, source, neighbors, face_weights, damping.reshape(1, cells), matrices)
+            for x in (initial, source, neighbors, face_weights, damping.reshape(1, cells), lead, matrices)
         ],
         fetch=True,
     )
@@ -723,7 +737,7 @@
         functools.partial(cross_kernel, own_pad, rows, starts),
         [wide(cross, nblk - 2 * PB), wide(rows, nblk), wide(rows, nblk)],
         [scratch(own_pad, nblk - 2 * PB), vm(nblk - 2 * PB, slots, LANES)], 3,
-        initial, scaled, idx, wt, matrices,
+        initial, scaled, idx, wt, lead, matrices,
     )
 
     def share(array, k):
@@ -749,7 +763,7 @@
          scratch(own_pad, 2 * PB), scratch(MODES, nblk + 4 * PB), scratch(MODES, nblk + 4 * PB),
          scratch(MODES, nblk + 4 * PB), scratch(MODES, nblk + 2 * PB),
          pltpu.VMEM((4 * PB, 8, LANES), jnp.int32), vm(4 * PB, slots, LANES), vm(2 * PB, slots, LANES)],
-        8, halo_a, halo_b, initial, smode, ends, push, mpart, first, m1, m2, rp, idx, wt, matrices,
+        8, halo_a, halo_b, initial, smode, ends, push, mpart, first, m1, m2, rp, idx, wt, lead, matrices,
     )
 
     def share_late(k):

time: 21.8 us -> 21.6 us (level)
  Pallas kernels: 9.89 us -> 9.59 us
    pallas_call x6, Pallas kernels: 9.89 us -> 9.59 us  [call(): pl.pallas_call(kernel, out_shape=out_shape, in_specs=[pl.BlockSpec(memory...]
  transfers between devices with their start and end apart: 4 -> 4, of which waited for: 2 -> 2; matrix products, arithmetic and copies ran while one was open for 0% -> 0% of each run, Pallas kernels for 30% -> 29%
where the time goes in v7:
time: 21.6 us; the launch traced here: 21.5 us
  Pallas kernels  9.59 us (44%)
  waiting for transfers between devices  7.48 us (35%)
  starting transfers between devices  4.35 us (20%)
    pallas_call x6, Pallas kernels, call(): pl.pallas_call(kernel, out_shape=out_shape, in_specs=[pl.BlockSpec(memory...  9.59 us
    ppermute x1, waiting for transfers between devices, per_device(): lax.ppermute(share_late(k), 'inst', shift(k))  4.1 us
    ppermute x1, waiting for transfers between devices, per_device(): halo_b = lax.ppermute(pack_b, 'cell', far_pairs)  3.37 us
    ppermute x1, starting transfers between devices, per_device(): halo_b = lax.ppermute(pack_b, 'cell', far_pairs)  3.05 us
    ppermute x1, starting transfers between devices, per_device(): halo_a = lax.ppermute(pack_a, 'cell', near_pairs)  0.71 us
  transfers between devices with their start and end apart: 4, of which 2 were waited for; matrix products, arithmetic and copies ran while one was open for 0% of the time, Pallas kernels for 29%

profile of v7, /device:TPU:19, one launch (start us, length us, event | category | flops | bytes accessed | tf_op | source)
XLA Modules:
  0.0 21.5 jit_solution(264252451165205335)
XLA Ops:
  0.0 2.4 %shard_map.73 = (f32[41,8,128]{2,1,0:T(8,128)S(1)}, f32[41,8,128]{2,1,0:T(8,128)S(1)}, f32[40,2048]{1,0:T(8,128)S(1)}, f32[40,2048]{1,0:T(8,128)S(1)}, f32[16,20...) custom-call(f32[40,2048]{1,0:T(8,128)} %init_hbm.1, ...), custom_call_target="tpu_custom_call" | custom-call | flops 200000000 | bytes 6000000 | tf_op jit(solution)/shard_map/pallas_call | solution.py:672
  2.4 0.7 %collective-permute-start = (f32[41,8,128]{2,1,0:T(8,128)S(1)}, f32[41,8,128]{2,1,0:T(8,128)S(1)}, u32[]{:S(2)}, u32[]{:S(2)}) collective-permute-start(f32[41,8,128]{2,1,0:T(8,128)S(1)} %get-tuple-element.36), channel_id=1, source_target_pairs={{0,2},{2,0},{4,6},{6,4},{8,10},{10,8},{12,14},{14,12},{16,18},{18,... | collective-permute-start | bytes 503816 | tf_op jit(solution)/shard_map/ppermute | solution.py:734
  3.1 3.0 %collective-permute-start.1 = (f32[41,8,128]{2,1,0:T(8,128)S(1)}, f32[41,8,128]{2,1,0:T(8,128)S(1)}, u32[]{:S(2)}, u32[]{:S(2)}) collective-permute-start(f32[41,8,128]{2,1,0:T(8,128)S(1)} %get-tuple-element.37), channel_id=1, source_target_pairs={{2,4},{4,2},{6,8},{8,6},{10,12},{12,10},{14,16},{16,14},{18,20},{2... | collective-permute-start | bytes 503816 | tf_op jit(solution)/shard_map/ppermute | solution.py:733
  6.2 1.4 %shard_map.74 = (f32[40,1536]{1,0:T(8,128)S(1)}, f32[80,2048]{1,0:T(8,128)S(1)}, f32[80,2048]{1,0:T(8,128)S(1)}) custom-call(f32[40,2048]{1,0:T(8,128)S(1)} %get-tuple-element.28.init_ref, f32[40,2048]{1,0:T(8,128)S(1)} %get-tuple-element.29.scaled_ref, s32[16,8,128]{2,1,0:T(8,128)S(1)} %get-tuple-element.30.idx_ref.idx_in, ...), custom_call_target="tpu_custom_call" | custom-call | flops 300000000 | bytes 9000000 | tf_op jit(solution)/shard_map/pallas_call | solution.py:672
  7.6 0.3 %collective-permute-start.2 = (f32[40,1536]{1,0:T(8,128)S(1)}, f32[40,1536]{1,0:T(8,128)S(1)}, u32[]{:S(2)}, u32[]{:S(2)}) collective-permute-start(f32[40,1536]{1,0:T(8,128)S(1)} %get-tuple-element.49), channel_id=1, source_target_pairs={{0,1},{1,0},{2,3},{3,2},{4,5},{5,4},{6,7},{7,6},{8,9},{9,8},{10,11... | collective-permute-start | bytes 737288 | tf_op jit(solution)/shard_map/ppermute | solution.py:752
  7.9 0.6 %shard_map.75 = (f32[16,512]{1,0:T(8,128)S(1)}, f32[16,1536]{1,0:T(8,128)S(1)}, f32[16,2048]{1,0:T(8,128)S(1)}) custom-call(f32[16,2048]{1,0:T(8,128)S(1)} %get-tuple-element.38.smode_ref, f32[16,1536]{1,0:T(8,128)S(1)} %get-tuple-element.41.m1_ref.m1i_ref, f32[16,1536]{1,0:T(8,128)S(1)} %get-tuple-element.42.m2_ref, ...), custom_call_target="tpu_custom_call" | custom-call | flops 300000000 | bytes 9000000 | tf_op jit(solution)/shard_map/pallas_call | solution.py:672
  8.5 0.0 collective-permute-done.a_ref
  8.5 3.4 %collective-permute-done.1.b_ref = f32[41,8,128]{2,1,0:T(8,128)S(1)} collective-permute-done((f32[41,8,128]{2,1,0:T(8,128)S(1)}, f32[41,8,128]{2,1,0:T(8,128)S(1)}, u32[]{:S(2)}, u32[]{:S(2)}) %collective-permute-start.1) | collective-permute-done | bytes 167968 | tf_op jit(solution)/shard_map/ppermute | solution.py:733
  11.9 3.0 %shard_map.76 = (f32[88,512]{1,0:T(8,128)S(1)}, f32[80,1024]{1,0:T(8,128)S(1)}, f32[80,512]{1,0:T(8,128)S(1)}, f32[16,2048]{1,0:T(8,128)S(1)}) custom-call(f32[41,8,128]{2,1,0:T(8,128)S(1)} %collective-permute-done.a_ref, f32[41,8,128]{2,1,0:T(8,128)S(1)} %collective-permute-done.1.b_ref, f32[40,2048]{1,0:T(8,128)S(1)} %get-tuple-element.28.init_ref, ...), custom_call_target="tpu_custom_call" | custom-call | flops 800000000 | bytes 24000000 | tf_op jit(solution)/shard_map/pallas_call | solution.py:672
  14.9 0.3 %collective-permute-start.3 = (f32[88,512]{1,0:T(8,128)S(1)}, f32[88,512]{1,0:T(8,128)S(1)}, u32[]{:S(2)}, u32[]{:S(2)}) collective-permute-start(f32[88,512]{1,0:T(8,128)S(1)} %get-tuple-element.50), channel_id=1, source_target_pairs={{0,1},{1,0},{2,3},{3,2},{4,5},{5,4},{6,7},{7,6},{8,9},{9,8},{10,11... | collective-permute-start | bytes 540680 | tf_op jit(solution)/shard_map/ppermute | solution.py:774
  15.2 1.3 %shard_map.77.base_ref = f32[40,2048]{1,0:T(8,128)S(1)} custom-call(f32[80,2048]{1,0:T(8,128)S(1)} %get-tuple-element.34.first_ref.first, f32[80,2048]{1,0:T(8,128)S(1)} %get-tuple-element.35.deriv, f32[80,1024]{1,0:T(8,128)S(1)} %get-tuple-element.46.v1_ref, f32[80,512]{1,0:T(8,128)S(1)} %get-tuple-element.47.ends_ref, ...), custom_call_target="tpu_custom_call" | custom-call | flops 200000000 | bytes 6000000 | tf_op jit(solution)/shard_map/pallas_call | solution.py:672
  16.5 0.0 collective-permute-done.2.refs_0_
  16.5 4.1 %collective-permute-done.3.refs_1_ = f32[88,512]{1,0:T(8,128)S(1)} collective-permute-done((f32[88,512]{1,0:T(8,128)S(1)}, f32[88,512]{1,0:T(8,128)S(1)}, u32[]{:S(2)}, u32[]{:S(2)}) %collective-permute-start.3) | collective-permute-done | bytes 180256 | tf_op jit(solution)/shard_map/ppermute | solution.py:774
  20.6 0.9 %shard_map.78 = f32[40,2048]{1,0:T(8,128)} custom-call(f32[40,2048]{1,0:T(8,128)S(1)} %shard_map.77.base_ref, bf16[224,256]{1,0:T(8,128)(2,1)S(1)} %get-tuple-element.33.matrix_ref, f32[40,1536]{1,0:T(8,128)S(1)} %collective-permute-done.2.refs_0_, f32[88,512]{1,0:T(8,128)S(1)} %collective-permute-done.3.refs_1_), custom_call_target="tpu_custom_call" | custom-call | flops 100000000 | bytes 3000000 | tf_op jit(solution)/shard_map/pallas_call | solution.py:672
Async XLA Ops:
  2.4 6.1 %collective-permute-start = (f32[41,8,128]{2,1,0:T(8,128)S(1)}, f32[41,8,128]{2,1,0:T(8,128)S(1)}, u32[]{:S(2)}, u32[]{:S(2)}) collective-permute-start(f32[41,8,128]{2,1,0:T(8,128)S(1)} %get-tuple-element.36), channel_id=1, source_target_pairs={{0,2},{2,0},{4,6},{6,4},{8,10},{10,8},{12,14},{14,12},{16,18},{18,... | collective-permute-start | bytes 503816 | tf_op jit(solution)/shard_map/ppermute | solution.py:734
  3.1 8.8 %collective-permute-start.1 = (f32[41,8,128]{2,1,0:T(8,128)S(1)}, f32[41,8,128]{2,1,0:T(8,128)S(1)}, u32[]{:S(2)}, u32[]{:S(2)}) collective-permute-start(f32[41,8,128]{2,1,0:T(8,128)S(1)} %get-tuple-element.37), channel_id=1, source_target_pairs={{2,4},{4,2},{6,8},{8,6},{10,12},{12,10},{14,16},{16,14},{18,20},{2... | collective-permute-start | bytes 503816 | tf_op jit(solution)/shard_map/ppermute | solution.py:733
  7.6 8.9 %collective-permute-start.2 = (f32[40,1536]{1,0:T(8,128)S(1)}, f32[40,1536]{1,0:T(8,128)S(1)}, u32[]{:S(2)}, u32[]{:S(2)}) collective-permute-start(f32[40,1536]{1,0:T(8,128)S(1)} %get-tuple-element.49), channel_id=1, source_target_pairs={{0,1},{1,0},{2,3},{3,2},{4,5},{5,4},{6,7},{7,6},{8,9},{9,8},{10,11... | collective-permute-start | bytes 737288 | tf_op jit(solution)/shard_map/ppermute | solution.py:752
  14.9 5.7 %collective-permute-start.3 = (f32[88,512]{1,0:T(8,128)S(1)}, f32[88,512]{1,0:T(8,128)S(1)}, u32[]{:S(2)}, u32[]{:S(2)}) collective-permute-start(f32[88,512]{1,0:T(8,128)S(1)} %get-tuple-element.50), channel_id=1, source_target_pairs={{0,1},{1,0},{2,3},{3,2},{4,5},{5,4},{6,7},{7,6},{8,9},{9,8},{10,11... | collective-permute-start | bytes 540680 | tf_op jit(solution)/shard_map/ppermute | solution.py:774

commit v8 on v7

--- a/solution.py
+++ b/solution.py
@@ -181,9 +181,16 @@
 
 def halo_layout(own_pad):
     fine, mode = own_pad // 8 * PB, MODES // 8 * PB
-    sizes = [fine, fine, mode, mode, mode, mode, 2 * PB, 1]
+    sizes = [fine, fine, mode, mode, mode, mode, 2 * PB]
     starts = [sum(sizes[:i]) for i in range(len(sizes))]
     return starts, sum(sizes)
+
+
+SPARE = 2
+
+
+def spare_tile(tiles, near_last, i):
+    return tiles[2 if (i >= PB) == bool(near_last) else 3] + PB + i % PB
 
 
 def pack_kernel(own_pad, starts, init_hbm, src_hbm, near_hbm, face_hbm, damp_hbm, lead_hbm, matrix_hbm,
@@ -304,7 +311,7 @@
         for i in range(2 * PB):
             out[first_tiles[6] + i, 0:NEIGH, :] = coef_ref[0:NEIGH, lanes(all_at + i)]
             out[first_tiles[6] + i, NEIGH : 2 * NEIGH, :] = near[:, lanes(all_at + i)]
-            out[first_tiles[7], i : i + 1, :] = coef_ref[NEIGH : NEIGH + 1, lanes(all_at + i)]
+            out[spare_tile(first_tiles, high, i), SPARE : SPARE + 1, :] = coef_ref[NEIGH : NEIGH + 1, lanes(all_at + i)]
 
     odd = lax.axis_index("cell") & 1
 
@@ -439,7 +446,8 @@
         for i in range(2 * PB):
             tile = tiles[6] + i
             build_table(idx, wt, side * 2 * PB + i, halo[side, tile, NEIGH : 2 * NEIGH, :].astype(jnp.int32),
-                        halo[side, tile, 0:NEIGH, :], halo[side, tiles[7], i : i + 1, :])
+                        halo[side, tile, 0:NEIGH, :],
+                        halo[side, spare_tile(tiles, side == 0, i), SPARE : SPARE + 1, :])
 
     def table(b):
         if 0 <= b < nblk:
@@ -469,7 +477,7 @@
         if own(b):
             return jnp.zeros((1, LANES), jnp.float32)
         side, i = side_of(b)
-        return halo[side, tiles[7], i : i + 1, :]
+        return halo[side, spare_tile(tiles, side == 0, i), SPARE : SPARE + 1, :]
 
     derive_cross = matrix_of(lead_ref, starts[0], rows, own_pad)
     for side in range(2):

time: 21.6 us -> 21.6 us (level)
  transfers between devices with their start and end apart: 4 -> 4, of which waited for: 2 -> 2; matrix products, arithmetic and copies ran while one was open for 0% -> 0% of each run, Pallas kernels for 29% -> 30%
where the time goes in v8:
time: 21.6 us; the launch traced here: 21.5 us
  Pallas kernels  9.74 us (45%)
  waiting for transfers between devices  7.35 us (34%)
  starting transfers between devices  4.35 us (20%)
    pallas_call x6, Pallas kernels, call(): pl.pallas_call(kernel, out_shape=out_shape, in_specs=[pl.BlockSpec(memory...  9.74 us
    ppermute x1, waiting for transfers between devices, per_device(): lax.ppermute(share_late(k), 'inst', shift(k))  4.13 us
    ppermute x1, waiting for transfers between devices, per_device(): halo_b = lax.ppermute(pack_b, 'cell', far_pairs)  3.21 us
    ppermute x1, starting transfers between devices, per_device(): halo_b = lax.ppermute(pack_b, 'cell', far_pairs)  3.05 us
    ppermute x1, starting transfers between devices, per_device(): halo_a = lax.ppermute(pack_a, 'cell', near_pairs)  0.72 us
  transfers between devices with their start and end apart: 4, of which 2 were waited for; matrix products, arithmetic and copies ran while one was open for 0% of the time, Pallas kernels for 30%

profile of v8, /device:TPU:19, one launch (start us, length us, event | category | flops | bytes accessed | tf_op | source)
XLA Modules:
  0.0 21.5 jit_solution(5941581917918240982)
XLA Ops:
  0.0 2.4 %shard_map.73 = (f32[40,8,128]{2,1,0:T(8,128)S(1)}, f32[40,8,128]{2,1,0:T(8,128)S(1)}, f32[40,2048]{1,0:T(8,128)S(1)}, f32[40,2048]{1,0:T(8,128)S(1)}, f32[16,20...) custom-call(f32[40,2048]{1,0:T(8,128)} %init_hbm.1, ...), custom_call_target="tpu_custom_call" | custom-call | flops 200000000 | bytes 6000000 | tf_op jit(solution)/shard_map/pallas_call | solution.py:680
  2.4 0.7 %collective-permute-start = (f32[40,8,128]{2,1,0:T(8,128)S(1)}, f32[40,8,128]{2,1,0:T(8,128)S(1)}, u32[]{:S(2)}, u32[]{:S(2)}) collective-permute-start(f32[40,8,128]{2,1,0:T(8,128)S(1)} %get-tuple-element.36), channel_id=1, source_target_pairs={{0,2},{2,0},{4,6},{6,4},{8,10},{10,8},{12,14},{14,12},{16,18},{18,... | collective-permute-start | bytes 491528 | tf_op jit(solution)/shard_map/ppermute | solution.py:742
  3.1 3.0 %collective-permute-start.1 = (f32[40,8,128]{2,1,0:T(8,128)S(1)}, f32[40,8,128]{2,1,0:T(8,128)S(1)}, u32[]{:S(2)}, u32[]{:S(2)}) collective-permute-start(f32[40,8,128]{2,1,0:T(8,128)S(1)} %get-tuple-element.37), channel_id=1, source_target_pairs={{2,4},{4,2},{6,8},{8,6},{10,12},{12,10},{14,16},{16,14},{18,20},{2... | collective-permute-start | bytes 491528 | tf_op jit(solution)/shard_map/ppermute | solution.py:741
  6.2 1.5 %shard_map.74 = (f32[40,1536]{1,0:T(8,128)S(1)}, f32[80,2048]{1,0:T(8,128)S(1)}, f32[80,2048]{1,0:T(8,128)S(1)}) custom-call(f32[40,2048]{1,0:T(8,128)S(1)} %get-tuple-element.28.init_ref, f32[40,2048]{1,0:T(8,128)S(1)} %get-tuple-element.29.scaled_ref, s32[16,8,128]{2,1,0:T(8,128)S(1)} %get-tuple-element.30.idx_ref.idx_in, ...), custom_call_target="tpu_custom_call" | custom-call | flops 300000000 | bytes 9000000 | tf_op jit(solution)/shard_map/pallas_call | solution.py:680
  7.7 0.3 %collective-permute-start.2 = (f32[40,1536]{1,0:T(8,128)S(1)}, f32[40,1536]{1,0:T(8,128)S(1)}, u32[]{:S(2)}, u32[]{:S(2)}) collective-permute-start(f32[40,1536]{1,0:T(8,128)S(1)} %get-tuple-element.49), channel_id=1, source_target_pairs={{0,1},{1,0},{2,3},{3,2},{4,5},{5,4},{6,7},{7,6},{8,9},{9,8},{10,11... | collective-permute-start | bytes 737288 | tf_op jit(solution)/shard_map/ppermute | solution.py:760
  8.0 0.6 %shard_map.75 = (f32[16,512]{1,0:T(8,128)S(1)}, f32[16,1536]{1,0:T(8,128)S(1)}, f32[16,2048]{1,0:T(8,128)S(1)}) custom-call(f32[16,2048]{1,0:T(8,128)S(1)} %get-tuple-element.38.smode_ref, f32[16,1536]{1,0:T(8,128)S(1)} %get-tuple-element.41.m1_ref.m1i_ref, f32[16,1536]{1,0:T(8,128)S(1)} %get-tuple-element.42.m2_ref, ...), custom_call_target="tpu_custom_call" | custom-call | flops 300000000 | bytes 9000000 | tf_op jit(solution)/shard_map/pallas_call | solution.py:680
  8.6 0.0 collective-permute-done.a_ref
  8.6 3.2 %collective-permute-done.1.b_ref = f32[40,8,128]{2,1,0:T(8,128)S(1)} collective-permute-done((f32[40,8,128]{2,1,0:T(8,128)S(1)}, f32[40,8,128]{2,1,0:T(8,128)S(1)}, u32[]{:S(2)}, u32[]{:S(2)}) %collective-permute-start.1) | collective-permute-done | bytes 163872 | tf_op jit(solution)/shard_map/ppermute | solution.py:741
  11.8 3.1 %shard_map.76 = (f32[88,512]{1,0:T(8,128)S(1)}, f32[80,1024]{1,0:T(8,128)S(1)}, f32[80,512]{1,0:T(8,128)S(1)}, f32[16,2048]{1,0:T(8,128)S(1)}) custom-call(f32[40,8,128]{2,1,0:T(8,128)S(1)} %collective-permute-done.a_ref, f32[40,8,128]{2,1,0:T(8,128)S(1)} %collective-permute-done.1.b_ref, f32[40,2048]{1,0:T(8,128)S(1)} %get-tuple-element.28.init_ref, ...), custom_call_target="tpu_custom_call" | custom-call | flops 800000000 | bytes 24000000 | tf_op jit(solution)/shard_map/pallas_call | solution.py:680
  14.9 0.3 %collective-permute-start.3 = (f32[88,512]{1,0:T(8,128)S(1)}, f32[88,512]{1,0:T(8,128)S(1)}, u32[]{:S(2)}, u32[]{:S(2)}) collective-permute-start(f32[88,512]{1,0:T(8,128)S(1)} %get-tuple-element.50), channel_id=1, source_target_pairs={{0,1},{1,0},{2,3},{3,2},{4,5},{5,4},{6,7},{7,6},{8,9},{9,8},{10,11... | collective-permute-start | bytes 540680 | tf_op jit(solution)/shard_map/ppermute | solution.py:782
  15.1 1.3 %shard_map.77.base_ref = f32[40,2048]{1,0:T(8,128)S(1)} custom-call(f32[80,2048]{1,0:T(8,128)S(1)} %get-tuple-element.34.first_ref.first, f32[80,2048]{1,0:T(8,128)S(1)} %get-tuple-element.35.deriv, f32[80,1024]{1,0:T(8,128)S(1)} %get-tuple-element.46.v1_ref, f32[80,512]{1,0:T(8,128)S(1)} %get-tuple-element.47.ends_ref, ...), custom_call_target="tpu_custom_call" | custom-call | flops 200000000 | bytes 6000000 | tf_op jit(solution)/shard_map/pallas_call | solution.py:680
  16.5 0.0 collective-permute-done.2.refs_0_
  16.5 4.1 %collective-permute-done.3.refs_1_ = f32[88,512]{1,0:T(8,128)S(1)} collective-permute-done((f32[88,512]{1,0:T(8,128)S(1)}, f32[88,512]{1,0:T(8,128)S(1)}, u32[]{:S(2)}, u32[]{:S(2)}) %collective-permute-start.3) | collective-permute-done | bytes 180256 | tf_op jit(solution)/shard_map/ppermute | solution.py:782
  20.6 0.9 %shard_map.78 = f32[40,2048]{1,0:T(8,128)} custom-call(f32[40,2048]{1,0:T(8,128)S(1)} %shard_map.77.base_ref, bf16[224,256]{1,0:T(8,128)(2,1)S(1)} %get-tuple-element.33.matrix_ref, f32[40,1536]{1,0:T(8,128)S(1)} %collective-permute-done.2.refs_0_, f32[88,512]{1,0:T(8,128)S(1)} %collective-permute-done.3.refs_1_), custom_call_target="tpu_custom_call" | custom-call | flops 100000000 | bytes 3000000 | tf_op jit(solution)/shard_map/pallas_call | solution.py:680
Async XLA Ops:
  2.4 6.2 %collective-permute-start = (f32[40,8,128]{2,1,0:T(8,128)S(1)}, f32[40,8,128]{2,1,0:T(8,128)S(1)}, u32[]{:S(2)}, u32[]{:S(2)}) collective-permute-start(f32[40,8,128]{2,1,0:T(8,128)S(1)} %get-tuple-element.36), channel_id=1, source_target_pairs={{0,2},{2,0},{4,6},{6,4},{8,10},{10,8},{12,14},{14,12},{16,18},{18,... | collective-permute-start | bytes 491528 | tf_op jit(solution)/shard_map/ppermute | solution.py:742
  3.1 8.7 %collective-permute-start.1 = (f32[40,8,128]{2,1,0:T(8,128)S(1)}, f32[40,8,128]{2,1,0:T(8,128)S(1)}, u32[]{:S(2)}, u32[]{:S(2)}) collective-permute-start(f32[40,8,128]{2,1,0:T(8,128)S(1)} %get-tuple-element.37), channel_id=1, source_target_pairs={{2,4},{4,2},{6,8},{8,6},{10,12},{12,10},{14,16},{16,14},{18,20},{2... | collective-permute-start | bytes 491528 | tf_op jit(solution)/shard_map/ppermute | solution.py:741
  7.7 8.8 %collective-permute-start.2 = (f32[40,1536]{1,0:T(8,128)S(1)}, f32[40,1536]{1,0:T(8,128)S(1)}, u32[]{:S(2)}, u32[]{:S(2)}) collective-permute-start(f32[40,1536]{1,0:T(8,128)S(1)} %get-tuple-element.49), channel_id=1, source_target_pairs={{0,1},{1,0},{2,3},{3,2},{4,5},{5,4},{6,7},{7,6},{8,9},{9,8},{10,11... | collective-permute-start | bytes 737288 | tf_op jit(solution)/shard_map/ppermute | solution.py:760
  14.9 5.7 %collective-permute-start.3 = (f32[88,512]{1,0:T(8,128)S(1)}, f32[88,512]{1,0:T(8,128)S(1)}, u32[]{:S(2)}, u32[]{:S(2)}) collective-permute-start(f32[88,512]{1,0:T(8,128)S(1)} %get-tuple-element.50), channel_id=1, source_target_pairs={{0,1},{1,0},{2,3},{3,2},{4,5},{5,4},{6,7},{7,6},{8,9},{9,8},{10,11... | collective-permute-start | bytes 540680 | tf_op jit(solution)/shard_map/ppermute | solution.py:782

commit v9 on v8

--- a/solution.py
+++ b/solution.py
@@ -658,10 +658,9 @@
                     + dot(lift, late[k][first : first + MODES, lanes(at, 2)])
                 )
         out_ref[:, lanes(b, 2)] = total
-        if b % 4 == 2:
-            piece = (slice(None), lanes(b - 2, 4))
-            copies.append(pltpu.make_async_copy(out_ref.at[piece], out_hbm.at[piece], sems.at[b // 4]))
-            copies[-1].start()
+        piece = (slice(None), lanes(b, 2))
+        copies.append(pltpu.make_async_copy(out_ref.at[piece], out_hbm.at[piece], sems.at[b // 2]))
+        copies[-1].start()
     for copy in copies:
         copy.wait()
 
@@ -787,7 +786,7 @@
     received = [r for pair in zip(early, late) for r in pair]
     out = call(
         functools.partial(final_kernel, inst_count - 1, starts), f32(own_pad, cells),
-        [vm(own_pad, cells), pltpu.SemaphoreType.DMA((nblk // 4,))], 1,
+        [vm(own_pad, cells), pltpu.SemaphoreType.DMA((nblk // 2,))], 1,
         base, matrices, *received, store=True,
     )
     return out[:own] if own_pad != own else out

time: 21.6 us -> 21.7 us (level)
  no operation moved by 1% of the time
where the time goes in v9:
time: 21.7 us; the launch traced here: 21.5 us
  Pallas kernels  9.76 us (45%)
  waiting for transfers between devices  7.35 us (34%)
  starting transfers between devices  4.35 us (20%)
    pallas_call x6, Pallas kernels, call(): pl.pallas_call(kernel, out_shape=out_shape, in_specs=[pl.BlockSpec(memory...  9.76 us
    ppermute x1, waiting for transfers between devices, per_device(): lax.ppermute(share_late(k), 'inst', shift(k))  4.13 us
    ppermute x1, waiting for transfers between devices, per_device(): halo_b = lax.ppermute(pack_b, 'cell', far_pairs)  3.21 us
    ppermute x1, starting transfers between devices, per_device(): halo_b = lax.ppermute(pack_b, 'cell', far_pairs)  3.05 us
    ppermute x1, starting transfers between devices, per_device(): halo_a = lax.ppermute(pack_a, 'cell', near_pairs)  0.72 us
  transfers between devices with their start and end apart: 4, of which 2 were waited for; matrix products, arithmetic and copies ran while one was open for 0% of the time, Pallas kernels for 30%

profile of v9, /device:TPU:19, one launch (start us, length us, event | category | flops | bytes accessed | tf_op | source)
XLA Modules:
  0.0 21.5 jit_solution(1530338321391269709)
XLA Ops:
  0.0 2.4 %shard_map.73 = (f32[40,8,128]{2,1,0:T(8,128)S(1)}, f32[40,8,128]{2,1,0:T(8,128)S(1)}, f32[40,2048]{1,0:T(8,128)S(1)}, f32[40,2048]{1,0:T(8,128)S(1)}, f32[16,20...) custom-call(f32[40,2048]{1,0:T(8,128)} %init_hbm.1, ...), custom_call_target="tpu_custom_call" | custom-call | flops 200000000 | bytes 6000000 | tf_op jit(solution)/shard_map/pallas_call | solution.py:679
  2.4 0.7 %collective-permute-start = (f32[40,8,128]{2,1,0:T(8,128)S(1)}, f32[40,8,128]{2,1,0:T(8,128)S(1)}, u32[]{:S(2)}, u32[]{:S(2)}) collective-permute-start(f32[40,8,128]{2,1,0:T(8,128)S(1)} %get-tuple-element.36), channel_id=1, source_target_pairs={{0,2},{2,0},{4,6},{6,4},{8,10},{10,8},{12,14},{14,12},{16,18},{18,... | collective-permute-start | bytes 491528 | tf_op jit(solution)/shard_map/ppermute | solution.py:741
  3.1 3.0 %collective-permute-start.1 = (f32[40,8,128]{2,1,0:T(8,128)S(1)}, f32[40,8,128]{2,1,0:T(8,128)S(1)}, u32[]{:S(2)}, u32[]{:S(2)}) collective-permute-start(f32[40,8,128]{2,1,0:T(8,128)S(1)} %get-tuple-element.37), channel_id=1, source_target_pairs={{2,4},{4,2},{6,8},{8,6},{10,12},{12,10},{14,16},{16,14},{18,20},{2... | collective-permute-start | bytes 491528 | tf_op jit(solution)/shard_map/ppermute | solution.py:740
  6.2 1.5 %shard_map.74 = (f32[40,1536]{1,0:T(8,128)S(1)}, f32[80,2048]{1,0:T(8,128)S(1)}, f32[80,2048]{1,0:T(8,128)S(1)}) custom-call(f32[40,2048]{1,0:T(8,128)S(1)} %get-tuple-element.28.init_ref, f32[40,2048]{1,0:T(8,128)S(1)} %get-tuple-element.29.scaled_ref, s32[16,8,128]{2,1,0:T(8,128)S(1)} %get-tuple-element.30.idx_ref.idx_in, ...), custom_call_target="tpu_custom_call" | custom-call | flops 300000000 | bytes 9000000 | tf_op jit(solution)/shard_map/pallas_call | solution.py:679
  7.7 0.3 %collective-permute-start.2 = (f32[40,1536]{1,0:T(8,128)S(1)}, f32[40,1536]{1,0:T(8,128)S(1)}, u32[]{:S(2)}, u32[]{:S(2)}) collective-permute-start(f32[40,1536]{1,0:T(8,128)S(1)} %get-tuple-element.49), channel_id=1, source_target_pairs={{0,1},{1,0},{2,3},{3,2},{4,5},{5,4},{6,7},{7,6},{8,9},{9,8},{10,11... | collective-permute-start | bytes 737288 | tf_op jit(solution)/shard_map/ppermute | solution.py:759
  8.0 0.6 %shard_map.75 = (f32[16,512]{1,0:T(8,128)S(1)}, f32[16,1536]{1,0:T(8,128)S(1)}, f32[16,2048]{1,0:T(8,128)S(1)}) custom-call(f32[16,2048]{1,0:T(8,128)S(1)} %get-tuple-element.38.smode_ref, f32[16,1536]{1,0:T(8,128)S(1)} %get-tuple-element.41.m1_ref.m1i_ref, f32[16,1536]{1,0:T(8,128)S(1)} %get-tuple-element.42.m2_ref, ...), custom_call_target="tpu_custom_call" | custom-call | flops 300000000 | bytes 9000000 | tf_op jit(solution)/shard_map/pallas_call | solution.py:679
  8.6 0.0 collective-permute-done.a_ref
  8.6 3.2 %collective-permute-done.1.b_ref = f32[40,8,128]{2,1,0:T(8,128)S(1)} collective-permute-done((f32[40,8,128]{2,1,0:T(8,128)S(1)}, f32[40,8,128]{2,1,0:T(8,128)S(1)}, u32[]{:S(2)}, u32[]{:S(2)}) %collective-permute-start.1) | collective-permute-done | bytes 163872 | tf_op jit(solution)/shard_map/ppermute | solution.py:740
  11.8 3.1 %shard_map.76 = (f32[88,512]{1,0:T(8,128)S(1)}, f32[80,1024]{1,0:T(8,128)S(1)}, f32[80,512]{1,0:T(8,128)S(1)}, f32[16,2048]{1,0:T(8,128)S(1)}) custom-call(f32[40,8,128]{2,1,0:T(8,128)S(1)} %collective-permute-done.a_ref, f32[40,8,128]{2,1,0:T(8,128)S(1)} %collective-permute-done.1.b_ref, f32[40,2048]{1,0:T(8,128)S(1)} %get-tuple-element.28.init_ref, ...), custom_call_target="tpu_custom_call" | custom-call | flops 800000000 | bytes 24000000 | tf_op jit(solution)/shard_map/pallas_call | solution.py:679
  14.9 0.3 %collective-permute-start.3 = (f32[88,512]{1,0:T(8,128)S(1)}, f32[88,512]{1,0:T(8,128)S(1)}, u32[]{:S(2)}, u32[]{:S(2)}) collective-permute-start(f32[88,512]{1,0:T(8,128)S(1)} %get-tuple-element.50), channel_id=1, source_target_pairs={{0,1},{1,0},{2,3},{3,2},{4,5},{5,4},{6,7},{7,6},{8,9},{9,8},{10,11... | collective-permute-start | bytes 540680 | tf_op jit(solution)/shard_map/ppermute | solution.py:781
  15.1 1.3 %shard_map.77.base_ref = f32[40,2048]{1,0:T(8,128)S(1)} custom-call(f32[80,2048]{1,0:T(8,128)S(1)} %get-tuple-element.34.first_ref.first, f32[80,2048]{1,0:T(8,128)S(1)} %get-tuple-element.35.deriv, f32[80,1024]{1,0:T(8,128)S(1)} %get-tuple-element.46.v1_ref, f32[80,512]{1,0:T(8,128)S(1)} %get-tuple-element.47.ends_ref, ...), custom_call_target="tpu_custom_call" | custom-call | flops 200000000 | bytes 6000000 | tf_op jit(solution)/shard_map/pallas_call | solution.py:679
  16.5 0.0 collective-permute-done.2.refs_0_
  16.5 4.1 %collective-permute-done.3.refs_1_ = f32[88,512]{1,0:T(8,128)S(1)} collective-permute-done((f32[88,512]{1,0:T(8,128)S(1)}, f32[88,512]{1,0:T(8,128)S(1)}, u32[]{:S(2)}, u32[]{:S(2)}) %collective-permute-start.3) | collective-permute-done | bytes 180256 | tf_op jit(solution)/shard_map/ppermute | solution.py:781
  20.6 0.9 %shard_map.78 = f32[40,2048]{1,0:T(8,128)} custom-call(f32[40,2048]{1,0:T(8,128)S(1)} %shard_map.77.base_ref, bf16[224,256]{1,0:T(8,128)(2,1)S(1)} %get-tuple-element.33.matrix_ref, f32[40,1536]{1,0:T(8,128)S(1)} %collective-permute-done.2.refs_0_, f32[88,512]{1,0:T(8,128)S(1)} %collective-permute-done.3.refs_1_), custom_call_target="tpu_custom_call" | custom-call | flops 100000000 | bytes 3000000 | tf_op jit(solution)/shard_map/pallas_call | solution.py:679
Async XLA Ops:
  2.4 6.2 %collective-permute-start = (f32[40,8,128]{2,1,0:T(8,128)S(1)}, f32[40,8,128]{2,1,0:T(8,128)S(1)}, u32[]{:S(2)}, u32[]{:S(2)}) collective-permute-start(f32[40,8,128]{2,1,0:T(8,128)S(1)} %get-tuple-element.36), channel_id=1, source_target_pairs={{0,2},{2,0},{4,6},{6,4},{8,10},{10,8},{12,14},{14,12},{16,18},{18,... | collective-permute-start | bytes 491528 | tf_op jit(solution)/shard_map/ppermute | solution.py:741
  3.1 8.7 %collective-permute-start.1 = (f32[40,8,128]{2,1,0:T(8,128)S(1)}, f32[40,8,128]{2,1,0:T(8,128)S(1)}, u32[]{:S(2)}, u32[]{:S(2)}) collective-permute-start(f32[40,8,128]{2,1,0:T(8,128)S(1)} %get-tuple-element.37), channel_id=1, source_target_pairs={{2,4},{4,2},{6,8},{8,6},{10,12},{12,10},{14,16},{16,14},{18,20},{2... | collective-permute-start | bytes 491528 | tf_op jit(solution)/shard_map/ppermute | solution.py:740
  7.7 8.8 %collective-permute-start.2 = (f32[40,1536]{1,0:T(8,128)S(1)}, f32[40,1536]{1,0:T(8,128)S(1)}, u32[]{:S(2)}, u32[]{:S(2)}) collective-permute-start(f32[40,1536]{1,0:T(8,128)S(1)} %get-tuple-element.49), channel_id=1, source_target_pairs={{0,1},{1,0},{2,3},{3,2},{4,5},{5,4},{6,7},{7,6},{8,9},{9,8},{10,11... | collective-permute-start | bytes 737288 | tf_op jit(solution)/shard_map/ppermute | solution.py:759
  14.9 5.7 %collective-permute-start.3 = (f32[88,512]{1,0:T(8,128)S(1)}, f32[88,512]{1,0:T(8,128)S(1)}, u32[]{:S(2)}, u32[]{:S(2)}) collective-permute-start(f32[88,512]{1,0:T(8,128)S(1)} %get-tuple-element.50), channel_id=1, source_target_pairs={{0,1},{1,0},{2,3},{3,2},{4,5},{5,4},{6,7},{7,6},{8,9},{9,8},{10,11... | collective-permute-start | bytes 540680 | tf_op jit(solution)/shard_map/ppermute | solution.py:781
